TPU v7x, 256 devices: a whole 4x4x8 slice. The times are simulated.
256 devices in a mesh: section: 8 (over y, core), dp: 32 (over z, x).
Axes of the slice: x: 4, y: 4, z: 8, core: 2. Of those that a mesh axis runs over, the one named last changes fastest.
Arguments:
- hidden_in: bfloat16 [4, 1024, 8192], P(None, 'dp'), may hold values from -6 to 6
- cotangent: bfloat16 [4, 1024, 8192], P(None, 'dp'), may hold values from -6 to 6
- adapter_in: bfloat16 [8, 8192, 128], P('section', 'dp'), may hold values from -0.0625 to 0.0625
- adapter_out: bfloat16 [8, 128, 8192], P('section', None, 'dp'), may hold values from -0.5 to 0.5
- norm_gain: bfloat16 [8, 8192], P('section', 'dp'), may hold values from 0.5 to 1.5
- user_of_row: int32 [4, 1024], P(None, 'dp'), may hold values from 0 to 63, as said below
- included: int32 [4, 64], P(None, 'dp'), may hold values 0 or 1
Outputs:
- grad_in: float32 [8, 8192, 128], P('section', 'dp')
- grad_out: float32 [8, 128, 8192], P('section', None, 'dp')
- user_weights: float32 [4, 64], P(None, 'dp')
Inputs may be any that keep to these rules, and one draw needn't show every extreme that they name: `user_of_row`: within one micro-batch, the rows of the j-th block of 32 rows belong to users j * 2 to j * 2 + 1, in rising order, each of them with one row or more.
All inputs are finite; a program needn't handle non-finite values. No bound on the sum of `included` on one device may be relied on, other than what follows from the above.
Results may differ from a plain program's by a relative error of at most 0.018.
Values may be sent and summed in bfloat16 or wider, within the bound.
A program may use at most 64 MiB of HBM per device.

v0:
```python
import math

import jax
import jax.numpy as jnp
from jax import lax
from jax.sharding import Mesh
from jax.sharding import PartitionSpec as P

DP = ("dp_0", "dp_1")


def gather_turned(arrays, axis, dims):
    turned = [jnp.moveaxis(a, dim, 0) for a, dim in zip(arrays, dims)]
    both = jnp.concatenate([t.reshape(len(t), -1) for t in turned], axis=1)
    result, at, done = (lax.all_gather(both, axis, axis=0, tiled=True), 0, [])
    for t, dim in zip(turned, dims):
        section = result[:, at : at + t[0].size].reshape(-1, *t.shape[1:])
        done.append(jnp.moveaxis(section, 0, dim))
        at += t[0].size
    return tuple(done)


def from_behind(block, axis, distance):
    devices = range(lax.axis_size(axis))
    route = [(i - distance, i) for i in devices if i - distance in devices]
    return lax.ppermute(block, axis, route)


def copy_for_each(x, axis):
    copies = jnp.broadcast_to(x, (lax.axis_size(axis), *x.shape))
    return lax.all_to_all(copies, axis, split_axis=0, concat_axis=0, tiled=True)


def taken_together(x, axis):
    return copy_for_each(x, axis).sum(axis=0)


def summed_rows(terms, axes):
    running = terms.astype(jnp.bfloat16)
    for axis in axes:
        running = lax.psum_scatter(running, axis, scatter_dimension=0, tiled=True)
    return running.astype(jnp.float32)


def normalize(stream_in, gain):
    stream = stream_in.astype(jnp.float32)
    scale = lax.rsqrt(jnp.mean(stream * stream, -1, keepdims=True) + 1e-05)
    unit = stream * scale
    normed = (unit * gain).astype(jnp.bfloat16)
    return (stream, scale, unit, normed)


def place(store, value, index, active):
    old = lax.dynamic_index_in_dim(store, index, 0, keepdims=False)
    return lax.dynamic_update_index_in_dim(store, jnp.where(active, value, old), index, 0)


def contract_last(left, right):
    return lax.dot_general(
        left, right, (((1,), (1,)), ((), ())), preferred_element_type=jnp.float32
    )


def contract_first(left, right):
    return lax.dot_general(
        left, right, (((0,), (0,)), ((), ())), preferred_element_type=jnp.float32
    )


def ghost(normed, err, low, delta, owners, onehot):
    same = owners[:, None] == owners[None, :]
    pairs = contract_last(normed, normed) * contract_last(err, err) + contract_last(
        low, low
    ) * contract_last(delta, delta)
    pairs = jnp.where(same, pairs, jnp.zeros_like(pairs))
    return jnp.sum(onehot * jnp.sum(pairs, -1)[:, None], 0)


def shards(hidden_in, cotangent, adapter_in, adapter_out, norm_gain, user_of_row, included):
    sections = lax.axis_size("section")
    section = lax.axis_index("section")
    dp_index = lax.axis_index(DP)
    a_full, b_full, g_full = gather_turned((adapter_in, adapter_out, norm_gain), DP, (1, 2, 1))
    a_mat = a_full[0]
    b_mat = b_full[0]
    gain = g_full[0].astype(jnp.float32)
    micro, rows, width = hidden_in.shape
    rank = a_mat.shape[1]
    users = included.shape[1]
    ticks = micro + sections - 1
    local_ids = user_of_row - dp_index * users
    onehot = (local_ids[:, :, None] == jnp.arange(users, dtype=jnp.int32)[None, None, :]).astype(
        jnp.float32
    )

    def forward_tick(carry, tick):
        incoming, keep_h, keep_n, keep_z = carry
        slot = tick - section
        active = (slot >= 0) & (slot < micro)
        index = jnp.clip(slot, 0, micro - 1)
        source = lax.dynamic_index_in_dim(hidden_in, index, 0, keepdims=False)
        current = jnp.where(section == 0, source, incoming)
        stream, scale, unit, normed = normalize(current, gain)
        low = jnp.dot(normed, a_mat, preferred_element_type=jnp.float32).astype(jnp.bfloat16)
        result = (stream + jnp.dot(low, b_mat, preferred_element_type=jnp.float32)).astype(
            jnp.bfloat16
        )
        keep_h = place(keep_h, current, index, active)
        keep_n = place(keep_n, normed, index, active)
        keep_z = place(keep_z, low, index, active)
        outgoing = from_behind(result, "section", 1)
        return ((outgoing, keep_h, keep_n, keep_z), None)

    start_fwd = (
        jnp.zeros((rows, width), jnp.bfloat16),
        jnp.zeros_like(hidden_in),
        jnp.zeros_like(hidden_in),
        jnp.zeros((micro, rows, rank), jnp.bfloat16),
    )
    (unused, keep_h, keep_n, keep_z), unused_out = lax.scan(
        forward_tick, start_fwd, jnp.arange(ticks, dtype=jnp.int32)
    )

    def backward_tick(carry, tick):
        incoming, carried, keep_e, keep_d, keep_p = carry
        slot = tick - (sections - 1 - section)
        active = (slot >= 0) & (slot < micro)
        index = jnp.clip(slot, 0, micro - 1)
        source = lax.dynamic_index_in_dim(cotangent, index, 0, keepdims=False)
        delta = jnp.where(section == sections - 1, source, incoming)
        current = lax.dynamic_index_in_dim(keep_h, index, 0, keepdims=False)
        normed = lax.dynamic_index_in_dim(keep_n, index, 0, keepdims=False)
        low = lax.dynamic_index_in_dim(keep_z, index, 0, keepdims=False)
        owners = lax.dynamic_index_in_dim(user_of_row, index, 0, keepdims=False)
        hot = lax.dynamic_index_in_dim(onehot, index, 0, keepdims=False)
        stream, scale, unit, unused_n = normalize(current, gain)
        err = contract_last(delta, b_mat).astype(jnp.bfloat16)
        slope = contract_last(err, a_mat) * gain
        grad_h = scale * (slope - unit * jnp.mean(slope * unit, -1, keepdims=True))
        previous = (delta.astype(jnp.float32) + grad_h).astype(jnp.bfloat16)
        partial_value = ghost(normed, err, low, delta, owners, hot)
        keep_e = place(keep_e, err, index, active)
        keep_d = place(keep_d, delta, index, active)
        keep_p = place(keep_p, partial_value, index, active)
        outgoing = from_behind(previous, "section", -1)
        return ((outgoing, carried, keep_e, keep_d, keep_p), None)

    start_bwd = (
        jnp.zeros((rows, width), jnp.bfloat16),
        jnp.zeros((users,), jnp.float32),
        jnp.zeros((micro, rows, rank), jnp.bfloat16),
        jnp.zeros_like(cotangent),
        jnp.zeros((micro, users), jnp.float32),
    )
    (unused_a, unused_b, keep_e, keep_d, keep_p), unused_out = lax.scan(
        backward_tick, start_bwd, jnp.arange(ticks, dtype=jnp.int32)
    )
    total = taken_together(keep_p, "section")
    bound = 0.8 * math.sqrt(sections * (rows // users) * width * width)
    user_weights = included.astype(jnp.float32) * (bound / jnp.maximum(jnp.sqrt(total), bound))
    row_weight = jnp.sum(onehot * user_weights[:, None, :], -1)[:, :, None]
    weighted_err = (
        (row_weight * keep_e.astype(jnp.float32)).astype(jnp.bfloat16).reshape(micro * rows, rank)
    )
    weighted_delta = (
        (row_weight * keep_d.astype(jnp.float32)).astype(jnp.bfloat16).reshape(micro * rows, width)
    )
    normed_rows = keep_n.reshape(micro * rows, width)
    low_rows = keep_z.reshape(micro * rows, rank)
    shard = summed_rows(
        jnp.concatenate(
            [contract_first(normed_rows, weighted_err), contract_first(weighted_delta, low_rows)], 1
        ),
        DP,
    )
    grad_in = shard[:, :rank]
    grad_out = shard[:, rank:].T
    return (grad_in[None], grad_out[None], user_weights)


def solution(mesh):
    torus = Mesh(mesh.devices.reshape(mesh.shape["section"], 8, 4), ("section", "dp_0", "dp_1"))
    return jax.shard_map(
        shards,
        mesh=torus,
        in_specs=(
            P(None, DP, None),
            P(None, DP, None),
            P("section", DP, None),
            P("section", None, DP),
            P("section", DP),
            P(None, DP),
            P(None, DP),
        ),
        out_specs=(P("section", DP, None), P("section", None, DP), P(None, DP)),
        check_vma=False,
    )
```

profile of v0, /device:TPU:1, one launch (start us, length us, event | category | flops | bytes accessed | tf_op | source)
XLA Modules:
  0.0 593.8 jit_solution(11264606444383854326)
XLA Ops:
  10.5 84.3 %all-gather.2.cloned.1.call-done = bf16[8192,257]{0,1:T(8,128)(2,1)} async-done(((bf16[256,257]{0,1:T(8,128)(2,1)}), bf16[8192,257]{0,1:T(8,128)(2,1)}) %all-gather.2.cloned.1.call-update) | async-done | bytes 4210704 | tf_op jit(solution)/shard_map/all_gather | solution.py:15
  106.8 180.2 %while.35 = (s32[]{:T(128)}, bf16[32,8192]{1,0:T(8,128)(2,1)S(1)}, bf16[4,32,8192]{2,1,0:T(8,128)(2,1)}, bf16[4,32,8192]{2,1,0:T(8,128)(2,1)}, bf16[4,32,128]{2,...) while((s32[]{:T(128)}, bf16[32,8192]{1,0:T(8,128)(2,1)S(1)}, ...), condition=%wide.region_2.3_spmd, body=%wide.region_0.2_spmd.sunk | while | flops 138682400 | bytes 23185208 | solution.py:120
  112.5 6.2 %collective-permute-start = (bf16[32,8192]{1,0:T(8,128)(2,1)S(1)}, bf16[32,8192]{1,0:T(8,128)(2,1)S(1)}, u32[]{:S(2)}, u32[]{:S(2)}) collective-permute-start(bf16[32,8192]{1,0:T(8,128)(2,1)S(1)} %fusion.73), channel_id=1, source_target_pairs={{0,32},{32,64},{64,96},{96,128},{128,160},{160,192},{192,224},{1,3... | collective-permute-start | bytes 1572872 | tf_op jit(solution)/shard_map/while/body/eval_jaxpr/ppermute | solution.py:26
  179.1 4.4 collective-permute-start
  195.3 4.4 collective-permute-start
  227.8 4.4 collective-permute-start
  244.0 4.4 collective-permute-start
  260.2 4.4 collective-permute-start
  276.4 4.4 collective-permute-start
  288.6 204.2 %while.36 = (s32[]{:T(128)}, bf16[32,8192]{1,0:T(8,128)(2,1)S(1)}, bf16[4,32,128]{2,1,0:T(8,128)(2,1)S(1)}, bf16[4,32,8192]{2,1,0:T(8,128)(2,1)}, f32[4,2]{1,0:T...) while((s32[]{:T(128)}, bf16[32,8192]{1,0:T(8,128)(2,1)S(1)}, ...), condition=%wide.region_8.9_spmd, body=%wide.region_3.8_spmd.sunk | while | flops 173029504 | bytes 33156040 | solution.py:155
  301.4 6.4 %collective-permute-done.1 = bf16[32,8192]{1,0:T(8,128)(2,1)S(1)} collective-permute-done((bf16[32,8192]{1,0:T(8,128)(2,1)S(1)}, bf16[32,8192]{1,0:T(8,128)(2,1)S(1)}, u32[]{:S(2)}, u32[]{:S(2)}) %collective-permute-start.1) | collective-permute-done | bytes 524320 | tf_op jit(solution)/shard_map/while/body/eval_jaxpr/ppermute | solution.py:26
  320.7 5.7 collective-permute-done.1
  339.2 5.7 collective-permute-done.1
  357.7 5.7 collective-permute-done.1
  376.2 5.7 collective-permute-done.1
  394.7 5.7 collective-permute-done.1
  413.2 5.7 collective-permute-done.1
  431.7 5.6 collective-permute-done.1
  450.1 5.7 collective-permute-done.1
  468.6 5.7 collective-permute-done.1
  487.1 5.7 collective-permute-done.1
  492.9 8.5 %all_to_all.5 = f32[8,4,2]{1,2,0:T(2,128)S(1)} all-to-all(f32[8,4,2]{1,2,0:T(2,128)S(1)} %broadcast_in_dim.47), channel_id=1, replica_groups=mesh['section'=8,'dp_0'=8,'dp_1'=4] {'section'}, dimensions={0} | all-to-all | bytes 512 | tf_op jit(solution)/shard_map/all_to_all | solution.py:31
  507.5 54.4 %reduce-scatter.3.cloned.1.call-done = bf16[1024,256]{0,1:T(8,128)(2,1)} async-done(((bf16[8192,256]{0,1:T(8,128)(2,1)}), bf16[1024,256]{0,1:T(8,128)(2,1)}) %reduce-scatter.3.cloned.1.call-update) | async-done | bytes 524304 | tf_op jit(solution)/shard_map/reduce_scatter | solution.py:41
  561.9 23.0 %reduce-scatter.5.cloned.1.call-done = bf16[256,256]{0,1:T(8,128)(2,1)} async-done(((bf16[1024,256]{0,1:T(8,128)(2,1)}), bf16[256,256]{0,1:T(8,128)(2,1)}) %reduce-scatter.5.cloned.1.call-update) | async-done | bytes 131088 | tf_op jit(solution)/shard_map/reduce_scatter | solution.py:41
  (441 shorter events, 298.3 us)
Async XLA Ops:
  7.2 87.5 %all-gather.2.cloned.1.call-start = ((), (), s32[]{:S(2)}) async-start(), calls=%async_computation.3 | async-start | bytes 4460544 | tf_op jit(solution)/shard_map/all_gather | solution.py:15
  9.7 552.2 %reduce-scatter.3.cloned.1.call-start = ((), (), s32[]{:S(2)}) async-start(), calls=%async_computation.4 | async-start | bytes 4718592 | tf_op jit(solution)/shard_map/reduce_scatter | solution.py:41
  112.5 12.3 %collective-permute-start = (bf16[32,8192]{1,0:T(8,128)(2,1)S(1)}, bf16[32,8192]{1,0:T(8,128)(2,1)S(1)}, u32[]{:S(2)}, u32[]{:S(2)}) collective-permute-start(bf16[32,8192]{1,0:T(8,128)(2,1)S(1)} %fusion.73), channel_id=1, source_target_pairs={{0,32},{32,64},{64,96},{96,128},{128,160},{160,192},{192,224},{1,3... | collective-permute-start | bytes 1572872 | tf_op jit(solution)/shard_map/while/body/eval_jaxpr/ppermute | solution.py:26
  130.5 10.5 %collective-permute-start = (bf16[32,8192]{1,0:T(8,128)(2,1)S(1)}, bf16[32,8192]{1,0:T(8,128)(2,1)S(1)}, u32[]{:S(2)}, u32[]{:S(2)}) collective-permute-start(bf16[32,8192]{1,0:T(8,128)(2,1)S(1)} %fusion.73), channel_id=1, source_target_pairs={{0,32},{32,64},{64,96},{96,128},{128,160},{160,192},{192,224},{1,3... | collective-permute-start | bytes 1572872 | tf_op jit(solution)/shard_map/while/body/eval_jaxpr/ppermute | solution.py:26
  162.9 10.5 %collective-permute-start = (bf16[32,8192]{1,0:T(8,128)(2,1)S(1)}, bf16[32,8192]{1,0:T(8,128)(2,1)S(1)}, u32[]{:S(2)}, u32[]{:S(2)}) collective-permute-start(bf16[32,8192]{1,0:T(8,128)(2,1)S(1)} %fusion.73), channel_id=1, source_target_pairs={{0,32},{32,64},{64,96},{96,128},{128,160},{160,192},{192,224},{1,3... | collective-permute-start | bytes 1572872 | tf_op jit(solution)/shard_map/while/body/eval_jaxpr/ppermute | solution.py:26
  179.1 10.5 %collective-permute-start = (bf16[32,8192]{1,0:T(8,128)(2,1)S(1)}, bf16[32,8192]{1,0:T(8,128)(2,1)S(1)}, u32[]{:S(2)}, u32[]{:S(2)}) collective-permute-start(bf16[32,8192]{1,0:T(8,128)(2,1)S(1)} %fusion.73), channel_id=1, source_target_pairs={{0,32},{32,64},{64,96},{96,128},{128,160},{160,192},{192,224},{1,3... | collective-permute-start | bytes 1572872 | tf_op jit(solution)/shard_map/while/body/eval_jaxpr/ppermute | solution.py:26
  195.3 10.5 %collective-permute-start = (bf16[32,8192]{1,0:T(8,128)(2,1)S(1)}, bf16[32,8192]{1,0:T(8,128)(2,1)S(1)}, u32[]{:S(2)}, u32[]{:S(2)}) collective-permute-start(bf16[32,8192]{1,0:T(8,128)(2,1)S(1)} %fusion.73), channel_id=1, source_target_pairs={{0,32},{32,64},{64,96},{96,128},{128,160},{160,192},{192,224},{1,3... | collective-permute-start | bytes 1572872 | tf_op jit(solution)/shard_map/while/body/eval_jaxpr/ppermute | solution.py:26
  211.6 10.5 %collective-permute-start = (bf16[32,8192]{1,0:T(8,128)(2,1)S(1)}, bf16[32,8192]{1,0:T(8,128)(2,1)S(1)}, u32[]{:S(2)}, u32[]{:S(2)}) collective-permute-start(bf16[32,8192]{1,0:T(8,128)(2,1)S(1)} %fusion.73), channel_id=1, source_target_pairs={{0,32},{32,64},{64,96},{96,128},{128,160},{160,192},{192,224},{1,3... | collective-permute-start | bytes 1572872 | tf_op jit(solution)/shard_map/while/body/eval_jaxpr/ppermute | solution.py:26
  227.8 10.5 %collective-permute-start = (bf16[32,8192]{1,0:T(8,128)(2,1)S(1)}, bf16[32,8192]{1,0:T(8,128)(2,1)S(1)}, u32[]{:S(2)}, u32[]{:S(2)}) collective-permute-start(bf16[32,8192]{1,0:T(8,128)(2,1)S(1)} %fusion.73), channel_id=1, source_target_pairs={{0,32},{32,64},{64,96},{96,128},{128,160},{160,192},{192,224},{1,3... | collective-permute-start | bytes 1572872 | tf_op jit(solution)/shard_map/while/body/eval_jaxpr/ppermute | solution.py:26
  244.0 10.5 %collective-permute-start = (bf16[32,8192]{1,0:T(8,128)(2,1)S(1)}, bf16[32,8192]{1,0:T(8,128)(2,1)S(1)}, u32[]{:S(2)}, u32[]{:S(2)}) collective-permute-start(bf16[32,8192]{1,0:T(8,128)(2,1)S(1)} %fusion.73), channel_id=1, source_target_pairs={{0,32},{32,64},{64,96},{96,128},{128,160},{160,192},{192,224},{1,3... | collective-permute-start | bytes 1572872 | tf_op jit(solution)/shard_map/while/body/eval_jaxpr/ppermute | solution.py:26
  260.2 10.5 %collective-permute-start = (bf16[32,8192]{1,0:T(8,128)(2,1)S(1)}, bf16[32,8192]{1,0:T(8,128)(2,1)S(1)}, u32[]{:S(2)}, u32[]{:S(2)}) collective-permute-start(bf16[32,8192]{1,0:T(8,128)(2,1)S(1)} %fusion.73), channel_id=1, source_target_pairs={{0,32},{32,64},{64,96},{96,128},{128,160},{160,192},{192,224},{1,3... | collective-permute-start | bytes 1572872 | tf_op jit(solution)/shard_map/while/body/eval_jaxpr/ppermute | solution.py:26
  276.4 10.5 %collective-permute-start = (bf16[32,8192]{1,0:T(8,128)(2,1)S(1)}, bf16[32,8192]{1,0:T(8,128)(2,1)S(1)}, u32[]{:S(2)}, u32[]{:S(2)}) collective-permute-start(bf16[32,8192]{1,0:T(8,128)(2,1)S(1)} %fusion.73), channel_id=1, source_target_pairs={{0,32},{32,64},{64,96},{96,128},{128,160},{160,192},{192,224},{1,3... | collective-permute-start | bytes 1572872 | tf_op jit(solution)/shard_map/while/body/eval_jaxpr/ppermute | solution.py:26
  296.6 11.2 %collective-permute-start.1 = (bf16[32,8192]{1,0:T(8,128)(2,1)S(1)}, bf16[32,8192]{1,0:T(8,128)(2,1)S(1)}, u32[]{:S(2)}, u32[]{:S(2)}) collective-permute-start(bf16[32,8192]{1,0:T(8,128)(2,1)S(1)} %fusion.86), channel_id=1, source_target_pairs={{32,0},{64,32},{96,64},{128,96},{160,128},{192,160},{224,192},{33,... | collective-permute-start | bytes 1572872 | tf_op jit(solution)/shard_map/while/body/eval_jaxpr/ppermute | solution.py:26
  315.8 10.5 %collective-permute-start.1 = (bf16[32,8192]{1,0:T(8,128)(2,1)S(1)}, bf16[32,8192]{1,0:T(8,128)(2,1)S(1)}, u32[]{:S(2)}, u32[]{:S(2)}) collective-permute-start(bf16[32,8192]{1,0:T(8,128)(2,1)S(1)} %fusion.86), channel_id=1, source_target_pairs={{32,0},{64,32},{96,64},{128,96},{160,128},{192,160},{224,192},{33,... | collective-permute-start | bytes 1572872 | tf_op jit(solution)/shard_map/while/body/eval_jaxpr/ppermute | solution.py:26
  334.3 10.5 %collective-permute-start.1 = (bf16[32,8192]{1,0:T(8,128)(2,1)S(1)}, bf16[32,8192]{1,0:T(8,128)(2,1)S(1)}, u32[]{:S(2)}, u32[]{:S(2)}) collective-permute-start(bf16[32,8192]{1,0:T(8,128)(2,1)S(1)} %fusion.86), channel_id=1, source_target_pairs={{32,0},{64,32},{96,64},{128,96},{160,128},{192,160},{224,192},{33,... | collective-permute-start | bytes 1572872 | tf_op jit(solution)/shard_map/while/body/eval_jaxpr/ppermute | solution.py:26
  352.8 10.5 %collective-permute-start.1 = (bf16[32,8192]{1,0:T(8,128)(2,1)S(1)}, bf16[32,8192]{1,0:T(8,128)(2,1)S(1)}, u32[]{:S(2)}, u32[]{:S(2)}) collective-permute-start(bf16[32,8192]{1,0:T(8,128)(2,1)S(1)} %fusion.86), channel_id=1, source_target_pairs={{32,0},{64,32},{96,64},{128,96},{160,128},{192,160},{224,192},{33,... | collective-permute-start | bytes 1572872 | tf_op jit(solution)/shard_map/while/body/eval_jaxpr/ppermute | solution.py:26
  371.3 10.5 %collective-permute-start.1 = (bf16[32,8192]{1,0:T(8,128)(2,1)S(1)}, bf16[32,8192]{1,0:T(8,128)(2,1)S(1)}, u32[]{:S(2)}, u32[]{:S(2)}) collective-permute-start(bf16[32,8192]{1,0:T(8,128)(2,1)S(1)} %fusion.86), channel_id=1, source_target_pairs={{32,0},{64,32},{96,64},{128,96},{160,128},{192,160},{224,192},{33,... | collective-permute-start | bytes 1572872 | tf_op jit(solution)/shard_map/while/body/eval_jaxpr/ppermute | solution.py:26
  389.8 10.5 %collective-permute-start.1 = (bf16[32,8192]{1,0:T(8,128)(2,1)S(1)}, bf16[32,8192]{1,0:T(8,128)(2,1)S(1)}, u32[]{:S(2)}, u32[]{:S(2)}) collective-permute-start(bf16[32,8192]{1,0:T(8,128)(2,1)S(1)} %fusion.86), channel_id=1, source_target_pairs={{32,0},{64,32},{96,64},{128,96},{160,128},{192,160},{224,192},{33,... | collective-permute-start | bytes 1572872 | tf_op jit(solution)/shard_map/while/body/eval_jaxpr/ppermute | solution.py:26
  408.3 10.5 %collective-permute-start.1 = (bf16[32,8192]{1,0:T(8,128)(2,1)S(1)}, bf16[32,8192]{1,0:T(8,128)(2,1)S(1)}, u32[]{:S(2)}, u32[]{:S(2)}) collective-permute-start(bf16[32,8192]{1,0:T(8,128)(2,1)S(1)} %fusion.86), channel_id=1, source_target_pairs={{32,0},{64,32},{96,64},{128,96},{160,128},{192,160},{224,192},{33,... | collective-permute-start | bytes 1572872 | tf_op jit(solution)/shard_map/while/body/eval_jaxpr/ppermute | solution.py:26
  426.8 10.5 %collective-permute-start.1 = (bf16[32,8192]{1,0:T(8,128)(2,1)S(1)}, bf16[32,8192]{1,0:T(8,128)(2,1)S(1)}, u32[]{:S(2)}, u32[]{:S(2)}) collective-permute-start(bf16[32,8192]{1,0:T(8,128)(2,1)S(1)} %fusion.86), channel_id=1, source_target_pairs={{32,0},{64,32},{96,64},{128,96},{160,128},{192,160},{224,192},{33,... | collective-permute-start | bytes 1572872 | tf_op jit(solution)/shard_map/while/body/eval_jaxpr/ppermute | solution.py:26
  445.3 10.5 %collective-permute-start.1 = (bf16[32,8192]{1,0:T(8,128)(2,1)S(1)}, bf16[32,8192]{1,0:T(8,128)(2,1)S(1)}, u32[]{:S(2)}, u32[]{:S(2)}) collective-permute-start(bf16[32,8192]{1,0:T(8,128)(2,1)S(1)} %fusion.86), channel_id=1, source_target_pairs={{32,0},{64,32},{96,64},{128,96},{160,128},{192,160},{224,192},{33,... | collective-permute-start | bytes 1572872 | tf_op jit(solution)/shard_map/while/body/eval_jaxpr/ppermute | solution.py:26
  463.8 10.5 %collective-permute-start.1 = (bf16[32,8192]{1,0:T(8,128)(2,1)S(1)}, bf16[32,8192]{1,0:T(8,128)(2,1)S(1)}, u32[]{:S(2)}, u32[]{:S(2)}) collective-permute-start(bf16[32,8192]{1,0:T(8,128)(2,1)S(1)} %fusion.86), channel_id=1, source_target_pairs={{32,0},{64,32},{96,64},{128,96},{160,128},{192,160},{224,192},{33,... | collective-permute-start | bytes 1572872 | tf_op jit(solution)/shard_map/while/body/eval_jaxpr/ppermute | solution.py:26
  482.3 10.5 %collective-permute-start.1 = (bf16[32,8192]{1,0:T(8,128)(2,1)S(1)}, bf16[32,8192]{1,0:T(8,128)(2,1)S(1)}, u32[]{:S(2)}, u32[]{:S(2)}) collective-permute-start(bf16[32,8192]{1,0:T(8,128)(2,1)S(1)} %fusion.86), channel_id=1, source_target_pairs={{32,0},{64,32},{96,64},{128,96},{160,128},{192,160},{224,192},{33,... | collective-permute-start | bytes 1572872 | tf_op jit(solution)/shard_map/while/body/eval_jaxpr/ppermute | solution.py:26
  507.4 77.5 %reduce-scatter.5.cloned.1.call-start = ((), (), s32[]{:S(2)}) async-start(), calls=%async_computation.5 | async-start | bytes 655360 | tf_op jit(solution)/shard_map/reduce_scatter | solution.py:41
  (37 other events, 335.7 us)
Sparse Core Ops, SparseCore 0:
  10.4 84.2 all-gather.1
  507.5 54.2 reduce-scatter.2
  564.4 20.4 reduce-scatter.4
where the time goes:
time: 599 us; the launch traced here: 594 us
  waiting for transfers between devices  268 us (45%)
  other arithmetic  87.2 us (15%)
  local copies, waits for them, and re-layouts  74 us (12%)
  starting transfers between devices  71.4 us (12%)
  matrix products  54.8 us (9%)
  loops' own time  15.8 us (3%)
  between operations  13.9 us (2%)
  blocking collectives  8.5 us (1%)
    ppermute x22, waiting for transfers between devices, from_behind(): return lax.ppermute(block, axis, route)  107 us
    all_gather x1, waiting for transfers between devices, gather_turned(): result, at, done = (lax.all_gather(both, axis, axis=0, tiled=True), 0, [])  84.3 us
    reduce_scatter x2, waiting for transfers between devices, summed_rows(): running = lax.psum_scatter(running, axis, scatter_dimension=0, tiled=True)  77.4 us
    ppermute x22, starting transfers between devices, from_behind(): return lax.ppermute(block, axis, route)  71.2 us
    dynamic_update_slice x33, other arithmetic, place(): lax.dynamic_update_index_in_dim(store, jnp.where(active, value, old), ind...  58.9 us
    dot_general x66, matrix products, contract_last(): lax.dot_general(left, right, (((1,), (1,)), ((), ())), preferred_element_...  41.6 us
    dynamic_slice x55, local copies, waits for them, and re-layouts, place(): old = lax.dynamic_index_in_dim(store, index, 0, keepdims=False)  37.5 us
    reduce_sum x22, other arithmetic, normalize(): scale = lax.rsqrt(jnp.mean(stream * stream, -1, keepdims=True) + 1e-05)  16.4 us
  transfers between devices with their start and end apart: 25, of which 25 were waited for; matrix products, arithmetic and copies ran while one was open for 9% of the time, Pallas kernels for 0%

commit v1 on v0

v1 whole, which is shorter than its diff:
```python
import math

import jax
import jax.numpy as jnp
from jax import lax
from jax.sharding import Mesh
from jax.sharding import PartitionSpec as P

F32 = jnp.float32
BF = jnp.bfloat16


def mm(a, b, ca, cb):
    return lax.dot_general(a, b, (((ca,), (cb,)), ((), ())), preferred_element_type=F32)


def swap_route(n, m):
    return [(i * m + j, j * m + i) for i in range(n) for j in range(m)]


def recurrence(z0, y0, c0, norm0, gram, width):
    layers, rows, rank = z0.shape
    z = [z0[l] for l in range(layers)]
    y = [y0[l] for l in range(layers)]
    c = [c0[l] for l in range(layers)]
    square = norm0
    lows, rinvs, fulls, seen = [], [], [], []
    for l in range(layers):
        rinv = lax.rsqrt(square / width + 1e-05)
        full = z[l] * rinv
        low = full.astype(BF)
        seen.append(list(y))
        for j in range(layers):
            both = mm(low, gram[l, j], 1, 0)
            z[j] = z[j] + both[:, :rank]
            y[j] = y[j] + both[:, rank:]
        square = square + jnp.sum(low.astype(F32) * (seen[l][l] + y[l]), -1, keepdims=True)
        lows.append(low)
        rinvs.append(rinv)
        fulls.append(full)
    errs, cors = [None] * layers, [None] * layers
    for l in range(layers - 1, -1, -1):
        err = c[l].astype(BF)
        mean = jnp.sum(err.astype(F32) * fulls[l], -1, keepdims=True) / width
        cor = rinvs[l] * rinvs[l] * mean
        for j in range(l):
            c[j] = c[j] + rinvs[l] * mm(err, gram[j, l][:, :rank], 1, 1) - cor * seen[l][j]
        errs[l] = err
        cors[l] = cor
    return lows, errs, rinvs, cors


def shards(hidden_in, cotangent, adapter_in, adapter_out, norm_gain, user_of_row, included):
    n_s, n_z, n_x = (lax.axis_size(a) for a in ("section", "z", "x"))
    s, zi, xi = (lax.axis_index(a) for a in ("section", "z", "x"))
    plane = ("section", "x")
    layers = n_s
    micro, rows, width = hidden_in.shape
    cols, rank = adapter_in.shape[1:]
    users = included.shape[1]
    dev_rows = micro * rows
    group_rows = dev_rows * n_x
    own_rows = group_rows // (n_s * n_x)
    gain = norm_gain[0]
    a = adapter_in[0]
    bt = adapter_out[0].T
    g = (a.astype(F32) * gain.astype(F32)[:, None]).astype(BF)
    w = jnp.concatenate([jnp.concatenate([g, bt], 1), jnp.broadcast_to(gain[None], (16, cols))], 0)
    w = lax.ppermute(w, ("section", "z"), swap_route(n_s, n_z))
    w = lax.all_gather(w, "z")
    gains = w[:, cols].astype(F32)
    w = w[:, :cols]
    base = (zi * n_x + xi) * users
    key = ((user_of_row - base) + users * jnp.arange(micro, dtype=jnp.int32)[:, None]).reshape(dev_rows)
    onehot = (user_of_row - base)[:, :, None] == jnp.arange(users, dtype=jnp.int32)
    inc = jnp.sum(jnp.where(onehot, included[:, None, :], 0), -1).reshape(dev_rows)
    info = jnp.stack([key, inc]).astype(BF)
    info_all = lax.all_gather(info, "x")
    span = n_x * cols
    both = jnp.concatenate([hidden_in.reshape(dev_rows, width), cotangent.reshape(dev_rows, width)], 0)
    both = lax.dynamic_slice_in_dim(both, s * span, span, 1)
    both = jnp.moveaxis(both.reshape(2 * dev_rows, n_x, cols), 1, 0)
    both = lax.all_to_all(both, "x", 0, 0, tiled=True)
    x = both[:, :dev_rows].reshape(group_rows, cols)
    cot = both[:, dev_rows:].reshape(group_rows, cols)
    own = lax.dynamic_index_in_dim(w, zi, 0, keepdims=False)[:, rank:]
    zy = jnp.stack([mm(x, w[l], 1, 0) for l in range(layers)])
    ct = jnp.stack([mm(cot, w[l][:, rank:], 1, 0) for l in range(layers)])
    proj = jnp.concatenate([zy, ct], -1).astype(BF)
    gram = jnp.stack([mm(own, w[l], 0, 0) for l in range(layers)]).astype(BF)
    n_plane = n_s * n_x
    proj = jnp.moveaxis(proj.reshape(layers, n_plane, own_rows, 3 * rank), 1, 0)
    gram = gram.reshape(n_plane, rank // n_x, 2 * rank)
    xf = x.astype(F32)
    norm0 = jnp.sum(xf * xf, -1).reshape(n_plane, own_rows, 1)
    proj = jnp.sum(lax.all_to_all(proj, plane, 0, 0, tiled=True).astype(F32), 0)
    gram = jnp.sum(lax.all_to_all(gram, plane, 0, 0, tiled=True).astype(F32), 0).astype(BF)
    norm0 = jnp.sum(lax.all_to_all(norm0, plane, 0, 0, tiled=True), 0)
    gram = lax.all_gather(gram, ("z", "section", "x"))
    gram = gram.reshape(layers, layers, rank, 2 * rank)
    lows, errs, rinvs, cors = recurrence(
        proj[..., :rank], proj[..., rank : 2 * rank], proj[..., 2 * rank :], norm0, gram, width
    )
    pack = jnp.stack(lows + errs)
    scal = jnp.concatenate(rinvs + cors, 1)
    pack = lax.all_gather(pack, plane, axis=1, tiled=True)
    scal = lax.all_gather(scal, plane, axis=0, tiled=True)
    low, err = pack[:layers], pack[layers:]
    h = x.astype(F32)
    normed = []
    hs = []
    for l in range(layers):
        hs.append(h.astype(BF))
        normed.append((h * scal[:, l : l + 1] * gains[l][None]).astype(BF))
        h = h + mm(low[l], w[l][:, rank:], 1, 1)
    delta = cot.astype(F32)
    deltas = [None] * layers
    for l in range(layers - 1, -1, -1):
        deltas[l] = delta.astype(BF)
        delta = (
            delta
            + scal[:, l : l + 1] * mm(err[l], w[l][:, :rank], 1, 1)
            - scal[:, layers + l : layers + l + 1] * hs[l].astype(F32)
        )
    totals = []
    for i in range(n_x):
        at = slice(i * dev_rows, (i + 1) * dev_rows)
        keys = info_all[i, 0]
        same = keys[:, None] == keys[None, :]
        pairs = 0.0
        for l in range(layers):
            n, e, lo, d = normed[l][at], err[l][at], low[l][at], deltas[l][at]
            pairs = pairs + mm(n, n, 1, 1) * mm(e, e, 1, 1) + mm(lo, lo, 1, 1) * mm(d, d, 1, 1)
        rowsum = jnp.sum(jnp.where(same, pairs, 0.0), -1)
        totals.append(jnp.sum(jnp.where(same, rowsum[None, :], 0.0), -1))
    totals = lax.psum(jnp.stack(totals), plane)
    bound = 0.8 * math.sqrt(layers * (rows // users) * width * width)
    row_w = info_all[:, 1].astype(F32) * (bound / jnp.maximum(jnp.sqrt(totals), bound))
    mine = lax.dynamic_index_in_dim(row_w, xi, 0, keepdims=False).reshape(micro, rows)
    user_weights = jnp.max(jnp.where(onehot, mine[:, :, None], 0.0), 1)
    row_w = row_w.reshape(group_rows, 1)
    grads = []
    for l in range(layers):
        we = (row_w * err[l].astype(F32)).astype(BF)
        wl = (row_w * low[l].astype(F32)).astype(BF)
        grads.append(jnp.concatenate([mm(normed[l], we, 0, 0), mm(deltas[l], wl, 0, 0)], 1))
    grads = jnp.stack(grads).astype(BF)
    grads = jnp.sum(lax.all_to_all(grads, "z", 0, 0, tiled=True).astype(F32), 0)
    grads = lax.ppermute(grads, ("section", "z"), swap_route(n_s, n_z))
    return (grads[None, :, :rank], grads[:, rank:].T[None], user_weights)


def solution(mesh):
    torus = Mesh(mesh.devices.reshape(mesh.shape["section"], 8, 4), ("section", "z", "x"))
    dp = ("z", "x")
    return jax.shard_map(
        shards,
        mesh=torus,
        in_specs=(
            P(None, dp, None),
            P(None, dp, None),
            P("section", dp, None),
            P("section", None, dp),
            P("section", dp),
            P(None, dp),
            P(None, dp),
        ),
        out_specs=(P("section", dp, None), P("section", None, dp), P(None, dp)),
        check_vma=False,
    )
```

time: 599 us -> 462 us (0.77)
  blocking collectives: 8.5 us -> 140 us
  waiting for transfers between devices: 268 us -> 157 us
  other arithmetic: 87.2 us -> 11.1 us
  local copies, waits for them, and re-layouts: 74 us -> 19.8 us
  starting transfers between devices: 71.4 us -> 45.1 us
  loops' own time: 15.8 us -> 0 us
  matrix products: 54.8 us -> 68.7 us
    ppermute x22 -> x2, waiting for transfers between devices: 107 us -> 8.04 us  [the longest x1 5.31 us: shards(): grads = lax.ppermute(grads, ('section', 'z'), swap_route(n_s, n_z))]
    reduce_scatter x2 -> x0, waiting for transfers between devices: 77.4 us -> none  [summed_rows(): running = lax.psum_scatter(running, axis, scatter_dimension=0, tiled=True)]
    psum x0 -> x1, blocking collectives: none -> 61.3 us  [shards(): totals = lax.psum(jnp.stack(totals), plane)]
    dynamic_update_slice x33 -> x0, other arithmetic: 58.9 us -> none  [place(): lax.dynamic_update_index_in_dim(store, jnp.where(active, value, old), ind...]
    ppermute x22 -> x2, starting transfers between devices: 71.2 us -> 17 us  [the longest x1 12 us: shards(): grads = lax.ppermute(grads, ('section', 'z'), swap_route(n_s, n_z))]
    all_to_all x0 -> x4, waiting for transfers between devices: none -> 53.9 us  [the longest x1 39 us: shards(): proj = jnp.sum(lax.all_to_all(proj, plane, 0, 0, tiled=True).astype(F32), 0)]
    all_gather x0 -> x2, blocking collectives: none -> 51.3 us  [the longest x1 43.7 us: shards(): scal = lax.all_gather(scal, plane, axis=0, tiled=True)]
    dynamic_slice x77 -> x2, local copies, waits for them, and re-layouts: 50.4 us -> 2.07 us  [the longest x1 2.05 us: shards(): both = lax.dynamic_slice_in_dim(both, s * span, span, 1)]
  transfers between devices with their start and end apart: 25 -> 9, of which waited for: 25 -> 7; matrix products, arithmetic and copies ran while one was open for 9% -> 5% of each run, Pallas kernels for 0% -> 0%
where the time goes in v1:
time: 462 us; the launch traced here: 457 us
  waiting for transfers between devices  157 us (34%)
  blocking collectives  140 us (30%)
  matrix products  68.7 us (15%)
  starting transfers between devices  45.1 us (10%)
  local copies, waits for them, and re-layouts  19.8 us (4%)
  between operations  15.9 us (3%)
  other arithmetic  11.1 us (2%)
    dot_general x266, matrix products, mm(): lax.dot_general(a, b, (((ca,), (cb,)), ((), ())), preferred_element_type=...  68.7 us
    psum x1, blocking collectives, shards(): totals = lax.psum(jnp.stack(totals), plane)  61.3 us
    all_gather x1, waiting for transfers between devices, shards(): gram = lax.all_gather(gram, ('z', 'section', 'x'))  49.5 us
    all_gather x1, waiting for transfers between devices, shards(): w = lax.all_gather(w, 'z')  45 us
    all_gather x1, blocking collectives, shards(): scal = lax.all_gather(scal, plane, axis=0, tiled=True)  43.7 us
    all_to_all x1, waiting for transfers between devices, shards(): proj = jnp.sum(lax.all_to_all(proj, plane, 0, 0, tiled=True).astype(F32), 0)  39 us
    all_to_all x1, blocking collectives, shards(): grads = jnp.sum(lax.all_to_all(grads, 'z', 0, 0, tiled=True).astype(F32), 0)  27.1 us
    all_to_all x1, starting transfers between devices, shards(): lax.all_to_all(gram, plane, 0, 0, tiled=True).astype(F32)  12.3 us
  transfers between devices with their start and end apart: 9, of which 7 were waited for; matrix products, arithmetic and copies ran while one was open for 5% of the time, Pallas kernels for 0%

profile of v1, /device:TPU:1, one launch (start us, length us, event | category | flops | bytes accessed | tf_op | source)
XLA Modules:
  0.0 456.9 jit_solution(16412173527792185459)
XLA Ops:
  9.9 4.9 %collective-permute-start = (bf16[272,256]{1,0:T(8,128)(2,1)S(1)}, bf16[272,256]{1,0:T(8,128)(2,1)S(1)}, u32[]{:S(2)}, u32[]{:S(2)}) collective-permute-start(bf16[272,256]{1,0:T(8,128)(2,1)S(1)} %pad_maximum_fusion), channel_id=1, source_target_pairs={{0,0},{4,32},{8,64},{12,96},{16,128},{20,160},{24,192},{28,224},{3... | collective-permute-start | bytes 417800 | tf_op jit(solution)/shard_map/ppermute | solution.py:69
  14.8 2.7 collective-permute-done
  18.2 45.0 %all-gather.8.cloned.1.call-done = bf16[2176,256]{1,0:T(8,128)(2,1)} async-done(((bf16[272,256]{1,0:T(8,128)(2,1)}), bf16[2176,256]{1,0:T(8,128)(2,1)}) %all-gather.8.cloned.1.call-update) | async-done | bytes 1114128 | tf_op jit(solution)/shard_map/all_gather | solution.py:70
  67.2 12.3 %all-to-all-start.3 = ((bf16[32,32,256]{2,1,0:T(8,128)(2,1)}), bf16[32,32,256]{2,1,0:T(8,128)(2,1)}, u32[]{:S(2)}, u32[]{:S(2)}) async-start(bf16[32,32,256]{2,1,0:T(8,128)(2,1)} %bitcast.1095), calls=%async_computation.3 | async-start | bytes 1048576 | tf_op jit(solution)/shard_map/all_to_all | solution.py:97
  79.5 1.8 fusion.201
  81.3 2.0 copy.59
  83.4 7.6 %all-to-all-done.3 = bf16[32,32,256]{2,1,0:T(8,128)(2,1)} async-done(((bf16[32,32,256]{2,1,0:T(8,128)(2,1)}), bf16[32,32,256]{2,1,0:T(8,128)(2,1)}, u32[]{:S(2)}, u32[]{:S(2)}) %all-to-all-start.3) | async-done | bytes 524320 | tf_op jit(solution)/shard_map/all_to_all | solution.py:97
  91.0 3.5 all-to-all-start
  94.5 1.7 reduce_sum.273
  96.3 7.3 %all-to-all-done = bf16[4,256,256]{1,2,0:T(8,128)(2,1)S(1)} async-done(((bf16[4,256,256]{1,2,0:T(8,128)(2,1)}), bf16[4,256,256]{1,2,0:T(8,128)(2,1)S(1)}, u32[]{:S(2)}, u32[]{:S(2)}) %all-to-all-start) | async-done | bytes 524320 | tf_op jit(solution)/shard_map/all_to_all | solution.py:83
  104.4 4.9 %all-to-all-start.1 = ((f32[32,16,1]{1,2,0:T(1,128)}), f32[32,16,1]{1,2,0:T(1,128)S(1)}, u32[]{:S(2)}, u32[]{:S(2)}) async-start(f32[32,16,1]{1,2,0:T(1,128)} %bitcast.4), calls=%async_computation.1 | async-start | bytes 32768 | tf_op jit(solution)/shard_map/all_to_all | solution.py:98
  114.1 2.2 copy.64
  116.3 7.4 %all-to-all-start.2 = ((bf16[32,8,16,384]{3,2,1,0:T(8,128)(2,1)}), bf16[32,8,16,384]{3,2,1,0:T(8,128)(2,1)}, u32[]{:S(2)}, u32[]{:S(2)}) async-start(bf16[32,8,16,384]{3,2,1,0:T(8,128)(2,1)} %copy.64), calls=%async_computation.2 | async-start | bytes 6291456 | tf_op jit(solution)/shard_map/all_to_all | solution.py:96
  123.9 39.0 %all-to-all-done.2 = bf16[32,8,16,384]{3,2,1,0:T(8,128)(2,1)} async-done(((bf16[32,8,16,384]{3,2,1,0:T(8,128)(2,1)}), bf16[32,8,16,384]{3,2,1,0:T(8,128)(2,1)}, u32[]{:S(2)}, u32[]{:S(2)}) %all-to-all-start.2) | async-done | bytes 3145760 | tf_op jit(solution)/shard_map/all_to_all | solution.py:96
  162.8 2.3 convert_reduce_fusion
  165.3 49.5 %all-gather.10.cloned.1.call-done = bf16[8192,256]{1,0:T(8,128)(2,1)} async-done(((bf16[32,256]{1,0:T(8,128)(2,1)}), bf16[8192,256]{1,0:T(8,128)(2,1)}) %all-gather.10.cloned.1.call-update) | async-done | bytes 4194320 | tf_op jit(solution)/shard_map/all_gather | solution.py:99
  214.8 1.5 slice_bitcast_fusion.99
  244.7 7.7 %all_gather.27 = bf16[4,2,128]{2,1,0:T(2,128)(2,1)S(1)} all-gather(bf16[1,2,128]{2,1,0:T(2,128)(2,1)S(1)} %pad_maximum_fusion.2), channel_id=1, replica_groups=mesh['section'=8,'z'=8,'x'=4] {'x'}, dimensions={0}, use_global_device_ids=true | all-gather | bytes 2560 | tf_op jit(solution)/shard_map/all_gather | solution.py:78
  254.1 43.7 %all_gather.26 = f32[512,16]{1,0:T(8,128)S(1)} all-gather(f32[16,16]{1,0:T(8,128)S(1)} %copy.65), channel_id=1, replica_groups=mesh['section'=8,'z'=8,'x'=4] {'section','x'}, dimensions={0}, use_global_device_ids=true | all-gather | bytes 33792 | tf_op jit(solution)/shard_map/all_gather | solution.py:107
  297.8 2.6 slice_reduce_fusion.14
  332.6 61.3 %psum.7 = f32[4,128]{1,0:T(4,128)S(1)} all-reduce(f32[4,128]{1,0:T(4,128)S(1)} %pad_maximum_fusion.1), channel_id=1, replica_groups=mesh['section'=8,'z'=8,'x'=4] {'section','x'}, use_global_device_ids=true, to_apply=%region_28.29 | all-reduce | flops 512 | bytes 4096 | tf_op jit(solution)/shard_map/psum | solution.py:136
  403.6 27.1 %all_to_all.25 = bf16[8,256,256]{1,2,0:T(8,128)(2,1)S(1)} all-to-all(bf16[8,256,256]{1,2,0:T(8,128)(2,1)S(1)} %fusion.217), channel_id=1, replica_groups=mesh['section'=8,'z'=8,'x'=4] {'z'}, dimensions={0} | all-to-all | bytes 2097152 | tf_op jit(solution)/shard_map/all_to_all | solution.py:148
  430.9 12.0 %collective-permute-start.1 = (f32[256,256]{0,1:T(8,128)S(1)}, f32[256,256]{0,1:T(8,128)S(1)}, u32[]{:S(2)}, u32[]{:S(2)}) collective-permute-start(f32[256,256]{0,1:T(8,128)S(1)} %convert_reduce_fusion.1), channel_id=1, source_target_pairs={{0,0},{4,32},{8,64},{12,96},{16,128},{20,160},{24,192},{28,224},{3... | collective-permute-start | bytes 786440 | tf_op jit(solution)/shard_map/ppermute | solution.py:149
  443.7 5.3 %collective-permute-done.1 = f32[256,256]{0,1:T(8,128)S(1)} collective-permute-done((f32[256,256]{0,1:T(8,128)S(1)}, f32[256,256]{0,1:T(8,128)S(1)}, u32[]{:S(2)}, u32[]{:S(2)}) %collective-permute-start.1) | collective-permute-done | bytes 262176 | tf_op jit(solution)/shard_map/ppermute | solution.py:149
  (521 shorter events, 85.5 us)
Async XLA Ops:
  7.2 56.1 %all-gather.8.cloned.1.call-start = ((), (), s32[]{:S(2)}) async-start(), calls=%async_computation.6 | async-start | bytes 1253376 | tf_op jit(solution)/shard_map/all_gather | solution.py:70
  9.9 7.7 %collective-permute-start = (bf16[272,256]{1,0:T(8,128)(2,1)S(1)}, bf16[272,256]{1,0:T(8,128)(2,1)S(1)}, u32[]{:S(2)}, u32[]{:S(2)}) collective-permute-start(bf16[272,256]{1,0:T(8,128)(2,1)S(1)} %pad_maximum_fusion), channel_id=1, source_target_pairs={{0,0},{4,32},{8,64},{12,96},{16,128},{20,160},{24,192},{28,224},{3... | collective-permute-start | bytes 417800 | tf_op jit(solution)/shard_map/ppermute | solution.py:69
  64.6 14.9 %copy-start.6 = (bf16[4,32,8192]{2,1,0:T(8,128)(2,1)S(1)}, bf16[4,32,8192]{2,1,0:T(8,128)(2,1)}, u32[]{:S(2)}) copy-start(bf16[4,32,8192]{2,1,0:T(8,128)(2,1)} %param.7) | copy-start | bytes 6291460
  67.2 23.8 %all-to-all-start.3 = ((bf16[32,32,256]{2,1,0:T(8,128)(2,1)}), bf16[32,32,256]{2,1,0:T(8,128)(2,1)}, u32[]{:S(2)}, u32[]{:S(2)}) async-start(bf16[32,32,256]{2,1,0:T(8,128)(2,1)} %bitcast.1095), calls=%async_computation.3 | async-start | bytes 1048576 | tf_op jit(solution)/shard_map/all_to_all | solution.py:97
  91.0 12.6 %all-to-all-start = ((bf16[4,256,256]{1,2,0:T(8,128)(2,1)}), bf16[4,256,256]{1,2,0:T(8,128)(2,1)S(1)}, u32[]{:S(2)}, u32[]{:S(2)}) async-start(bf16[4,256,256]{1,2,0:T(8,128)(2,1)} %bitcast.3), calls=%async_computation | async-start | bytes 1048576 | tf_op jit(solution)/shard_map/all_to_all | solution.py:83
  94.5 120.3 %all-gather.10.cloned.1.call-start = ((), (), s32[]{:S(2)}) async-start(), calls=%async_computation.7 | async-start | bytes 4210688 | tf_op jit(solution)/shard_map/all_gather | solution.py:99
  103.6 196.8 %copy-start.3 = (bf16[4,256,256]{1,2,0:T(8,128)(2,1)}, bf16[4,256,256]{1,2,0:T(8,128)(2,1)S(1)}, u32[]{:S(2)}) copy-start(bf16[4,256,256]{1,2,0:T(8,128)(2,1)S(1)} %all-to-all-done) | copy-start | bytes 1572868
  104.4 12.0 %all-to-all-start.1 = ((f32[32,16,1]{1,2,0:T(1,128)}), f32[32,16,1]{1,2,0:T(1,128)S(1)}, u32[]{:S(2)}, u32[]{:S(2)}) async-start(f32[32,16,1]{1,2,0:T(1,128)} %bitcast.4), calls=%async_computation.1 | async-start | bytes 32768 | tf_op jit(solution)/shard_map/all_to_all | solution.py:98
  116.3 46.5 %all-to-all-start.2 = ((bf16[32,8,16,384]{3,2,1,0:T(8,128)(2,1)}), bf16[32,8,16,384]{3,2,1,0:T(8,128)(2,1)}, u32[]{:S(2)}, u32[]{:S(2)}) async-start(bf16[32,8,16,384]{3,2,1,0:T(8,128)(2,1)} %copy.64), calls=%async_computation.2 | async-start | bytes 6291456 | tf_op jit(solution)/shard_map/all_to_all | solution.py:96
  123.8 180.3 %all-gather.6.cloned.1.call-start = ((), (), s32[]{:S(2)}) async-start(), calls=%async_computation.5 | async-start | bytes 2162688 | tf_op jit(solution)/shard_map/all_gather | solution.py:106
  214.8 17.7 %copy-start.2 = (bf16[8192,256]{1,0:T(8,128)(2,1)S(1)}, bf16[8192,256]{1,0:T(8,128)(2,1)}, u32[]{:S(2)}) copy-start(bf16[8192,256]{1,0:T(8,128)(2,1)} %all-gather.10.cloned.1.call-done) | copy-start | bytes 12582916
  253.7 50.4 %copy-start.5 = (f32[4,128,256]{2,1,0:T(8,128)}, f32[4,128,256]{2,1,0:T(8,128)S(1)}, u32[]{:S(2)}) copy-start(f32[4,128,256]{2,1,0:T(8,128)S(1)} %copy.68) | copy-start | bytes 1572868
  300.4 9.1 %copy-start.56 = (f32[512]{0:T(512)}, f32[512]{0:T(512)S(1)}, u32[]{:S(2)}) copy-start(f32[512]{0:T(512)S(1)} %get-tuple-element.19) | copy-start | bytes 6148
  300.4 9.7 %copy-start.58 = (f32[512]{0:T(512)}, f32[512]{0:T(512)S(1)}, u32[]{:S(2)}) copy-start(f32[512]{0:T(512)S(1)} %get-tuple-element.21) | copy-start | bytes 6148
  314.4 17.4 %copy-start.20 = (bf16[512,256]{1,0:T(8,128)(2,1)}, bf16[512,256]{1,0:T(8,128)(2,1)S(1)}, u32[]{:S(2)}) copy-start(bf16[512,256]{1,0:T(8,128)(2,1)S(1)} %get-tuple-element.197) | copy-start | bytes 786436
  314.7 16.6 %copy-start.22 = (bf16[512,256]{1,0:T(8,128)(2,1)}, bf16[512,256]{1,0:T(8,128)(2,1)S(1)}, u32[]{:S(2)}) copy-start(bf16[512,256]{1,0:T(8,128)(2,1)S(1)} %get-tuple-element.193) | copy-start | bytes 786436
  315.0 15.8 %copy-start.24 = (bf16[512,256]{1,0:T(8,128)(2,1)}, bf16[512,256]{1,0:T(8,128)(2,1)S(1)}, u32[]{:S(2)}) copy-start(bf16[512,256]{1,0:T(8,128)(2,1)S(1)} %get-tuple-element.189) | copy-start | bytes 786436
  315.3 14.9 %copy-start.26 = (bf16[512,256]{1,0:T(8,128)(2,1)}, bf16[512,256]{1,0:T(8,128)(2,1)S(1)}, u32[]{:S(2)}) copy-start(bf16[512,256]{1,0:T(8,128)(2,1)S(1)} %get-tuple-element.185) | copy-start | bytes 786436
  315.7 14.1 %copy-start.28 = (bf16[512,256]{1,0:T(8,128)(2,1)}, bf16[512,256]{1,0:T(8,128)(2,1)S(1)}, u32[]{:S(2)}) copy-start(bf16[512,256]{1,0:T(8,128)(2,1)S(1)} %get-tuple-element.181) | copy-start | bytes 786436
  316.3 13.0 %copy-start.29 = (bf16[512,256]{1,0:T(8,128)(2,1)}, bf16[512,256]{1,0:T(8,128)(2,1)S(1)}, u32[]{:S(2)}) copy-start(bf16[512,256]{1,0:T(8,128)(2,1)S(1)} %get-tuple-element.177) | copy-start | bytes 786436
  329.0 65.0 %copy-start.62 = (bf16[4,1,128]{2,1,0:T(2,128)(2,1)S(1)}, bf16[4,1,128]{2,1,0:T(2,128)(2,1)}, u32[]{:S(2)}) copy-start(bf16[4,1,128]{2,1,0:T(2,128)(2,1)} %slice.2329) | copy-start | bytes 3076
  330.6 66.4 %copy-start.14 = (bf16[512,256]{1,0:T(8,128)(2,1)S(1)}, bf16[512,256]{1,0:T(8,128)(2,1)}, u32[]{:S(2)}) copy-start(bf16[512,256]{1,0:T(8,128)(2,1)} %copy-done.13) | copy-start | bytes 786436
  332.5 67.6 %copy-start.27 = (bf16[512,256]{1,0:T(8,128)(2,1)S(1)}, bf16[512,256]{1,0:T(8,128)(2,1)}, u32[]{:S(2)}) copy-start(bf16[512,256]{1,0:T(8,128)(2,1)} %copy-done.26) | copy-start | bytes 786436
  430.9 18.1 %collective-permute-start.1 = (f32[256,256]{0,1:T(8,128)S(1)}, f32[256,256]{0,1:T(8,128)S(1)}, u32[]{:S(2)}, u32[]{:S(2)}) collective-permute-start(f32[256,256]{0,1:T(8,128)S(1)} %convert_reduce_fusion.1), channel_id=1, source_target_pairs={{0,0},{4,32},{8,64},{12,96},{16,128},{20,160},{24,192},{28,224},{3... | collective-permute-start | bytes 786440 | tf_op jit(solution)/shard_map/ppermute | solution.py:149
  (59 other events, 180.6 us)
Sparse Core Ops, SparseCore 0:
  18.3 44.8 all-gather.7
  99.0 115.7 all-gather.9
  244.4 46.9 all-gather.5

commit v2 on v1

v2 whole, which is shorter than its diff:
```python
import functools
import math

import jax
import jax.numpy as jnp
from jax import lax
from jax.experimental import pallas as pl
from jax.experimental.pallas import tpu as pltpu
from jax.sharding import Mesh
from jax.sharding import PartitionSpec as P

F32 = jnp.float32
BF = jnp.bfloat16
MESH = pl.DeviceIdType.MESH
VMEM = pl.BlockSpec(memory_space=pltpu.VMEM)
ANY = pl.BlockSpec(memory_space=pl.ANY)
LIMIT = 60 * 1024 * 1024


def mm(a, b, ca, cb):
    return lax.dot_general(a, b, (((ca,), (cb,)), ((), ())), preferred_element_type=F32)


def loop(n, body):
    lax.fori_loop(0, n, lambda i, c: (body(i), c)[1], 0)


def remote(src, dst, send, recv, device):
    return pltpu.make_async_remote_copy(
        src_ref=src, dst_ref=dst, send_sem=send, recv_sem=recv, device_id=device, device_id_type=MESH
    )


def params(cid):
    return pltpu.CompilerParams(collective_id=cid, has_side_effects=True, vmem_limit_bytes=LIMIT)


def where_am_i():
    return tuple(lax.axis_index(a) for a in ("section", "z", "x"))


def exchange_kernel(sizes, w_ref, act_ref, w_all, act_all, ws, wr, asend, arecv, lsem):
    n_s, n_z, n_x = sizes
    s, z, x = where_am_i()
    barrier = pltpu.get_barrier_semaphore()
    diag = s == z

    def greet(k):
        @pl.when(jnp.logical_not(jnp.logical_and(k == z, diag)))
        def _():
            pl.semaphore_signal(barrier, inc=1, device_id=(z, k, x), device_id_type=MESH)
            pl.semaphore_signal(barrier, inc=1, device_id=(k, s, x), device_id_type=MESH)

    loop(n_z, greet)
    for k in range(1, n_x):
        pl.semaphore_signal(
            barrier, inc=1, device_id=(s, z, lax.rem(x + k, n_x)), device_id_type=MESH
        )
    pl.semaphore_wait(barrier, 2 * n_z + n_x - 1 - jnp.where(diag, 2, 0))

    def w_copy(to, slot):
        return remote(w_ref, w_all.at[slot], ws.at[to], wr.at[slot], (z, to, x))

    def a_copy(to, slot):
        return remote(act_ref.at[to], act_all.at[slot], asend.at[to], arecv.at[slot], (s, z, to))

    def each(n, skip, fn):
        def body(k):
            @pl.when(jnp.logical_not(skip(k)))
            def _():
                fn(k)

        loop(n, body)

    def is_me(k):
        return jnp.logical_and(k == z, diag)

    def from_me(k):
        return jnp.logical_and(k == s, diag)

    each(n_z, is_me, lambda k: w_copy(k, s).start())
    each(n_x, lambda k: k == x, lambda k: a_copy(k, x).start())
    own = pltpu.make_async_copy(act_ref.at[x], act_all.at[x], lsem.at[0])
    own.start()

    @pl.when(diag)
    def _():
        mine = pltpu.make_async_copy(w_ref, w_all.at[s], lsem.at[1])
        mine.start()
        mine.wait()

    own.wait()
    each(n_x, lambda k: k == x, lambda k: a_copy(k, k).wait_recv())
    each(n_s, from_me, lambda k: w_copy(lax.rem(z + 1, n_z), k).wait_recv())
    each(n_x, lambda k: k == x, lambda k: a_copy(k, x).wait_send())
    each(n_z, is_me, lambda k: w_copy(k, s).wait_send())


def exchange(sizes, w, act):
    n_s, n_z, n_x = sizes
    dma = pltpu.SemaphoreType.DMA
    return pl.pallas_call(
        functools.partial(exchange_kernel, sizes),
        out_shape=(
            jax.ShapeDtypeStruct((n_s, *w.shape), w.dtype),
            jax.ShapeDtypeStruct(act.shape, act.dtype),
        ),
        in_specs=[ANY, ANY],
        out_specs=(ANY, ANY),
        scratch_shapes=[dma((n_z,)), dma((n_s,)), dma((n_x,)), dma((n_x,)), dma((2,))],
        compiler_params=params(0),
        name="exchange",
    )(w, act)


class Plane:
    def __init__(self, sizes):
        n_s, n_z, n_x = sizes
        self.n_x = n_x
        self.chips = (n_s // 2) * n_x
        self.s, self.z, self.x = where_am_i()
        self.core = lax.rem(self.s, 2)
        self.chip = (self.s // 2) * n_x + self.x
        self.partner = (self.s + 1 - 2 * self.core, self.z, self.x)

    def peer(self, chip):
        return (2 * (chip // self.n_x) + self.core, self.z, lax.rem(chip, self.n_x))

    def ahead(self, k):
        return lax.rem(self.chip + k, self.chips)

    def behind(self, k):
        return lax.rem(self.chip + self.chips - k, self.chips)

    def others(self, fn):
        loop(self.chips - 1, lambda k: fn(k + 1))

    def greet_all(self, barrier):
        def one(chip):
            s2, z2, x2 = self.peer(chip)
            pl.semaphore_signal(barrier, inc=1, device_id=(s2, z2, x2), device_id_type=MESH)
            pl.semaphore_signal(
                barrier, inc=1, device_id=(s2 + 1 - 2 * self.core, z2, x2), device_id_type=MESH
            )

        self.others(lambda k: one(self.ahead(k)))
        pl.semaphore_signal(barrier, inc=1, device_id=self.partner, device_id_type=MESH)
        return 2 * self.chips - 1


class Cast:
    def __init__(self, plane, view, sems):
        self.p, self.view, self.sems = plane, view, sems

    def far(self, chip, owner):
        send, recv = self.sems[0].at[chip], self.sems[1].at[owner]
        ref = self.view(owner, self.p.core)
        return remote(ref, ref, send, recv, self.p.peer(chip))

    def near(self, chip, core):
        ref = self.view(chip, core)
        return remote(ref, ref, self.sems[2].at[chip], self.sems[3].at[chip], self.p.partner)

    def start(self):
        p = self.p
        p.others(lambda k: self.far(p.ahead(k), p.chip).start())
        self.near(p.chip, p.core).start()

    def relay(self):
        p = self.p

        def one(k):
            chip = p.behind(k)
            self.far(chip, chip).wait_recv()
            self.near(chip, p.core).start()

        p.others(one)

    def finish(self):
        p = self.p
        loop(p.chips, lambda i: self.near(i, 1 - p.core).wait_recv())
        loop(p.chips, lambda i: self.near(i, p.core).wait_send())
        p.others(lambda k: self.far(p.ahead(k), p.chip).wait_send())


def solve_kernel(
    sizes, dims, w_all, act_all, low_out, err_out,
    gsend, grecv, gz, gram, pbuf, prev, psum, crev, state, snap, full, rin,
    gs, gr, zs, zr, ps, pr, cs, cr, m0, m1, m2, m3, l0, l1, l2, l3, e0, e1, e2, e3,
):
    n_s, n_z, n_x = sizes
    rows, cols, rank, width = dims
    layers = n_s
    own = rows // n_s
    part = rank // n_x
    p = Plane(sizes)
    barrier = pltpu.get_barrier_semaphore()
    count = p.greet_all(barrier)
    for k in range(1, n_z):
        pl.semaphore_signal(
            barrier, inc=1, device_id=(p.s, lax.rem(p.z + k, n_z), p.x), device_id_type=MESH
        )
    mine = w_all[p.z, :cols, rank:]
    for l in range(layers):
        g = mm(mine, w_all[l, :cols], 0, 0).astype(BF)
        gsend[l] = g.reshape(n_x, part, 2 * rank)
    pl.semaphore_wait(barrier, count + n_z - 1)
    n_plane = 2 * p.chips
    me = p.s * n_x + p.x

    def g_copy(to, slot):
        return remote(
            gsend.at[to // n_x, lax.rem(to, n_x)], grecv.at[slot], gs.at[to], gr.at[slot],
            (to // n_x, p.z, lax.rem(to, n_x)),
        )

    loop(n_plane - 1, lambda k: g_copy(lax.rem(me + 1 + k, n_plane), me).start())
    for l in range(layers):
        for i in range(n_x):
            zy = mm(act_all[i, :rows], w_all[l, :cols], 1, 0).astype(BF)
            ct = mm(act_all[i, rows : 2 * rows], w_all[l, :cols, rank:], 1, 0).astype(BF)
            at = slice(i * n_s, (i + 1) * n_s)
            for c, value in enumerate((zy[:, :rank], zy[:, rank:], ct)):
                r0 = (c * layers + l) * own
                pbuf[at, r0 : r0 + own, :] = value.reshape(n_s, own, rank)
    for i in range(n_x):
        xf = act_all[i, :rows].astype(F32)
        sq = jnp.broadcast_to(jnp.sum(xf * xf, -1, keepdims=True), (rows, rank)).astype(BF)
        pbuf[i * n_s : (i + 1) * n_s, 3 * layers * own :, :] = sq.reshape(n_s, own, rank)

    def block(chip, core):
        return (2 * (chip // n_x) + core) * n_x + lax.rem(chip, n_x)

    def pre(i):
        return remote(pbuf.at[block(i, 1 - p.core)], prev.at[i], ps.at[i], pr.at[i], p.partner)

    def pre_wait(i):
        return remote(pbuf.at[block(i, p.core)], prev.at[i], ps.at[i], pr.at[i], p.partner)

    def c_copy(to, slot):
        return remote(psum.at[to], crev.at[slot], cs.at[to], cr.at[slot], p.peer(to))

    loop(p.chips, lambda k: pre(p.ahead(k)).start())

    loop(n_plane - 1, lambda k: g_copy(me, lax.rem(me + n_plane - 1 - k, n_plane)).wait_recv())
    grecv[me] = gsend[p.s, p.x]
    gsum = grecv[0].astype(F32)
    for k in range(1, n_plane):
        gsum = gsum + grecv[k].astype(F32)
    gz[...] = gsum.astype(BF)

    def z_copy(to, slot):
        return remote(
            gz, gram.at[p.s, p.x, slot], zs.at[to], zr.at[slot], (p.s, to, p.x)
        )

    loop(n_z - 1, lambda k: z_copy(lax.rem(p.z + 1 + k, n_z), p.z).start())
    gram[p.s, p.x, p.z] = gz[...]

    def forward(k):
        i = p.ahead(k)
        pre_wait(i).wait_recv()
        total = pbuf[block(i, p.core)].astype(F32) + prev[i].astype(F32)
        psum[i] = total.astype(BF)

        @pl.when(i != p.chip)
        def _():
            c_copy(i, p.chip).start()

    loop(p.chips, lambda k: forward(lax.rem(k + 1, p.chips)))

    loop(n_z - 1, lambda k: z_copy(p.z, lax.rem(p.z + n_z - 1 - k, n_z)).wait_recv())

    def gram_view(chip, core):
        return gram.at[2 * (chip // n_x) + core, lax.rem(chip, n_x)]

    spread = Cast(p, gram_view, (m0, m1, m2, m3))
    spread.start()
    p.others(lambda k: c_copy(p.chip, p.behind(k)).wait_recv())
    total = psum[p.chip].astype(F32)

    crev[p.chip] = psum[p.chip]
    total = crev[0].astype(F32)
    for k in range(1, p.chips):
        total = total + crev[k].astype(F32)
    state[...] = total.reshape(3 * layers + 1, own, rank)
    spread.relay()
    spread.finish()

    def low_view(chip, core):
        dev = block(chip, core)
        return low_out.at[:, pl.ds(pl.multiple_of(dev * own, own), own), :]

    def err_view(chip, core):
        dev = block(chip, core)
        return err_out.at[:, pl.ds(pl.multiple_of(dev * own, own), own), :]

    here = pl.ds(pl.multiple_of(me * own, own), own)
    square = state[3 * layers]
    zero = jnp.zeros((own, rank), F32)
    lane = lax.broadcasted_iota(jnp.int32, (own, rank), 1)
    scal = zero
    for l in range(layers):
        rinv = lax.rsqrt(square / width + 1e-05)
        u = state[l] * rinv
        low = u.astype(BF)
        full[l] = u
        rin[l] = rinv
        low_out[l, here, :] = low
        before = state[layers + l]
        for j in range(layers):
            snap[l, j] = state[layers + j]
            if j > l:
                both = mm(low, gram[j, :, l].reshape(rank, 2 * rank), 1, 0)
                state[j] = state[j] + both[:, :rank]
                state[layers + j] = state[layers + j] + both[:, rank:]
            else:
                one = mm(low, gram[j, :, l, :, rank:].reshape(rank, rank), 1, 0)
                state[layers + j] = state[layers + j] + one
        after = state[layers + l]
        square = square + jnp.sum(low.astype(F32) * (before + after), -1, keepdims=True)
        high = rinv.astype(BF).astype(F32)
        scal = jnp.where(lane == l, high, scal)
        scal = jnp.where(lane == layers + l, rinv - high, scal)
    lows = Cast(p, low_view, (l0, l1, l2, l3))
    lows.start()
    for l in range(layers - 1, -1, -1):
        err = state[2 * layers + l].astype(BF)
        mean = jnp.sum(err.astype(F32) * full[l], -1, keepdims=True) / width
        rinv = rin[l]
        cor = rinv * rinv * mean
        for j in range(l):
            back = mm(err, gram[l, :, j, :, :rank].reshape(rank, rank), 1, 1)
            state[2 * layers + j] = state[2 * layers + j] + rinv * back - cor * snap[l, j]
        err_out[l, here, :] = err
        scal = jnp.where(lane == 2 * layers + l, cor, scal)
    err_out[layers, here, :] = scal.astype(BF)
    errs = Cast(p, err_view, (e0, e1, e2, e3))
    errs.start()
    lows.relay()
    errs.relay()
    lows.finish()
    errs.finish()
    loop(n_plane - 1, lambda k: g_copy(lax.rem(me + 1 + k, n_plane), me).wait_send())
    loop(n_z - 1, lambda k: z_copy(lax.rem(p.z + 1 + k, n_z), p.z).wait_send())
    loop(p.chips, lambda k: pre(p.ahead(k)).wait_send())
    p.others(lambda k: c_copy(p.ahead(k), p.chip).wait_send())


def solve(sizes, dims, w_all, act_all):
    n_s, n_z, n_x = sizes
    rows, cols, rank, width = dims
    layers = n_s
    chips = (n_s // 2) * n_x
    plane = n_s * n_x
    own = rows // n_s
    group = rows * n_x
    part = rank // n_x
    high = (3 * layers + 1) * own
    dma = pltpu.SemaphoreType.DMA
    v = pltpu.VMEM
    return pl.pallas_call(
        functools.partial(solve_kernel, sizes, dims),
        out_shape=(
            jax.ShapeDtypeStruct((layers, group, rank), BF),
            jax.ShapeDtypeStruct((layers + 1, group, rank), BF),
        ),
        in_specs=[VMEM, VMEM],
        out_specs=(VMEM, VMEM),
        scratch_shapes=[
            v((n_s, n_x, part, 2 * rank), BF),
            v((plane, part, 2 * rank), BF),
            v((part, 2 * rank), BF),
            v((n_s, n_x, n_z, part, 2 * rank), BF),
            v((plane, high, rank), BF),
            v((chips, high, rank), BF),
            v((chips, high, rank), BF),
            v((chips, high, rank), BF),
            v((3 * layers + 1, own, rank), F32),
            v((layers, layers, own, rank), F32),
            v((layers, own, rank), F32),
            v((layers, own, rank), F32),
            dma((plane,)), dma((plane,)), dma((n_z,)), dma((n_z,)),
        ]
        + [dma((chips,))] * 16,
        compiler_params=params(1),
        name="solve",
    )(w_all, act_all)


def finish_kernel(
    sizes, dims, bound, w_all, act_all, low_ref, err_ref, gi_out, go_out, uw_out,
    normed, deltas, hold, tot, gbuf, grecv, ts, tr, gs, gr, lsem,
):
    n_s, n_z, n_x = sizes
    rows, cols, rank, width, users = dims
    layers = n_s
    p = Plane(sizes)
    s, z, x = p.s, p.z, p.x
    barrier = pltpu.get_barrier_semaphore()
    count = p.greet_all(barrier)
    to_me = jnp.logical_and(s == z, True)

    def greet(k):
        @pl.when(jnp.logical_not(jnp.logical_and(to_me, k == s)))
        def _():
            pl.semaphore_signal(barrier, inc=1, device_id=(k, s, x), device_id_type=MESH)
            pl.semaphore_signal(barrier, inc=1, device_id=(z, k, x), device_id_type=MESH)

    loop(n_s, greet)
    count = count + 2 * n_s - jnp.where(to_me, 2, 0)

    sums = []
    for i in range(n_x):
        at = slice(i * rows, (i + 1) * rows)
        keyrow = act_all[i, 2 * rows : 2 * rows + 8].astype(F32)[0:1, :rows]
        keys = jnp.broadcast_to(keyrow, (rows, rows))
        same = keys == keys.T
        scal = err_ref[layers, at].astype(F32)
        h = act_all[i, :rows].astype(F32)
        pairs = jnp.zeros((rows, rows), F32)
        for l in range(layers):
            gain = w_all[l, cols : cols + 8].astype(F32)[0:1, :]
            rinv = scal[:, l : l + 1] + scal[:, layers + l : layers + l + 1]
            n = (h * rinv * gain).astype(BF)
            e = err_ref[l, at]
            normed[l, at] = n
            hold[l] = h.astype(BF)
            pairs = pairs + mm(n, n, 1, 1) * mm(e, e, 1, 1)
            if l + 1 < layers:
                h = h + mm(low_ref[l, at], w_all[l, :cols, rank:], 1, 1)
        d = act_all[i, rows : 2 * rows].astype(F32)
        for l in range(layers - 1, -1, -1):
            db = d.astype(BF)
            deltas[l, at] = db
            lo = low_ref[l, at]
            pairs = pairs + mm(lo, lo, 1, 1) * mm(db, db, 1, 1)
            if l > 0:
                rinv = scal[:, l : l + 1] + scal[:, layers + l : layers + l + 1]
                cor = scal[:, 2 * layers + l : 2 * layers + l + 1]
                d = d + rinv * mm(err_ref[l, at], w_all[l, :cols, :rank], 1, 1)
                d = d - cor * hold[l].astype(F32)
        pairs = jnp.where(same, pairs, 0.0)
        rowsum = jnp.broadcast_to(jnp.sum(pairs, -1, keepdims=True), (rows, rows))
        sums.append(jnp.sum(jnp.where(same, rowsum, 0.0), 0, keepdims=True))
    me = s * n_x + x
    n_plane = n_s * n_x
    pad = [jnp.zeros((8 - n_x, rows), F32)] if n_x < 8 else []
    tot[me] = jnp.concatenate(sums + pad, 0)
    pl.semaphore_wait(barrier, count)

    def t_copy(to, slot):
        return remote(
            tot.at[slot], tot.at[slot], ts.at[to], tr.at[slot], (to // n_x, z, lax.rem(to, n_x))
        )

    loop(n_plane - 1, lambda k: t_copy(lax.rem(me + 1 + k, n_plane), me).start())
    loop(n_plane - 1, lambda k: t_copy(me, lax.rem(me + n_plane - 1 - k, n_plane)).wait_recv())
    total = tot[0]
    for k in range(1, n_plane):
        total = total + tot[k]
    clip = bound / jnp.maximum(jnp.sqrt(total), bound)

    weights = []
    for i in range(n_x):
        inc = act_all[i, 2 * rows : 2 * rows + 8].astype(F32)[1:2, :rows]
        w = jnp.broadcast_to(inc * clip[i : i + 1], (rows, rows))
        weights.append(w.T[:, :rank])

        @pl.when(x == i)
        def _(w=w, i=i):
            keyrow = act_all[i, 2 * rows : 2 * rows + 8].astype(F32)[0:1, :rows]
            which = lax.broadcasted_iota(jnp.int32, (users, rows), 0).astype(F32)
            mine = jnp.where(which == keyrow, w[:users], 0.0)
            uw_out[...] = jnp.broadcast_to(jnp.max(mine, -1, keepdims=True), (users, rows))

    weight = jnp.concatenate(weights, 0)

    def g_copy(to, slot):
        return remote(gbuf.at[to], grecv.at[slot], gs.at[to], gr.at[slot], (to, s, x))

    for l in range(layers):
        we = (weight * err_ref[l].astype(F32)).astype(BF)
        wl = (weight * low_ref[l].astype(F32)).astype(BF)
        gbuf[l, :, :rank] = mm(normed[l], we, 0, 0).astype(BF)
        gbuf[l, :, rank:] = mm(deltas[l], wl, 0, 0).astype(BF)

        @pl.when(jnp.logical_not(jnp.logical_and(to_me, s == l)))
        def _(l=l):
            g_copy(l, z).start()

    @pl.when(to_me)
    def _():
        mine = pltpu.make_async_copy(gbuf.at[s], grecv.at[z], lsem.at[0])
        mine.start()
        mine.wait()

    def others(fn):
        def body(k):
            @pl.when(jnp.logical_not(jnp.logical_and(to_me, k == s)))
            def _():
                fn(k)

        loop(n_s, body)

    others(lambda k: g_copy(lax.rem(s + 1, n_s), k).wait_recv())
    grad = grecv[0].astype(F32)
    for k in range(1, n_z):
        grad = grad + grecv[k].astype(F32)
    gi_out[...] = grad[:, :rank]
    go_out[...] = grad[:, rank:].T
    others(lambda k: g_copy(k, z).wait_send())
    loop(n_plane - 1, lambda k: t_copy(lax.rem(me + 1 + k, n_plane), me).wait_send())


def finish(sizes, dims, bound, w_all, act_all, low, err):
    n_s, n_z, n_x = sizes
    rows, cols, rank, width, users = dims
    layers = n_s
    plane = n_s * n_x
    dma = pltpu.SemaphoreType.DMA
    v = pltpu.VMEM
    return pl.pallas_call(
        functools.partial(finish_kernel, sizes, dims, bound),
        out_shape=(
            jax.ShapeDtypeStruct((cols, rank), F32),
            jax.ShapeDtypeStruct((rank, cols), F32),
            jax.ShapeDtypeStruct((users, rows), F32),
        ),
        in_specs=[VMEM] * 4,
        out_specs=(VMEM,) * 3,
        scratch_shapes=[
            v((layers, rows * n_x, cols), BF),
            v((layers, rows * n_x, cols), BF),
            v((layers, rows, cols), BF),
            v((plane, 8, rows), F32),
            v((layers, cols, 2 * rank), BF),
            v((n_z, cols, 2 * rank), BF),
            dma((plane,)), dma((plane,)), dma((n_s,)), dma((n_z,)), dma((1,)),
        ],
        compiler_params=params(2),
        name="finish",
    )(w_all, act_all, low, err)


def shards(hidden_in, cotangent, adapter_in, adapter_out, norm_gain, user_of_row, included):
    sizes = tuple(lax.axis_size(a) for a in ("section", "z", "x"))
    n_s, n_z, n_x = sizes
    s, zi, xi = where_am_i()
    micro, rows, width = hidden_in.shape
    cols, rank = adapter_in.shape[1:]
    users = included.shape[1]
    dev_rows = micro * rows
    a = adapter_in[0]
    g = (a.astype(F32) * norm_gain[0].astype(F32)[:, None]).astype(BF)
    w = jnp.concatenate([g, adapter_out[0].T], 1)
    w = jnp.concatenate([w, jnp.broadcast_to(norm_gain, (16, cols))], 0)
    base = (zi * n_x + xi) * users
    local = user_of_row - base
    key = (local + users * jnp.arange(micro, dtype=jnp.int32)[:, None]).reshape(1, dev_rows)
    onehot = local[:, :, None] == jnp.arange(users, dtype=jnp.int32)
    inc = jnp.sum(jnp.where(onehot, included[:, None, :], 0), -1).reshape(1, dev_rows)
    info = jnp.pad(jnp.concatenate([key, inc], 0).astype(BF), ((0, 14), (0, cols - dev_rows)))
    span = n_x * cols

    def slab(array):
        flat = lax.dynamic_slice_in_dim(array.reshape(dev_rows, width), s * span, span, 1)
        return jnp.moveaxis(flat.reshape(dev_rows, n_x, cols), 1, 0)

    act = jnp.concatenate(
        [slab(hidden_in), slab(cotangent), jnp.broadcast_to(info, (n_x, 16, cols))], 1
    )
    w_all, act_all = exchange(sizes, w, act)
    low, err = solve(sizes, (dev_rows, cols, rank, width), w_all, act_all)
    bound = 0.8 * math.sqrt(n_s * (rows // users) * width * width)
    gi, go, uw = finish(
        sizes, (dev_rows, cols, rank, width, micro * users), bound, w_all, act_all, low, err
    )
    return (gi[None], go[None], uw[:, 0].reshape(micro, users))


def build(torus):
    dp = ("z", "x")
    return jax.shard_map(
        shards,
        mesh=torus,
        in_specs=(
            P(None, dp, None),
            P(None, dp, None),
            P("section", dp, None),
            P("section", None, dp),
            P("section", dp),
            P(None, dp),
            P(None, dp),
        ),
        out_specs=(P("section", dp, None), P("section", None, dp), P(None, dp)),
        check_vma=False,
    )


def solution(mesh):
    return build(Mesh(mesh.devices.reshape(mesh.shape["section"], 8, 4), ("section", "z", "x")))
```

time: 462 us -> 240 us (0.52)
  the two profiles are of different devices: /device:TPU:1 before, /device:TPU:89 now
where the time goes in v2:
time: 240 us; the launch traced here: 239 us
  Pallas kernels  226 us (94%)
  local copies, waits for them, and re-layouts  7.49 us (3%)
  other arithmetic  4.7 us (2%)
    pallas_call x1, Pallas kernels, finish(): pl.pallas_call(functools.partial(finish_kernel, sizes, dims, bound), out_...  97.2 us
    pallas_call x1, Pallas kernels, solve(): pl.pallas_call(functools.partial(solve_kernel, sizes, dims), out_shape=(j...  89.4 us
    pallas_call x1, Pallas kernels, exchange(): pl.pallas_call(functools.partial(exchange_kernel, sizes), out_shape=(jax....  39.8 us

profile of v2, /device:TPU:89, one launch (start us, length us, event | category | flops | bytes accessed | tf_op | source)
XLA Modules:
  0.0 239.4 jit_solution(14349779551545075868)
XLA Ops:
  0.6 0.7 reduce
  1.3 0.8 add_convert_fusion
  2.1 0.1 reshape.44
  2.2 0.8 select_reduce_fusion
  3.0 0.1 reshape.45
  3.1 0.9 fusion
  4.0 1.0 copy.27
  5.0 0.7 pad_maximum_fusion.1.w_ref
  5.7 1.1 constant_dynamic-slice_fusion
  6.7 0.2 copy.30
  6.9 0.1 copy.31
  7.1 0.2 copy.28
  7.2 0.1 copy.29
  7.4 0.8 pad_maximum_fusion.act_ref
  8.2 39.8 %exchange.1 = (bf16[8,272,256]{2,1,0:T(8,128)(2,1)}, bf16[4,272,256]{2,1,0:T(8,128)(2,1)}) custom-call(bf16[272,256]{1,0:T(8,128)(2,1)} %pad_maximum_fusion.1.w_ref, bf16[4,272,256]{2,1,0:T(8,128)(2,1)} %pad_maximum_fusion.act_ref), custom_call_target="tpu_custom_call" | custom-call | tf_op jit(solution)/shard_map/exchange/pallas_call | solution.py:102
  48.1 89.4 %solve.1 = (bf16[8,512,128]{2,1,0:T(8,128)(2,1)}, bf16[9,512,128]{2,1,0:T(8,128)(2,1)}) custom-call(bf16[8,272,256]{2,1,0:T(8,128)(2,1)} %get-tuple-element.10.w_all, bf16[4,272,256]{2,1,0:T(8,128)(2,1)} %get-tuple-element.11.act_all), custom_call_target="tpu_custom_call" | custom-call | tf_op jit(solution)/shard_map/solve/pallas_call | solution.py:362
  137.5 97.2 %finish.1 = (f32[256,128]{1,0:T(8,128)}, f32[128,256]{1,0:T(8,128)}, f32[8,128]{1,0:T(8,128)}) custom-call(bf16[8,272,256]{2,1,0:T(8,128)(2,1)} %get-tuple-element.10.w_all, bf16[4,272,256]{2,1,0:T(8,128)(2,1)} %get-tuple-element.11.act_all, bf16[8,512,128]{2,1,0:T(8,128)(2,1)} %get-tuple-element.12.low_ref, bf16[9,512,128]{2,1,0:T(8,128)(2,1)} %get-tuple-element.13.err_ref), custom_call_target="tpu_custom_call" | custom-call | tf_op jit(solution)/shard_map/finish/pallas_call | solution.py:523
  234.7 0.8 slice_reduce_fusion
  235.5 0.1 reshape_squeeze.3
  235.6 0.7 copy.32
  236.3 1.6 copy.35
  237.8 1.6 copy.36
  (6 shorter events, 0.0 us)

commit v3 on v2

--- a/solution.py
+++ b/solution.py
@@ -39,78 +39,159 @@
     return tuple(lax.axis_index(a) for a in ("section", "z", "x"))
 
 
-def exchange_kernel(sizes, w_ref, act_ref, w_all, act_all, ws, wr, asend, arecv, lsem):
+class Ring:
+    def __init__(self, n, me, place, view, pieces, sems):
+        self.n, self.me, self.place, self.view, self.pieces, self.sems = n, me, place, view, pieces, sems
+        self.steps = (n // 2, n - 1 - n // 2)
+
+    def copy(self, way, step, piece, from_me):
+        n, me = self.n, self.me
+        sign = 1 - 2 * way
+        block = (me - sign * step) if from_me else (me - sign * (step + 1))
+        ref = self.view(lax.rem(block + 2 * n, n), piece)
+        send, recv = self.sems[2 * way].at[step, piece], self.sems[2 * way + 1].at[step, piece]
+        return remote(ref, ref, send, recv, self.place(lax.rem(me + sign + n, n)))
+
+    def start(self):
+        for piece in range(self.pieces):
+            for way in (0, 1):
+                self.copy(way, 0, piece, True).start()
+
+    def run(self, arrived):
+        for step in range(self.steps[0]):
+            for piece in range(self.pieces):
+                for way in (0, 1):
+                    if step < self.steps[way]:
+                        self.copy(way, step, piece, False).wait_recv()
+                        if step + 1 < self.steps[way]:
+                            self.copy(way, step + 1, piece, True).start()
+                        sign = 1 - 2 * way
+                        block = lax.rem(self.me - sign * (step + 1) + 2 * self.n, self.n)
+                        arrived(block, piece)
+
+    def finish(self):
+        for way in (0, 1):
+            for step in range(self.steps[way]):
+                for piece in range(self.pieces):
+                    self.copy(way, step, piece, True).wait_send()
+
+
+def exchange_kernel(
+    sizes, a_ref, b_ref, g_ref, hid_ref, cot_ref, info_ref, w_all, h_all, c_all, i_all,
+    column, rs, rr, ls, lr, ys, yr, asend, arecv, lsem,
+):
     n_s, n_z, n_x = sizes
     s, z, x = where_am_i()
+    cols, rank = a_ref.shape
     barrier = pltpu.get_barrier_semaphore()
-    diag = s == z
-
-    def greet(k):
-        @pl.when(jnp.logical_not(jnp.logical_and(k == z, diag)))
-        def _():
-            pl.semaphore_signal(barrier, inc=1, device_id=(z, k, x), device_id_type=MESH)
-            pl.semaphore_signal(barrier, inc=1, device_id=(k, s, x), device_id_type=MESH)
-
-    loop(n_z, greet)
+    for k in range(1, n_s):
+        pl.semaphore_signal(
+            barrier, inc=1, device_id=(lax.rem(s + k, n_s), z, x), device_id_type=MESH
+        )
+    for k in (1, n_z - 1):
+        pl.semaphore_signal(
+            barrier, inc=1, device_id=(s, lax.rem(z + k, n_z), x), device_id_type=MESH
+        )
     for k in range(1, n_x):
         pl.semaphore_signal(
             barrier, inc=1, device_id=(s, z, lax.rem(x + k, n_x)), device_id_type=MESH
         )
-    pl.semaphore_wait(barrier, 2 * n_z + n_x - 1 - jnp.where(diag, 2, 0))
-
-    def w_copy(to, slot):
-        return remote(w_ref, w_all.at[slot], ws.at[to], wr.at[slot], (z, to, x))
-
-    def a_copy(to, slot):
-        return remote(act_ref.at[to], act_all.at[slot], asend.at[to], arecv.at[slot], (s, z, to))
-
-    def each(n, skip, fn):
+    gain = jnp.broadcast_to(g_ref[...].astype(F32), (rank, cols))
+    column[z, :cols, :rank] = (a_ref[...].astype(F32) * gain.T).astype(BF)
+    column[z, :cols, rank:] = b_ref[...].astype(F32).T.astype(BF)
+    column[z, cols:, :] = jnp.broadcast_to(g_ref[...].astype(F32), (16, cols)).astype(BF)
+    pl.semaphore_wait(barrier, n_s - 1 + 2 + n_x - 1)
+
+    def act(which, to, slot):
+        at = pl.ds(pl.multiple_of((s * n_x + to) * cols, cols), cols)
+        src = (hid_ref.at[:, :, at], cot_ref.at[:, :, at], info_ref)[which]
+        dst = (h_all, c_all, i_all)[which].at[slot]
+        return src, dst
+
+    def a_copy(which, to, slot):
+        src, dst = act(which, to, slot)
+        return remote(src, dst, asend.at[which, to], arecv.at[which, slot], (s, z, to))
+
+    split = cols // 2
+
+    def view(block, piece):
+        return column.at[block, :split] if piece == 0 else column.at[block, split:]
+
+    ring = Ring(n_z, z, lambda to: (s, to, x), view, 2, (rs, rr, ls, lr))
+    ring.start()
+    for which in range(3):
+        for k in range(1, n_x):
+            a_copy(which, lax.rem(x + k, n_x), x).start()
+    for which in range(3):
+        src, dst = act(which, x, x)
+        pltpu.make_async_copy(src, dst, lsem.at[which]).start()
+
+    def y_copy(block, slot):
+        return remote(column.at[block], w_all.at[slot], ys.at[block], yr.at[slot], (block, z, x))
+
+    def keep():
+        return pltpu.make_async_copy(column.at[s], w_all.at[s], lsem.at[3])
+
+    def onward(block):
+        @pl.when(block == s)
+        def _():
+            keep().start()
+
+        @pl.when(block != s)
+        def _():
+            y_copy(block, s).start()
+
+    onward(z)
+
+    def arrived(block, piece):
+        if piece == 1:
+            onward(block)
+
+    ring.run(arrived)
+    for which in range(3):
+        src, dst = act(which, x, x)
+        pltpu.make_async_copy(src, dst, lsem.at[which]).wait()
+        for k in range(1, n_x):
+            a_copy(which, x, lax.rem(x + n_x - k, n_x)).wait_recv()
+    keep().wait()
+
+    def not_me(fn):
         def body(k):
-            @pl.when(jnp.logical_not(skip(k)))
-            def _():
-                fn(k)
-
-        loop(n, body)
-
-    def is_me(k):
-        return jnp.logical_and(k == z, diag)
-
-    def from_me(k):
-        return jnp.logical_and(k == s, diag)
-
-    each(n_z, is_me, lambda k: w_copy(k, s).start())
-    each(n_x, lambda k: k == x, lambda k: a_copy(k, x).start())
-    own = pltpu.make_async_copy(act_ref.at[x], act_all.at[x], lsem.at[0])
-    own.start()
-
-    @pl.when(diag)
-    def _():
-        mine = pltpu.make_async_copy(w_ref, w_all.at[s], lsem.at[1])
-        mine.start()
-        mine.wait()
-
-    own.wait()
-    each(n_x, lambda k: k == x, lambda k: a_copy(k, k).wait_recv())
-    each(n_s, from_me, lambda k: w_copy(lax.rem(z + 1, n_z), k).wait_recv())
-    each(n_x, lambda k: k == x, lambda k: a_copy(k, x).wait_send())
-    each(n_z, is_me, lambda k: w_copy(k, s).wait_send())
-
-
-def exchange(sizes, w, act):
+            fn(lax.rem(s + 1 + k, n_s))
+
+        loop(n_s - 1, body)
+
+    not_me(lambda k: y_copy(s, k).wait_recv())
+    not_me(lambda k: y_copy(k, s).wait_send())
+    for which in range(3):
+        for k in range(1, n_x):
+            a_copy(which, lax.rem(x + k, n_x), x).wait_send()
+    ring.finish()
+
+
+def exchange(sizes, a, b, g, hidden, cot, info):
     n_s, n_z, n_x = sizes
+    cols, rank = a.shape
     dma = pltpu.SemaphoreType.DMA
+    part = (n_x, *hidden.shape[:2], cols)
     return pl.pallas_call(
         functools.partial(exchange_kernel, sizes),
         out_shape=(
-            jax.ShapeDtypeStruct((n_s, *w.shape), w.dtype),
-            jax.ShapeDtypeStruct(act.shape, act.dtype),
+            jax.ShapeDtypeStruct((n_s, cols + 16, 2 * rank), BF),
+            jax.ShapeDtypeStruct(part, BF),
+            jax.ShapeDtypeStruct(part, BF),
+            jax.ShapeDtypeStruct((n_x, *info.shape), BF),
         ),
-        in_specs=[ANY, ANY],
-        out_specs=(ANY, ANY),
-        scratch_shapes=[dma((n_z,)), dma((n_s,)), dma((n_x,)), dma((n_x,)), dma((2,))],
+        in_specs=[VMEM, VMEM, VMEM, ANY, ANY, ANY],
+        out_specs=(ANY,) * 4,
+        scratch_shapes=[
+            pltpu.VMEM((n_z, cols + 16, 2 * rank), BF),
+            dma((n_z, 2)), dma((n_z, 2)), dma((n_z, 2)), dma((n_z, 2)),
+            dma((n_z,)), dma((n_s,)), dma((3, n_x)), dma((3, n_x)), dma((4,)),
+        ],
         compiler_params=params(0),
         name="exchange",
-    )(w, act)
+    )(a, b, g, hidden, cot, info)
 
 
 class Plane:
@@ -184,9 +265,9 @@
 
 
 def solve_kernel(
-    sizes, dims, w_all, act_all, low_out, err_out,
-    gsend, grecv, gz, gram, pbuf, prev, psum, crev, state, snap, full, rin,
-    gs, gr, zs, zr, ps, pr, cs, cr, m0, m1, m2, m3, l0, l1, l2, l3, e0, e1, e2, e3,
+    sizes, dims, w_all, h_all, c_all, low_out, err_out,
+    gsend, grecv, gram, pbuf, prev, psum, crev, state, snap, full, rin,
+    gs, gr, rs, rr, ls, lr, ns, nr, ps, pr, cs, cr, m0, m1, m2, m3, l0, l1, l2, l3, e0, e1, e2, e3,
 ):
     n_s, n_z, n_x = sizes
     rows, cols, rank, width = dims
@@ -196,7 +277,7 @@
     p = Plane(sizes)
     barrier = pltpu.get_barrier_semaphore()
     count = p.greet_all(barrier)
-    for k in range(1, n_z):
+    for k in (1, n_z - 1):
         pl.semaphore_signal(
             barrier, inc=1, device_id=(p.s, lax.rem(p.z + k, n_z), p.x), device_id_type=MESH
         )
@@ -204,7 +285,7 @@
     for l in range(layers):
         g = mm(mine, w_all[l, :cols], 0, 0).astype(BF)
         gsend[l] = g.reshape(n_x, part, 2 * rank)
-    pl.semaphore_wait(barrier, count + n_z - 1)
+    pl.semaphore_wait(barrier, count + 2)
     n_plane = 2 * p.chips
     me = p.s * n_x + p.x
 
@@ -217,14 +298,14 @@
     loop(n_plane - 1, lambda k: g_copy(lax.rem(me + 1 + k, n_plane), me).start())
     for l in range(layers):
         for i in range(n_x):
-            zy = mm(act_all[i, :rows], w_all[l, :cols], 1, 0).astype(BF)
-            ct = mm(act_all[i, rows : 2 * rows], w_all[l, :cols, rank:], 1, 0).astype(BF)
+            zy = mm(h_all[i], w_all[l, :cols], 1, 0).astype(BF)
+            ct = mm(c_all[i], w_all[l, :cols, rank:], 1, 0).astype(BF)
             at = slice(i * n_s, (i + 1) * n_s)
             for c, value in enumerate((zy[:, :rank], zy[:, rank:], ct)):
                 r0 = (c * layers + l) * own
                 pbuf[at, r0 : r0 + own, :] = value.reshape(n_s, own, rank)
     for i in range(n_x):
-        xf = act_all[i, :rows].astype(F32)
+        xf = h_all[i].astype(F32)
         sq = jnp.broadcast_to(jnp.sum(xf * xf, -1, keepdims=True), (rows, rank)).astype(BF)
         pbuf[i * n_s : (i + 1) * n_s, 3 * layers * own :, :] = sq.reshape(n_s, own, rank)
 
@@ -247,15 +328,23 @@
     gsum = grecv[0].astype(F32)
     for k in range(1, n_plane):
         gsum = gsum + grecv[k].astype(F32)
-    gz[...] = gsum.astype(BF)
-
-    def z_copy(to, slot):
-        return remote(
-            gz, gram.at[p.s, p.x, slot], zs.at[to], zr.at[slot], (p.s, to, p.x)
-        )
-
-    loop(n_z - 1, lambda k: z_copy(lax.rem(p.z + 1 + k, n_z), p.z).start())
-    gram[p.s, p.x, p.z] = gz[...]
+    gram[p.z, p.s, p.x] = gsum.astype(BF)
+
+    def gram_view(chip, core):
+        return gram.at[p.z, 2 * (chip // n_x) + core, lax.rem(chip, n_x)]
+
+    spread = Cast(p, gram_view, (m0, m1, m2, m3))
+    spread.start()
+    spread.relay()
+    spread.finish()
+
+    half = layers // 2
+
+    def ring_view(block, piece):
+        return gram.at[block, half * p.core + piece]
+
+    ring = Ring(n_z, p.z, lambda to: (p.s, to, p.x), ring_view, half, (rs, rr, ls, lr))
+    ring.start()
 
     def forward(k):
         i = p.ahead(k)
@@ -269,23 +358,27 @@
 
     loop(p.chips, lambda k: forward(lax.rem(k + 1, p.chips)))
 
-    loop(n_z - 1, lambda k: z_copy(p.z, lax.rem(p.z + n_z - 1 - k, n_z)).wait_recv())
-
-    def gram_view(chip, core):
-        return gram.at[2 * (chip // n_x) + core, lax.rem(chip, n_x)]
-
-    spread = Cast(p, gram_view, (m0, m1, m2, m3))
-    spread.start()
+    def share(layer, piece, core):
+        ref = gram.at[layer, half * core + piece]
+        return remote(ref, ref, ns.at[layer, piece], nr.at[layer, piece], p.partner)
+
+    ring.run(lambda layer, piece: share(layer, piece, p.core).start())
     p.others(lambda k: c_copy(p.chip, p.behind(k)).wait_recv())
-    total = psum[p.chip].astype(F32)
-
     crev[p.chip] = psum[p.chip]
     total = crev[0].astype(F32)
     for k in range(1, p.chips):
         total = total + crev[k].astype(F32)
     state[...] = total.reshape(3 * layers + 1, own, rank)
-    spread.relay()
-    spread.finish()
+
+    def each_share(fn):
+        def body(k):
+            layer = lax.rem(p.z + 1 + k, n_z)
+            for piece in range(half):
+                fn(layer, piece)
+
+        loop(n_z - 1, body)
+
+    each_share(lambda layer, piece: share(layer, piece, 1 - p.core).wait_recv())
 
     def low_view(chip, core):
         dev = block(chip, core)
@@ -311,11 +404,11 @@
         for j in range(layers):
             snap[l, j] = state[layers + j]
             if j > l:
-                both = mm(low, gram[j, :, l].reshape(rank, 2 * rank), 1, 0)
+                both = mm(low, gram[l, j].reshape(rank, 2 * rank), 1, 0)
                 state[j] = state[j] + both[:, :rank]
                 state[layers + j] = state[layers + j] + both[:, rank:]
             else:
-                one = mm(low, gram[j, :, l, :, rank:].reshape(rank, rank), 1, 0)
+                one = mm(low, gram[l, j, :, :, rank:].reshape(rank, rank), 1, 0)
                 state[layers + j] = state[layers + j] + one
         after = state[layers + l]
         square = square + jnp.sum(low.astype(F32) * (before + after), -1, keepdims=True)
@@ -330,7 +423,7 @@
         rinv = rin[l]
         cor = rinv * rinv * mean
         for j in range(l):
-            back = mm(err, gram[l, :, j, :, :rank].reshape(rank, rank), 1, 1)
+            back = mm(err, gram[j, l, :, :, :rank].reshape(rank, rank), 1, 1)
             state[2 * layers + j] = state[2 * layers + j] + rinv * back - cor * snap[l, j]
         err_out[l, here, :] = err
         scal = jnp.where(lane == 2 * layers + l, cor, scal)
@@ -342,12 +435,13 @@
     lows.finish()
     errs.finish()
     loop(n_plane - 1, lambda k: g_copy(lax.rem(me + 1 + k, n_plane), me).wait_send())
-    loop(n_z - 1, lambda k: z_copy(lax.rem(p.z + 1 + k, n_z), p.z).wait_send())
+    ring.finish()
+    each_share(lambda layer, piece: share(layer, piece, p.core).wait_send())
     loop(p.chips, lambda k: pre(p.ahead(k)).wait_send())
     p.others(lambda k: c_copy(p.ahead(k), p.chip).wait_send())
 
 
-def solve(sizes, dims, w_all, act_all):
+def solve(sizes, dims, w_all, h_all, c_all):
     n_s, n_z, n_x = sizes
     rows, cols, rank, width = dims
     layers = n_s
@@ -365,13 +459,12 @@
             jax.ShapeDtypeStruct((layers, group, rank), BF),
             jax.ShapeDtypeStruct((layers + 1, group, rank), BF),
         ),
-        in_specs=[VMEM, VMEM],
+        in_specs=[VMEM, VMEM, VMEM],
         out_specs=(VMEM, VMEM),
         scratch_shapes=[
             v((n_s, n_x, part, 2 * rank), BF),
             v((plane, part, 2 * rank), BF),
-            v((part, 2 * rank), BF),
-            v((n_s, n_x, n_z, part, 2 * rank), BF),
+            v((n_z, n_s, n_x, part, 2 * rank), BF),
             v((plane, high, rank), BF),
             v((chips, high, rank), BF),
             v((chips, high, rank), BF),
@@ -380,17 +473,18 @@
             v((layers, layers, own, rank), F32),
             v((layers, own, rank), F32),
             v((layers, own, rank), F32),
-            dma((plane,)), dma((plane,)), dma((n_z,)), dma((n_z,)),
+            dma((plane,)), dma((plane,)),
         ]
+        + [dma((n_z, layers // 2))] * 6
         + [dma((chips,))] * 16,
         compiler_params=params(1),
         name="solve",
-    )(w_all, act_all)
+    )(w_all, h_all, c_all)
 
 
 def finish_kernel(
-    sizes, dims, bound, w_all, act_all, low_ref, err_ref, gi_out, go_out, uw_out,
-    normed, deltas, hold, tot, gbuf, grecv, ts, tr, gs, gr, lsem,
+    sizes, dims, bound, w_all, h_all, c_all, i_all, low_ref, err_ref, gi_out, go_out, uw_out,
+    normed, deltas, hold, tot, gbuf, mid, grecv, ts, tr, gs, gr, zs, zr, lsem,
 ):
     n_s, n_z, n_x = sizes
     rows, cols, rank, width, users = dims
@@ -399,25 +493,18 @@
     s, z, x = p.s, p.z, p.x
     barrier = pltpu.get_barrier_semaphore()
     count = p.greet_all(barrier)
-    to_me = jnp.logical_and(s == z, True)
-
-    def greet(k):
-        @pl.when(jnp.logical_not(jnp.logical_and(to_me, k == s)))
-        def _():
-            pl.semaphore_signal(barrier, inc=1, device_id=(k, s, x), device_id_type=MESH)
-            pl.semaphore_signal(barrier, inc=1, device_id=(z, k, x), device_id_type=MESH)
-
-    loop(n_s, greet)
-    count = count + 2 * n_s - jnp.where(to_me, 2, 0)
+    for k in range(1, n_z):
+        pl.semaphore_signal(barrier, inc=1, device_id=(s, lax.rem(z + k, n_z), x), device_id_type=MESH)
+    count = count + n_z - 1
 
     sums = []
     for i in range(n_x):
         at = slice(i * rows, (i + 1) * rows)
-        keyrow = act_all[i, 2 * rows : 2 * rows + 8].astype(F32)[0:1, :rows]
+        keyrow = i_all[i].astype(F32)[0:1, :rows]
         keys = jnp.broadcast_to(keyrow, (rows, rows))
         same = keys == keys.T
         scal = err_ref[layers, at].astype(F32)
-        h = act_all[i, :rows].astype(F32)
+        h = h_all[i].astype(F32)
         pairs = jnp.zeros((rows, rows), F32)
         for l in range(layers):
             gain = w_all[l, cols : cols + 8].astype(F32)[0:1, :]
@@ -429,7 +516,7 @@
             pairs = pairs + mm(n, n, 1, 1) * mm(e, e, 1, 1)
             if l + 1 < layers:
                 h = h + mm(low_ref[l, at], w_all[l, :cols, rank:], 1, 1)
-        d = act_all[i, rows : 2 * rows].astype(F32)
+        d = c_all[i].astype(F32)
         for l in range(layers - 1, -1, -1):
             db = d.astype(BF)
             deltas[l, at] = db
@@ -463,13 +550,13 @@
 
     weights = []
     for i in range(n_x):
-        inc = act_all[i, 2 * rows : 2 * rows + 8].astype(F32)[1:2, :rows]
+        inc = i_all[i].astype(F32)[1:2, :rows]
         w = jnp.broadcast_to(inc * clip[i : i + 1], (rows, rows))
         weights.append(w.T[:, :rank])
 
         @pl.when(x == i)
         def _(w=w, i=i):
-            keyrow = act_all[i, 2 * rows : 2 * rows + 8].astype(F32)[0:1, :rows]
+            keyrow = i_all[i].astype(F32)[0:1, :rows]
             which = lax.broadcasted_iota(jnp.int32, (users, rows), 0).astype(F32)
             mine = jnp.where(which == keyrow, w[:users], 0.0)
             uw_out[...] = jnp.broadcast_to(jnp.max(mine, -1, keepdims=True), (users, rows))
@@ -477,7 +564,10 @@
     weight = jnp.concatenate(weights, 0)
 
     def g_copy(to, slot):
-        return remote(gbuf.at[to], grecv.at[slot], gs.at[to], gr.at[slot], (to, s, x))
+        return remote(gbuf.at[to], mid.at[slot], gs.at[to], gr.at[slot], (to, z, x))
+
+    def z_copy(to, slot):
+        return remote(mid.at[to], grecv.at[slot], zs.at[to], zr.at[slot], (s, to, x))
 
     for l in range(layers):
         we = (weight * err_ref[l].astype(F32)).astype(BF)
@@ -485,35 +575,44 @@
         gbuf[l, :, :rank] = mm(normed[l], we, 0, 0).astype(BF)
         gbuf[l, :, rank:] = mm(deltas[l], wl, 0, 0).astype(BF)
 
-        @pl.when(jnp.logical_not(jnp.logical_and(to_me, s == l)))
+        @pl.when(s != l)
         def _(l=l):
-            g_copy(l, z).start()
-
-    @pl.when(to_me)
-    def _():
-        mine = pltpu.make_async_copy(gbuf.at[s], grecv.at[z], lsem.at[0])
-        mine.start()
-        mine.wait()
-
-    def others(fn):
-        def body(k):
-            @pl.when(jnp.logical_not(jnp.logical_and(to_me, k == s)))
-            def _():
-                fn(k)
-
-        loop(n_s, body)
-
-    others(lambda k: g_copy(lax.rem(s + 1, n_s), k).wait_recv())
+            g_copy(l, s).start()
+
+    local = pltpu.make_async_copy(gbuf.at[s], mid.at[s], lsem.at[0])
+    local.start()
+    local.wait()
+
+    def onward(k):
+        @pl.when(k == z)
+        def _():
+            pltpu.make_async_copy(mid.at[z], grecv.at[z], lsem.at[1]).start()
+
+        @pl.when(k != z)
+        def _():
+            z_copy(k, z).start()
+
+    onward(s)
+
+    def relay(k):
+        at = lax.rem(s + 1 + k, n_s)
+        g_copy(s, at).wait_recv()
+        onward(at)
+
+    loop(n_s - 1, relay)
+    pltpu.make_async_copy(mid.at[z], grecv.at[z], lsem.at[1]).wait()
+    loop(n_z - 1, lambda k: z_copy(z, lax.rem(z + 1 + k, n_z)).wait_recv())
     grad = grecv[0].astype(F32)
     for k in range(1, n_z):
         grad = grad + grecv[k].astype(F32)
     gi_out[...] = grad[:, :rank]
     go_out[...] = grad[:, rank:].T
-    others(lambda k: g_copy(k, z).wait_send())
+    loop(n_s - 1, lambda k: g_copy(lax.rem(s + 1 + k, n_s), s).wait_send())
+    loop(n_z - 1, lambda k: z_copy(lax.rem(z + 1 + k, n_z), z).wait_send())
     loop(n_plane - 1, lambda k: t_copy(lax.rem(me + 1 + k, n_plane), me).wait_send())
 
 
-def finish(sizes, dims, bound, w_all, act_all, low, err):
+def finish(sizes, dims, bound, *arrays):
     n_s, n_z, n_x = sizes
     rows, cols, rank, width, users = dims
     layers = n_s
@@ -527,7 +626,7 @@
             jax.ShapeDtypeStruct((rank, cols), F32),
             jax.ShapeDtypeStruct((users, rows), F32),
         ),
-        in_specs=[VMEM] * 4,
+        in_specs=[VMEM] * 6,
         out_specs=(VMEM,) * 3,
         scratch_shapes=[
             v((layers, rows * n_x, cols), BF),
@@ -535,46 +634,38 @@
             v((layers, rows, cols), BF),
             v((plane, 8, rows), F32),
             v((layers, cols, 2 * rank), BF),
+            v((n_s, cols, 2 * rank), BF),
             v((n_z, cols, 2 * rank), BF),
-            dma((plane,)), dma((plane,)), dma((n_s,)), dma((n_z,)), dma((1,)),
+            dma((plane,)), dma((plane,)), dma((n_s,)), dma((n_s,)), dma((n_z,)), dma((n_z,)), dma((2,)),
         ],
         compiler_params=params(2),
         name="finish",
-    )(w_all, act_all, low, err)
+    )(*arrays)
 
 
 def shards(hidden_in, cotangent, adapter_in, adapter_out, norm_gain, user_of_row, included):
     sizes = tuple(lax.axis_size(a) for a in ("section", "z", "x"))
     n_s, n_z, n_x = sizes
-    s, zi, xi = where_am_i()
+    _, zi, xi = where_am_i()
     micro, rows, width = hidden_in.shape
     cols, rank = adapter_in.shape[1:]
     users = included.shape[1]
     dev_rows = micro * rows
-    a = adapter_in[0]
-    g = (a.astype(F32) * norm_gain[0].astype(F32)[:, None]).astype(BF)
-    w = jnp.concatenate([g, adapter_out[0].T], 1)
-    w = jnp.concatenate([w, jnp.broadcast_to(norm_gain, (16, cols))], 0)
     base = (zi * n_x + xi) * users
     local = user_of_row - base
     key = (local + users * jnp.arange(micro, dtype=jnp.int32)[:, None]).reshape(1, dev_rows)
     onehot = local[:, :, None] == jnp.arange(users, dtype=jnp.int32)
     inc = jnp.sum(jnp.where(onehot, included[:, None, :], 0), -1).reshape(1, dev_rows)
     info = jnp.pad(jnp.concatenate([key, inc], 0).astype(BF), ((0, 14), (0, cols - dev_rows)))
-    span = n_x * cols
-
-    def slab(array):
-        flat = lax.dynamic_slice_in_dim(array.reshape(dev_rows, width), s * span, span, 1)
-        return jnp.moveaxis(flat.reshape(dev_rows, n_x, cols), 1, 0)
-
-    act = jnp.concatenate(
-        [slab(hidden_in), slab(cotangent), jnp.broadcast_to(info, (n_x, 16, cols))], 1
+    w_all, h_all, c_all, i_all = exchange(
+        sizes, adapter_in[0], adapter_out[0], norm_gain, hidden_in, cotangent, info
     )
-    w_all, act_all = exchange(sizes, w, act)
-    low, err = solve(sizes, (dev_rows, cols, rank, width), w_all, act_all)
+    h_all = h_all.reshape(n_x, dev_rows, cols)
+    c_all = c_all.reshape(n_x, dev_rows, cols)
+    low, err = solve(sizes, (dev_rows, cols, rank, width), w_all, h_all, c_all)
     bound = 0.8 * math.sqrt(n_s * (rows // users) * width * width)
     gi, go, uw = finish(
-        sizes, (dev_rows, cols, rank, width, micro * users), bound, w_all, act_all, low, err
+        sizes, (dev_rows, cols, rank, width, micro * users), bound, w_all, h_all, c_all, i_all, low, err
     )
     return (gi[None], go[None], uw[:, 0].reshape(micro, users))
 

time: 240 us -> 173 us (0.72)
  the two profiles are of different devices: /device:TPU:89 before, /device:TPU:1 now
where the time goes in v3:
time: 173 us; the launch traced here: 171 us
  Pallas kernels  164 us (95%)
  local copies, waits for them, and re-layouts  4.84 us (3%)
  other arithmetic  2.14 us (1%)
    pallas_call x1, Pallas kernels, solve(): pl.pallas_call(functools.partial(solve_kernel, sizes, dims), out_shape=(j...  79.6 us
    pallas_call x1, Pallas kernels, finish(): pl.pallas_call(functools.partial(finish_kernel, sizes, dims, bound), out_...  54.2 us
    pallas_call x1, Pallas kernels, exchange(): pl.pallas_call(functools.partial(exchange_kernel, sizes), out_shape=(jax....  29.9 us
    unnamed x3, local copies, waits for them, and re-layouts  3.79 us

profile of v3, /device:TPU:1, one launch (start us, length us, event | category | flops | bytes accessed | tf_op | source)
XLA Modules:
  0.0 171.3 jit_solution(15390941277396435801)
XLA Ops:
  0.6 0.8 add_convert_fusion
  1.4 0.1 reshape.27
  1.5 0.8 select_reduce_fusion
  2.3 0.1 reshape.28
  2.3 0.6 fusion.5.info_ref
  3.0 29.9 %exchange.1 = (bf16[8,272,256]{2,1,0:T(8,128)(2,1)}, bf16[4,4,32,256]{3,2,1,0:T(8,128)(2,1)}, bf16[4,4,32,256]{3,2,1,0:T(8,128)(2,1)}, bf16[4,16,256]{2,1,0:T(8,128)(2,1)}) custom-call(bf16[256,128]{1,0:T(8,128)(2,1)} %bitcast.12, bf16[128,256]{1,0:T(8,128)(2,1)} %bitcast.13, bf16[1,256]{1,0:T(2,128)(2,1)} %g_ref.1, bf16[4,32,8192]{2,1,0:T(8,128)(2,1)} %hid_ref.1, ...), custom_call_target="tpu_custom_call" | custom-call | tf_op jit(solution)/shard_map/exchange/pallas_call | solution.py:177
  32.9 79.6 %solve.1 = (bf16[8,512,128]{2,1,0:T(8,128)(2,1)}, bf16[9,512,128]{2,1,0:T(8,128)(2,1)}) custom-call(bf16[8,272,256]{2,1,0:T(8,128)(2,1)} %get-tuple-element.12.w_all, bf16[4,128,256]{2,1,0:T(8,128)(2,1)} %bitcast.6, bf16[4,128,256]{2,1,0:T(8,128)(2,1)} %bitcast.8), custom_call_target="tpu_custom_call" | custom-call | tf_op jit(solution)/shard_map/solve/pallas_call | solution.py:456
  112.5 54.2 %finish.1 = (f32[256,128]{1,0:T(8,128)}, f32[128,256]{1,0:T(8,128)}, f32[8,128]{1,0:T(8,128)}) custom-call(bf16[8,272,256]{2,1,0:T(8,128)(2,1)} %get-tuple-element.12.w_all, bf16[4,128,256]{2,1,0:T(8,128)(2,1)} %bitcast.7, bf16[4,128,256]{2,1,0:T(8,128)(2,1)} %bitcast.9, bf16[4,16,256]{2,1,0:T(8,128)(2,1)} %get-tuple-element.15.i_all, ...), custom_call_target="tpu_custom_call" | custom-call | tf_op jit(solution)/shard_map/finish/pallas_call | solution.py:622
  166.7 0.8 slice_reduce_fusion
  167.4 0.1 reshape_squeeze.3
  167.5 0.7 copy.14
  168.2 1.6 copy.17
  169.7 1.6 copy.18
  (2 shorter events, 0.0 us)

commit v4 on v3

--- a/solution.py
+++ b/solution.py
@@ -76,35 +76,43 @@
                     self.copy(way, step, piece, True).wait_send()
 
 
-def exchange_kernel(
-    sizes, a_ref, b_ref, g_ref, hid_ref, cot_ref, info_ref, w_all, h_all, c_all, i_all,
-    column, rs, rr, ls, lr, ys, yr, asend, arecv, lsem,
+def exchange_phase(
+    sizes, a_ref, b_ref, g_ref, hid_ref, cot_ref, user_ref, inc_ref, w_all, h_all, c_all, i_all, ready,
+    column, info, rs, rr, ls, lr, ys, yr, asend, arecv, lsem,
 ):
     n_s, n_z, n_x = sizes
     s, z, x = where_am_i()
     cols, rank = a_ref.shape
-    barrier = pltpu.get_barrier_semaphore()
-    for k in range(1, n_s):
-        pl.semaphore_signal(
-            barrier, inc=1, device_id=(lax.rem(s + k, n_s), z, x), device_id_type=MESH
-        )
-    for k in (1, n_z - 1):
-        pl.semaphore_signal(
-            barrier, inc=1, device_id=(s, lax.rem(z + k, n_z), x), device_id_type=MESH
-        )
-    for k in range(1, n_x):
-        pl.semaphore_signal(
-            barrier, inc=1, device_id=(s, z, lax.rem(x + k, n_x)), device_id_type=MESH
-        )
+    micro, rows = user_ref.shape
+    users = inc_ref.shape[1]
     gain = jnp.broadcast_to(g_ref[...].astype(F32), (rank, cols))
     column[z, :cols, :rank] = (a_ref[...].astype(F32) * gain.T).astype(BF)
     column[z, :cols, rank:] = b_ref[...].astype(F32).T.astype(BF)
     column[z, cols:, :] = jnp.broadcast_to(g_ref[...].astype(F32), (16, cols)).astype(BF)
-    pl.semaphore_wait(barrier, n_s - 1 + 2 + n_x - 1)
+    local = user_ref[...] - (z * n_x + x) * users
+    included = jnp.zeros((micro, rows), F32)
+    for u in range(users):
+        included = jnp.where(local == u, inc_ref[:, u : u + 1].astype(F32), included)
+    key = (local + users * lax.broadcasted_iota(jnp.int32, (micro, rows), 0)).astype(F32)
+    dev_rows = micro * rows
+    lane = lax.broadcasted_iota(jnp.int32, (rows, dev_rows), 1)
+    row = lax.broadcasted_iota(jnp.int32, (rows, dev_rows), 0)
+    place = sum(jnp.where(lane == row + m * rows, 1.0, 0.0) for m in range(micro)).astype(BF)
+    top = lax.broadcasted_iota(jnp.int32, (micro, dev_rows), 0)
+    along = lax.broadcasted_iota(jnp.int32, (micro, dev_rows), 1)
+    mine = jnp.logical_and(along >= top * rows, along < (top + 1) * rows)
+
+    def flat(v):
+        wide = mm(v.astype(BF), place, 1, 0)
+        return jnp.sum(jnp.where(mine, wide, 0.0), 0, keepdims=True)
+
+    which_row = lax.broadcasted_iota(jnp.int32, (16, dev_rows), 0)
+    info[...] = jnp.where(which_row == 0, flat(key), flat(included)).astype(BF)
+    ready()
 
     def act(which, to, slot):
         at = pl.ds(pl.multiple_of((s * n_x + to) * cols, cols), cols)
-        src = (hid_ref.at[:, :, at], cot_ref.at[:, :, at], info_ref)[which]
+        src = (hid_ref.at[:, :, at], cot_ref.at[:, :, at], info)[which]
         dst = (h_all, c_all, i_all)[which].at[slot]
         return src, dst
 
@@ -113,9 +121,10 @@
         return remote(src, dst, asend.at[which, to], arecv.at[which, slot], (s, z, to))
 
     split = cols // 2
+    half = (slice(0, split), slice(split, cols + 16))
 
     def view(block, piece):
-        return column.at[block, :split] if piece == 0 else column.at[block, split:]
+        return column.at[block, half[piece]]
 
     ring = Ring(n_z, z, lambda to: (s, to, x), view, 2, (rs, rr, ls, lr))
     ring.start()
@@ -126,72 +135,54 @@
         src, dst = act(which, x, x)
         pltpu.make_async_copy(src, dst, lsem.at[which]).start()
 
-    def y_copy(block, slot):
-        return remote(column.at[block], w_all.at[slot], ys.at[block], yr.at[slot], (block, z, x))
-
-    def keep():
-        return pltpu.make_async_copy(column.at[s], w_all.at[s], lsem.at[3])
-
-    def onward(block):
+    def y_copy(block, slot, piece):
+        return remote(
+            column.at[block, half[piece]], w_all.at[slot, half[piece]],
+            ys.at[block, piece], yr.at[slot, piece], (block, z, x),
+        )
+
+    def keep(piece):
+        return pltpu.make_async_copy(
+            column.at[s, half[piece]], w_all.at[s, half[piece]], lsem.at[3 + piece]
+        )
+
+    def onward(block, piece):
         @pl.when(block == s)
         def _():
-            keep().start()
+            keep(piece).start()
 
         @pl.when(block != s)
         def _():
-            y_copy(block, s).start()
-
-    onward(z)
-
-    def arrived(block, piece):
-        if piece == 1:
-            onward(block)
-
-    ring.run(arrived)
+            y_copy(block, s, piece).start()
+
+    for piece in (0, 1):
+        onward(z, piece)
+    ring.run(onward)
     for which in range(3):
         src, dst = act(which, x, x)
         pltpu.make_async_copy(src, dst, lsem.at[which]).wait()
         for k in range(1, n_x):
             a_copy(which, x, lax.rem(x + n_x - k, n_x)).wait_recv()
-    keep().wait()
 
     def not_me(fn):
         def body(k):
-            fn(lax.rem(s + 1 + k, n_s))
+            for piece in (0, 1):
+                fn(lax.rem(s + 1 + k, n_s), piece)
 
         loop(n_s - 1, body)
 
-    not_me(lambda k: y_copy(s, k).wait_recv())
-    not_me(lambda k: y_copy(k, s).wait_send())
-    for which in range(3):
-        for k in range(1, n_x):
-            a_copy(which, lax.rem(x + k, n_x), x).wait_send()
-    ring.finish()
-
-
-def exchange(sizes, a, b, g, hidden, cot, info):
-    n_s, n_z, n_x = sizes
-    cols, rank = a.shape
-    dma = pltpu.SemaphoreType.DMA
-    part = (n_x, *hidden.shape[:2], cols)
-    return pl.pallas_call(
-        functools.partial(exchange_kernel, sizes),
-        out_shape=(
-            jax.ShapeDtypeStruct((n_s, cols + 16, 2 * rank), BF),
-            jax.ShapeDtypeStruct(part, BF),
-            jax.ShapeDtypeStruct(part, BF),
-            jax.ShapeDtypeStruct((n_x, *info.shape), BF),
-        ),
-        in_specs=[VMEM, VMEM, VMEM, ANY, ANY, ANY],
-        out_specs=(ANY,) * 4,
-        scratch_shapes=[
-            pltpu.VMEM((n_z, cols + 16, 2 * rank), BF),
-            dma((n_z, 2)), dma((n_z, 2)), dma((n_z, 2)), dma((n_z, 2)),
-            dma((n_z,)), dma((n_s,)), dma((3, n_x)), dma((3, n_x)), dma((4,)),
-        ],
-        compiler_params=params(0),
-        name="exchange",
-    )(a, b, g, hidden, cot, info)
+    for piece in (0, 1):
+        keep(piece).wait()
+    not_me(lambda k, piece: y_copy(s, k, piece).wait_recv())
+
+    def drain():
+        not_me(lambda k, piece: y_copy(k, s, piece).wait_send())
+        for which in range(3):
+            for k in range(1, n_x):
+                a_copy(which, lax.rem(x + k, n_x), x).wait_send()
+        ring.finish()
+
+    return drain
 
 
 class Plane:
@@ -264,7 +255,7 @@
         p.others(lambda k: self.far(p.ahead(k), p.chip).wait_send())
 
 
-def solve_kernel(
+def solve_phase(
     sizes, dims, w_all, h_all, c_all, low_out, err_out,
     gsend, grecv, gram, pbuf, prev, psum, crev, state, snap, full, rin,
     gs, gr, rs, rr, ls, lr, ns, nr, ps, pr, cs, cr, m0, m1, m2, m3, l0, l1, l2, l3, e0, e1, e2, e3,
@@ -275,17 +266,10 @@
     own = rows // n_s
     part = rank // n_x
     p = Plane(sizes)
-    barrier = pltpu.get_barrier_semaphore()
-    count = p.greet_all(barrier)
-    for k in (1, n_z - 1):
-        pl.semaphore_signal(
-            barrier, inc=1, device_id=(p.s, lax.rem(p.z + k, n_z), p.x), device_id_type=MESH
-        )
     mine = w_all[p.z, :cols, rank:]
     for l in range(layers):
         g = mm(mine, w_all[l, :cols], 0, 0).astype(BF)
         gsend[l] = g.reshape(n_x, part, 2 * rank)
-    pl.semaphore_wait(barrier, count + 2)
     n_plane = 2 * p.chips
     me = p.s * n_x + p.x
 
@@ -298,14 +282,14 @@
     loop(n_plane - 1, lambda k: g_copy(lax.rem(me + 1 + k, n_plane), me).start())
     for l in range(layers):
         for i in range(n_x):
-            zy = mm(h_all[i], w_all[l, :cols], 1, 0).astype(BF)
-            ct = mm(c_all[i], w_all[l, :cols, rank:], 1, 0).astype(BF)
+            zy = mm(h_all[i].reshape(rows, cols), w_all[l, :cols], 1, 0).astype(BF)
+            ct = mm(c_all[i].reshape(rows, cols), w_all[l, :cols, rank:], 1, 0).astype(BF)
             at = slice(i * n_s, (i + 1) * n_s)
             for c, value in enumerate((zy[:, :rank], zy[:, rank:], ct)):
                 r0 = (c * layers + l) * own
                 pbuf[at, r0 : r0 + own, :] = value.reshape(n_s, own, rank)
     for i in range(n_x):
-        xf = h_all[i].astype(F32)
+        xf = h_all[i].reshape(rows, cols).astype(F32)
         sq = jnp.broadcast_to(jnp.sum(xf * xf, -1, keepdims=True), (rows, rank)).astype(BF)
         pbuf[i * n_s : (i + 1) * n_s, 3 * layers * own :, :] = sq.reshape(n_s, own, rank)
 
@@ -434,77 +418,34 @@
     errs.relay()
     lows.finish()
     errs.finish()
-    loop(n_plane - 1, lambda k: g_copy(lax.rem(me + 1 + k, n_plane), me).wait_send())
-    ring.finish()
-    each_share(lambda layer, piece: share(layer, piece, p.core).wait_send())
-    loop(p.chips, lambda k: pre(p.ahead(k)).wait_send())
-    p.others(lambda k: c_copy(p.ahead(k), p.chip).wait_send())
-
-
-def solve(sizes, dims, w_all, h_all, c_all):
+
+    def drain():
+        loop(n_plane - 1, lambda k: g_copy(lax.rem(me + 1 + k, n_plane), me).wait_send())
+        ring.finish()
+        each_share(lambda layer, piece: share(layer, piece, p.core).wait_send())
+        loop(p.chips, lambda k: pre(p.ahead(k)).wait_send())
+        p.others(lambda k: c_copy(p.ahead(k), p.chip).wait_send())
+
+    return drain
+
+
+def finish_phase(
+    sizes, dims, bound, w_all, h_all, c_all, i_all, low_ref, err_ref, grad_out, row_out,
+    normed, deltas, hold, tot, gbuf, mid, acc, rbuf, lbuf, ts, tr, gs, gr, zs, zr, us, ur, lsem,
+):
     n_s, n_z, n_x = sizes
     rows, cols, rank, width = dims
     layers = n_s
-    chips = (n_s // 2) * n_x
-    plane = n_s * n_x
-    own = rows // n_s
-    group = rows * n_x
-    part = rank // n_x
-    high = (3 * layers + 1) * own
-    dma = pltpu.SemaphoreType.DMA
-    v = pltpu.VMEM
-    return pl.pallas_call(
-        functools.partial(solve_kernel, sizes, dims),
-        out_shape=(
-            jax.ShapeDtypeStruct((layers, group, rank), BF),
-            jax.ShapeDtypeStruct((layers + 1, group, rank), BF),
-        ),
-        in_specs=[VMEM, VMEM, VMEM],
-        out_specs=(VMEM, VMEM),
-        scratch_shapes=[
-            v((n_s, n_x, part, 2 * rank), BF),
-            v((plane, part, 2 * rank), BF),
-            v((n_z, n_s, n_x, part, 2 * rank), BF),
-            v((plane, high, rank), BF),
-            v((chips, high, rank), BF),
-            v((chips, high, rank), BF),
-            v((chips, high, rank), BF),
-            v((3 * layers + 1, own, rank), F32),
-            v((layers, layers, own, rank), F32),
-            v((layers, own, rank), F32),
-            v((layers, own, rank), F32),
-            dma((plane,)), dma((plane,)),
-        ]
-        + [dma((n_z, layers // 2))] * 6
-        + [dma((chips,))] * 16,
-        compiler_params=params(1),
-        name="solve",
-    )(w_all, h_all, c_all)
-
-
-def finish_kernel(
-    sizes, dims, bound, w_all, h_all, c_all, i_all, low_ref, err_ref, gi_out, go_out, uw_out,
-    normed, deltas, hold, tot, gbuf, mid, grecv, ts, tr, gs, gr, zs, zr, lsem,
-):
-    n_s, n_z, n_x = sizes
-    rows, cols, rank, width, users = dims
-    layers = n_s
     p = Plane(sizes)
     s, z, x = p.s, p.z, p.x
-    barrier = pltpu.get_barrier_semaphore()
-    count = p.greet_all(barrier)
-    for k in range(1, n_z):
-        pl.semaphore_signal(barrier, inc=1, device_id=(s, lax.rem(z + k, n_z), x), device_id_type=MESH)
-    count = count + n_z - 1
-
     sums = []
     for i in range(n_x):
         at = slice(i * rows, (i + 1) * rows)
-        keyrow = i_all[i].astype(F32)[0:1, :rows]
+        keyrow = i_all[i].astype(F32)[0:1, :]
         keys = jnp.broadcast_to(keyrow, (rows, rows))
         same = keys == keys.T
         scal = err_ref[layers, at].astype(F32)
-        h = h_all[i].astype(F32)
+        h = h_all[i].reshape(rows, cols).astype(F32)
         pairs = jnp.zeros((rows, rows), F32)
         for l in range(layers):
             gain = w_all[l, cols : cols + 8].astype(F32)[0:1, :]
@@ -516,7 +457,7 @@
             pairs = pairs + mm(n, n, 1, 1) * mm(e, e, 1, 1)
             if l + 1 < layers:
                 h = h + mm(low_ref[l, at], w_all[l, :cols, rank:], 1, 1)
-        d = c_all[i].astype(F32)
+        d = c_all[i].reshape(rows, cols).astype(F32)
         for l in range(layers - 1, -1, -1):
             db = d.astype(BF)
             deltas[l, at] = db
@@ -534,7 +475,6 @@
     n_plane = n_s * n_x
     pad = [jnp.zeros((8 - n_x, rows), F32)] if n_x < 8 else []
     tot[me] = jnp.concatenate(sums + pad, 0)
-    pl.semaphore_wait(barrier, count)
 
     def t_copy(to, slot):
         return remote(
@@ -550,24 +490,22 @@
 
     weights = []
     for i in range(n_x):
-        inc = i_all[i].astype(F32)[1:2, :rows]
+        inc = i_all[i].astype(F32)[1:2, :]
         w = jnp.broadcast_to(inc * clip[i : i + 1], (rows, rows))
         weights.append(w.T[:, :rank])
 
         @pl.when(x == i)
         def _(w=w, i=i):
-            keyrow = i_all[i].astype(F32)[0:1, :rows]
-            which = lax.broadcasted_iota(jnp.int32, (users, rows), 0).astype(F32)
-            mine = jnp.where(which == keyrow, w[:users], 0.0)
-            uw_out[...] = jnp.broadcast_to(jnp.max(mine, -1, keepdims=True), (users, rows))
+            row_out[0:1, :] = w[0:1, :]
+            row_out[1:2, :] = i_all[i].astype(F32)[0:1, :]
 
     weight = jnp.concatenate(weights, 0)
 
     def g_copy(to, slot):
         return remote(gbuf.at[to], mid.at[slot], gs.at[to], gr.at[slot], (to, z, x))
 
-    def z_copy(to, slot):
-        return remote(mid.at[to], grecv.at[slot], zs.at[to], zr.at[slot], (s, to, x))
+    def keep():
+        return pltpu.make_async_copy(gbuf.at[s], mid.at[s], lsem.at[0])
 
     for l in range(layers):
         we = (weight * err_ref[l].astype(F32)).astype(BF)
@@ -579,95 +517,209 @@
         def _(l=l):
             g_copy(l, s).start()
 
-    local = pltpu.make_async_copy(gbuf.at[s], mid.at[s], lsem.at[0])
-    local.start()
-    local.wait()
-
-    def onward(k):
-        @pl.when(k == z)
+        @pl.when(s == l)
         def _():
-            pltpu.make_async_copy(mid.at[z], grecv.at[z], lsem.at[1]).start()
-
-        @pl.when(k != z)
+            keep().start()
+
+    def have(slot):
+        @pl.when(slot == s)
         def _():
-            z_copy(k, z).start()
-
-    onward(s)
-
-    def relay(k):
-        at = lax.rem(s + 1 + k, n_s)
-        g_copy(s, at).wait_recv()
-        onward(at)
-
-    loop(n_s - 1, relay)
-    pltpu.make_async_copy(mid.at[z], grecv.at[z], lsem.at[1]).wait()
-    loop(n_z - 1, lambda k: z_copy(z, lax.rem(z + 1 + k, n_z)).wait_recv())
-    grad = grecv[0].astype(F32)
-    for k in range(1, n_z):
-        grad = grad + grecv[k].astype(F32)
+            keep().wait()
+
+        @pl.when(slot != s)
+        def _():
+            g_copy(s, slot).wait_recv()
+
+    right = n_z // 2
+    left = n_z - 1 - right
+    halves = (slice(0, cols // 2), slice(cols // 2, cols))
+
+    def hop(way, step, piece, src):
+        last = step + 1 == (right, left)[way]
+        part = halves[piece]
+        dst = grad_out.at[1 + way, part] if last else (rbuf, lbuf)[way].at[step, part]
+        send, recv = ((zs, zr), (us, ur))[way]
+        to = lax.rem(z + (1, n_z - 1)[way], n_z)
+        return remote(src, dst, send.at[step, piece], recv.at[step, piece], (s, to, x))
+
+    def source(way, step, piece, slot):
+        part = halves[piece]
+        return mid.at[slot, part] if step == 0 else acc.at[way, step - 1, part]
+
+    def slot_of(way, step):
+        gap = (right - step) if way == 0 else (n_z - left + step)
+        return lax.rem(z + gap, n_z)
+
+    for step in range(right):
+        for way in (0, 1):
+            if step < (right, left)[way]:
+                have(slot_of(way, step))
+        for piece in (0, 1):
+            for way in (0, 1):
+                if step >= (right, left)[way]:
+                    continue
+                slot = slot_of(way, step)
+                part = halves[piece]
+                src = source(way, step, piece, slot)
+                if step > 0:
+                    hop(way, step - 1, piece, source(way, step - 1, piece, slot)).wait_recv()
+                    came = (rbuf, lbuf)[way][step - 1, part].astype(F32)
+                    acc[way, step - 1, part] = (came + mid[slot, part].astype(F32)).astype(BF)
+                hop(way, step, piece, src).start()
+    have(z)
+    grad_out[0] = mid[z]
+    for way in (0, 1):
+        step = (right, left)[way] - 1
+        for piece in (0, 1):
+            hop(way, step, piece, source(way, step, piece, z)).wait_recv()
+
+    def drain():
+        for way in (0, 1):
+            for step in range((right, left)[way]):
+                for piece in (0, 1):
+                    hop(way, step, piece, source(way, step, piece, z)).wait_send()
+        loop(n_s - 1, lambda k: g_copy(lax.rem(s + 1 + k, n_s), s).wait_send())
+        loop(n_plane - 1, lambda k: t_copy(lax.rem(me + 1 + k, n_plane), me).wait_send())
+
+    return drain
+
+
+def main_kernel(
+    sizes, dims, bound, n_ex, n_so, a_ref, b_ref, g_ref, hid_ref, cot_ref, user_ref, inc_ref,
+    grad_out, row_out, w_all, h_all, c_all, i_all, low, err, *scratch,
+):
+    n_s, n_z, n_x = sizes
+    p = Plane(sizes)
+    barrier = pltpu.get_barrier_semaphore()
+    count = p.greet_all(barrier)
+    for k in (1, n_z - 1):
+        pl.semaphore_signal(
+            barrier, inc=1, device_id=(p.s, lax.rem(p.z + k, n_z), p.x), device_id_type=MESH
+        )
+    first = exchange_phase(
+        sizes, a_ref, b_ref, g_ref, hid_ref, cot_ref, user_ref, inc_ref, w_all, h_all, c_all, i_all,
+        lambda: pl.semaphore_wait(barrier, count + 2), *scratch[:n_ex],
+    )
+    second = solve_phase(sizes, dims, w_all, h_all, c_all, low, err, *scratch[n_ex : n_ex + n_so])
+    third = finish_phase(
+        sizes, dims, bound, w_all, h_all, c_all, i_all, low, err, grad_out, row_out,
+        *scratch[n_ex + n_so :],
+    )
+    first()
+    second()
+    third()
+
+
+def main(sizes, dims, bound, a, b, g, hidden, cot, users, inc):
+    n_s, n_z, n_x = sizes
+    rows, cols, rank, width = dims
+    layers = n_s
+    chips = (n_s // 2) * n_x
+    plane = n_s * n_x
+    own = rows // n_s
+    group = rows * n_x
+    part = rank // n_x
+    high = (3 * layers + 1) * own
+    dma = pltpu.SemaphoreType.DMA
+    v = pltpu.VMEM
+    slab = (n_x, *hidden.shape[:2], cols)
+    shared = [
+        v((n_s, cols + 16, 2 * rank), BF),
+        v(slab, BF),
+        v(slab, BF),
+        v((n_x, 16, rows), BF),
+        v((layers, group, rank), BF),
+        v((layers + 1, group, rank), BF),
+    ]
+    ex = [
+        v((n_z, cols + 16, 2 * rank), BF),
+        v((16, rows), BF),
+        dma((n_z, 2)), dma((n_z, 2)), dma((n_z, 2)), dma((n_z, 2)),
+        dma((n_z, 2)), dma((n_s, 2)), dma((3, n_x)), dma((3, n_x)), dma((5,)),
+    ]
+    so = [
+        v((n_s, n_x, part, 2 * rank), BF),
+        v((plane, part, 2 * rank), BF),
+        v((n_z, n_s, n_x, part, 2 * rank), BF),
+        v((plane, high, rank), BF),
+        v((chips, high, rank), BF),
+        v((chips, high, rank), BF),
+        v((chips, high, rank), BF),
+        v((3 * layers + 1, own, rank), F32),
+        v((layers, layers, own, rank), F32),
+        v((layers, own, rank), F32),
+        v((layers, own, rank), F32),
+        dma((plane,)), dma((plane,)),
+    ]
+    so += [dma((n_z, layers // 2))] * 6 + [dma((chips,))] * 16
+    fi = [
+        v((layers, group, cols), BF),
+        v((layers, group, cols), BF),
+        v((layers, rows, cols), BF),
+        v((plane, 8, rows), F32),
+        v((layers, cols, 2 * rank), BF),
+        v((n_s, cols, 2 * rank), BF),
+        v((2, n_z // 2, cols, 2 * rank), BF),
+        v((n_z // 2, cols, 2 * rank), BF),
+        v((n_z // 2, cols, 2 * rank), BF),
+        dma((plane,)), dma((plane,)), dma((n_s,)), dma((n_s,)),
+    ]
+    fi += [dma((n_z // 2, 2))] * 4 + [dma((1,))]
+    return pl.pallas_call(
+        functools.partial(main_kernel, sizes, dims, bound, len(ex), len(so)),
+        out_shape=(
+            jax.ShapeDtypeStruct((3, cols, 2 * rank), BF),
+            jax.ShapeDtypeStruct((8, rows), F32),
+        ),
+        in_specs=[VMEM, VMEM, VMEM, ANY, ANY, VMEM, VMEM],
+        out_specs=(VMEM, VMEM),
+        scratch_shapes=shared + ex + so + fi,
+        compiler_params=params(0),
+        name="main",
+    )(a, b, g, hidden, cot, users, inc)
+
+
+def close_kernel(parts, row, gi_out, go_out, uw_out):
+    rank = gi_out.shape[1]
+    grad = parts[0].astype(F32) + parts[1].astype(F32) + parts[2].astype(F32)
     gi_out[...] = grad[:, :rank]
     go_out[...] = grad[:, rank:].T
-    loop(n_s - 1, lambda k: g_copy(lax.rem(s + 1 + k, n_s), s).wait_send())
-    loop(n_z - 1, lambda k: z_copy(lax.rem(z + 1 + k, n_z), z).wait_send())
-    loop(n_plane - 1, lambda k: t_copy(lax.rem(me + 1 + k, n_plane), me).wait_send())
-
-
-def finish(sizes, dims, bound, *arrays):
-    n_s, n_z, n_x = sizes
-    rows, cols, rank, width, users = dims
-    layers = n_s
-    plane = n_s * n_x
-    dma = pltpu.SemaphoreType.DMA
-    v = pltpu.VMEM
-    return pl.pallas_call(
-        functools.partial(finish_kernel, sizes, dims, bound),
+    micro, users = uw_out.shape
+    width = row.shape[1]
+    weight = jnp.broadcast_to(row[0:1, :], (micro, width))
+    key = jnp.broadcast_to(row[1:2, :], (micro, width))
+    first = (lax.broadcasted_iota(jnp.int32, (micro, width), 0) * users).astype(F32)
+    lane = lax.broadcasted_iota(jnp.int32, (micro, users), 1)
+    result = jnp.zeros((micro, users), F32)
+    for u in range(users):
+        most = jnp.max(jnp.where(key == first + u, weight, 0.0), -1, keepdims=True)
+        result = jnp.where(lane == u, most, result)
+    uw_out[...] = result
+
+
+def shards(hidden_in, cotangent, adapter_in, adapter_out, norm_gain, user_of_row, included):
+    sizes = tuple(lax.axis_size(a) for a in ("section", "z", "x"))
+    n_s = sizes[0]
+    micro, rows, width = hidden_in.shape
+    cols, rank = adapter_in.shape[1:]
+    users = included.shape[1]
+    bound = 0.8 * math.sqrt(n_s * (rows // users) * width * width)
+    parts, row = main(
+        sizes, (micro * rows, cols, rank, width), bound, adapter_in[0], adapter_out[0], norm_gain,
+        hidden_in, cotangent, user_of_row, included,
+    )
+    gi, go, uw = pl.pallas_call(
+        close_kernel,
         out_shape=(
             jax.ShapeDtypeStruct((cols, rank), F32),
             jax.ShapeDtypeStruct((rank, cols), F32),
-            jax.ShapeDtypeStruct((users, rows), F32),
+            jax.ShapeDtypeStruct((micro, users), F32),
         ),
-        in_specs=[VMEM] * 6,
+        in_specs=[VMEM, VMEM],
         out_specs=(VMEM,) * 3,
-        scratch_shapes=[
-            v((layers, rows * n_x, cols), BF),
-            v((layers, rows * n_x, cols), BF),
-            v((layers, rows, cols), BF),
-            v((plane, 8, rows), F32),
-            v((layers, cols, 2 * rank), BF),
-            v((n_s, cols, 2 * rank), BF),
-            v((n_z, cols, 2 * rank), BF),
-            dma((plane,)), dma((plane,)), dma((n_s,)), dma((n_s,)), dma((n_z,)), dma((n_z,)), dma((2,)),
-        ],
-        compiler_params=params(2),
-        name="finish",
-    )(*arrays)
-
-
-def shards(hidden_in, cotangent, adapter_in, adapter_out, norm_gain, user_of_row, included):
-    sizes = tuple(lax.axis_size(a) for a in ("section", "z", "x"))
-    n_s, n_z, n_x = sizes
-    _, zi, xi = where_am_i()
-    micro, rows, width = hidden_in.shape
-    cols, rank = adapter_in.shape[1:]
-    users = included.shape[1]
-    dev_rows = micro * rows
-    base = (zi * n_x + xi) * users
-    local = user_of_row - base
-    key = (local + users * jnp.arange(micro, dtype=jnp.int32)[:, None]).reshape(1, dev_rows)
-    onehot = local[:, :, None] == jnp.arange(users, dtype=jnp.int32)
-    inc = jnp.sum(jnp.where(onehot, included[:, None, :], 0), -1).reshape(1, dev_rows)
-    info = jnp.pad(jnp.concatenate([key, inc], 0).astype(BF), ((0, 14), (0, cols - dev_rows)))
-    w_all, h_all, c_all, i_all = exchange(
-        sizes, adapter_in[0], adapter_out[0], norm_gain, hidden_in, cotangent, info
-    )
-    h_all = h_all.reshape(n_x, dev_rows, cols)
-    c_all = c_all.reshape(n_x, dev_rows, cols)
-    low, err = solve(sizes, (dev_rows, cols, rank, width), w_all, h_all, c_all)
-    bound = 0.8 * math.sqrt(n_s * (rows // users) * width * width)
-    gi, go, uw = finish(
-        sizes, (dev_rows, cols, rank, width, micro * users), bound, w_all, h_all, c_all, i_all, low, err
-    )
-    return (gi[None], go[None], uw[:, 0].reshape(micro, users))
+        name="close",
+    )(parts, row)
+    return (gi[None], go[None], uw)
 
 
 def build(torus):

time: 173 us -> 158 us (0.913)
  Pallas kernels: 164 us -> 153 us
  local copies, waits for them, and re-layouts: 4.84 us -> 2.64 us
  other arithmetic: 2.14 us -> 0 us
    pallas_call x3 -> x2, Pallas kernels: 164 us -> 153 us  [the longest x1 151 us: main(): pl.pallas_call(functools.partial(main_kernel, sizes, dims, bound, len(ex)...]
    unnamed x3 -> x2, local copies, waits for them, and re-layouts: 3.79 us -> 2.64 us
where the time goes in v4:
time: 158 us; the launch traced here: 156 us
  Pallas kernels  153 us (97%)
  local copies, waits for them, and re-layouts  2.64 us (2%)
    pallas_call x1, Pallas kernels, main(): pl.pallas_call(functools.partial(main_kernel, sizes, dims, bound, len(ex)...  151 us

profile of v4, /device:TPU:1, one launch (start us, length us, event | category | flops | bytes accessed | tf_op | source)
XLA Modules:
  0.0 155.8 jit_solution(13618803914227926794)
XLA Ops:
  0.6 1.3 copy.10.inc_ref
  2.0 150.8 %main.1 = (bf16[3,256,256]{2,1,0:T(8,128)(2,1)}, f32[8,128]{1,0:T(8,128)}) custom-call(bf16[256,128]{1,0:T(8,128)(2,1)} %bitcast.4, bf16[128,256]{1,0:T(8,128)(2,1)} %bitcast.5, bf16[1,256]{1,0:T(2,128)(2,1)} %g_ref.1, bf16[4,32,8192]{2,1,0:T(8,128)(2,1)} %hid_ref.1, bf16[4,32,8192]{2,1,0:T(8,128)(2,1)} %cot_ref.1, s32[4,32]{1,0:T(4,128)} %user_ref.1, ...), custom_call_target="tpu_custom_call" | custom-call | tf_op jit(solution)/shard_map/main/pallas_call | solution.py:668
  152.7 1.8 %close.1 = (f32[256,128]{1,0:T(8,128)}, f32[128,256]{1,0:T(8,128)}, f32[4,2]{1,0:T(4,128)}) custom-call(bf16[3,256,256]{2,1,0:T(8,128)(2,1)} %get-tuple-element.8.parts, f32[8,128]{1,0:T(8,128)} %get-tuple-element.9.row), custom_call_target="tpu_custom_call" | custom-call | tf_op jit(solution)/shard_map/close/pallas_call | solution.py:711
  154.5 1.3 copy.11

commit v5 on v4

--- a/solution.py
+++ b/solution.py
@@ -40,40 +40,83 @@
 
 
 class Ring:
-    def __init__(self, n, me, place, view, pieces, sems):
+    def __init__(self, n, me, place, view, pieces, sems, want=None):
         self.n, self.me, self.place, self.view, self.pieces, self.sems = n, me, place, view, pieces, sems
-        self.steps = (n // 2, n - 1 - n // 2)
-
-    def copy(self, way, step, piece, from_me):
-        n, me = self.n, self.me
+        self.want = want
+        self.far = n // 2
+
+    def block(self, way, step):
         sign = 1 - 2 * way
-        block = (me - sign * step) if from_me else (me - sign * (step + 1))
-        ref = self.view(lax.rem(block + 2 * n, n), piece)
+        return lax.rem(self.me - sign * step + 2 * self.n, self.n)
+
+    def copy(self, way, step, piece, block):
+        sign = 1 - 2 * way
+        ref = self.view(block, piece)
         send, recv = self.sems[2 * way].at[step, piece], self.sems[2 * way + 1].at[step, piece]
-        return remote(ref, ref, send, recv, self.place(lax.rem(me + sign + n, n)))
+        return remote(ref, ref, send, recv, self.place(lax.rem(self.me + sign + self.n, self.n)))
+
+    def guard(self, block, piece, fn):
+        if self.want is None:
+            fn()
+        else:
+            pl.when(self.want(block, piece))(fn)
+
+    def each(self, step, fn):
+        half = self.pieces // 2
+
+        def body(i):
+            if step + 1 < self.far:
+                for way in (0, 1):
+                    fn(way, i)
+            else:
+                fn(0, i)
+                fn(1, i + half)
+
+        count = self.pieces if step + 1 < self.far else half
+        if self.want is None:
+            for i in range(count):
+                body(i)
+        else:
+            loop(count, body)
+
+    def send(self, way, step, piece):
+        block = self.block(way, step)
+        self.guard(block, piece, lambda: self.copy(way, step, piece, block).start())
 
     def start(self):
-        for piece in range(self.pieces):
-            for way in (0, 1):
-                self.copy(way, 0, piece, True).start()
+        self.each(0, lambda way, piece: self.send(way, 0, piece))
 
     def run(self, arrived):
-        for step in range(self.steps[0]):
-            for piece in range(self.pieces):
-                for way in (0, 1):
-                    if step < self.steps[way]:
-                        self.copy(way, step, piece, False).wait_recv()
-                        if step + 1 < self.steps[way]:
-                            self.copy(way, step + 1, piece, True).start()
-                        sign = 1 - 2 * way
-                        block = lax.rem(self.me - sign * (step + 1) + 2 * self.n, self.n)
-                        arrived(block, piece)
+        half = self.pieces // 2
+
+        def one(step, way, piece):
+            block = self.block(way, step + 1)
+
+            def take():
+                self.copy(way, step, piece, block).wait_recv()
+                if step + 2 < self.far:
+                    self.copy(way, step + 1, piece, block).start()
+                elif step + 2 == self.far:
+                    onward = piece < half if way == 0 else piece >= half
+                    if isinstance(onward, bool):
+                        if onward:
+                            self.copy(way, step + 1, piece, block).start()
+                    else:
+                        pl.when(onward)(lambda: self.copy(way, step + 1, piece, block).start())
+                arrived(block, piece)
+
+            self.guard(block, piece, take)
+
+        for step in range(self.far):
+            self.each(step, lambda way, piece: one(step, way, piece))
 
     def finish(self):
-        for way in (0, 1):
-            for step in range(self.steps[way]):
-                for piece in range(self.pieces):
-                    self.copy(way, step, piece, True).wait_send()
+        def one(step, way, piece):
+            block = self.block(way, step)
+            self.guard(block, piece, lambda: self.copy(way, step, piece, block).wait_send())
+
+        for step in range(self.far):
+            self.each(step, lambda way, piece: one(step, way, piece))
 
 
 def exchange_phase(
@@ -84,16 +127,19 @@
     s, z, x = where_am_i()
     cols, rank = a_ref.shape
     micro, rows = user_ref.shape
-    users = inc_ref.shape[1]
+    users = inc_ref.shape[0]
     gain = jnp.broadcast_to(g_ref[...].astype(F32), (rank, cols))
     column[z, :cols, :rank] = (a_ref[...].astype(F32) * gain.T).astype(BF)
     column[z, :cols, rank:] = b_ref[...].astype(F32).T.astype(BF)
     column[z, cols:, :] = jnp.broadcast_to(g_ref[...].astype(F32), (16, cols)).astype(BF)
     local = user_ref[...] - (z * n_x + x) * users
     included = jnp.zeros((micro, rows), F32)
+    level = lax.broadcasted_iota(jnp.int32, (micro, rows), 0)
     for u in range(users):
-        included = jnp.where(local == u, inc_ref[:, u : u + 1].astype(F32), included)
-    key = (local + users * lax.broadcasted_iota(jnp.int32, (micro, rows), 0)).astype(F32)
+        for m in range(micro):
+            here = jnp.logical_and(local == u, level == m)
+            included = jnp.where(here, inc_ref[u : u + 1, m : m + 1].astype(F32), included)
+    key = (local + users * level).astype(F32)
     dev_rows = micro * rows
     lane = lax.broadcasted_iota(jnp.int32, (rows, dev_rows), 1)
     row = lax.broadcasted_iota(jnp.int32, (rows, dev_rows), 0)
@@ -307,43 +353,55 @@
 
     loop(p.chips, lambda k: pre(p.ahead(k)).start())
 
+    early = (p.chips - 1) // 4
+
+    def pair(k):
+        i = p.ahead(k)
+        pre_wait(i).wait_recv()
+        total = pbuf[block(i, p.core)].astype(F32) + prev[i].astype(F32)
+        psum[i] = total.astype(BF)
+
+        @pl.when(jnp.logical_and(k >= 1, k <= early))
+        def _():
+            c_copy(i, p.chip).start()
+
+    loop(p.chips, lambda k: pair(lax.rem(k + 1, p.chips)))
+
     loop(n_plane - 1, lambda k: g_copy(me, lax.rem(me + n_plane - 1 - k, n_plane)).wait_recv())
     grecv[me] = gsend[p.s, p.x]
     gsum = grecv[0].astype(F32)
     for k in range(1, n_plane):
         gsum = gsum + grecv[k].astype(F32)
-    gram[p.z, p.s, p.x] = gsum.astype(BF)
+    gram[0, p.z, p.s, p.x] = gsum[:, :rank].astype(BF)
+    gram[1, p.z, p.s, p.x] = gsum[:, rank:].astype(BF)
 
     def gram_view(chip, core):
-        return gram.at[p.z, 2 * (chip // n_x) + core, lax.rem(chip, n_x)]
+        return gram.at[:, p.z, 2 * (chip // n_x) + core, lax.rem(chip, n_x)]
 
     spread = Cast(p, gram_view, (m0, m1, m2, m3))
     spread.start()
     spread.relay()
     spread.finish()
 
-    half = layers // 2
-
-    def ring_view(block, piece):
-        return gram.at[block, half * p.core + piece]
-
-    ring = Ring(n_z, p.z, lambda to: (p.s, to, p.x), ring_view, half, (rs, rr, ls, lr))
+    def gram_part(layer, piece, core):
+        return gram.at[lax.rem(piece, 2), layer, 2 * (piece // 2) + core]
+
+    def wanted(layer, piece, core):
+        other = 2 * (piece // 2) + core
+        upper = layer < other
+        last = jnp.where(lax.rem(piece, 2) == 0, layer > other, layer == other)
+        return jnp.logical_or(upper, last)
+
+    ring = Ring(
+        n_z, p.z, lambda to: (p.s, to, p.x), lambda layer, piece: gram_part(layer, piece, p.core),
+        layers, (rs, rr, ls, lr), lambda layer, piece: wanted(layer, piece, p.core),
+    )
     ring.start()
 
-    def forward(k):
-        i = p.ahead(k)
-        pre_wait(i).wait_recv()
-        total = pbuf[block(i, p.core)].astype(F32) + prev[i].astype(F32)
-        psum[i] = total.astype(BF)
-
-        @pl.when(i != p.chip)
-        def _():
-            c_copy(i, p.chip).start()
-
-    loop(p.chips, lambda k: forward(lax.rem(k + 1, p.chips)))
+    loop(p.chips - 1 - early, lambda k: c_copy(p.ahead(k + 1 + early), p.chip).start())
 
     def share(layer, piece, core):
-        ref = gram.at[layer, half * core + piece]
+        ref = gram_part(layer, piece, core)
         return remote(ref, ref, ns.at[layer, piece], nr.at[layer, piece], p.partner)
 
     ring.run(lambda layer, piece: share(layer, piece, p.core).start())
@@ -354,15 +412,15 @@
         total = total + crev[k].astype(F32)
     state[...] = total.reshape(3 * layers + 1, own, rank)
 
-    def each_share(fn):
+    def each_share(core, fn):
         def body(k):
-            layer = lax.rem(p.z + 1 + k, n_z)
-            for piece in range(half):
-                fn(layer, piece)
-
-        loop(n_z - 1, body)
-
-    each_share(lambda layer, piece: share(layer, piece, 1 - p.core).wait_recv())
+            layer = lax.rem(p.z + 1 + k // layers, n_z)
+            piece = lax.rem(k, layers)
+            pl.when(wanted(layer, piece, core))(lambda: fn(share(layer, piece, core)))
+
+        loop((n_z - 1) * layers, body)
+
+    each_share(1 - p.core, lambda copy: copy.wait_recv())
 
     def low_view(chip, core):
         dev = block(chip, core)
@@ -388,49 +446,52 @@
         for j in range(layers):
             snap[l, j] = state[layers + j]
             if j > l:
-                both = mm(low, gram[l, j].reshape(rank, 2 * rank), 1, 0)
+                pair_gram = jnp.concatenate(
+                    [gram[0, l, j].reshape(rank, rank), gram[1, l, j].reshape(rank, rank)], 1
+                )
+                both = mm(low, pair_gram, 1, 0)
                 state[j] = state[j] + both[:, :rank]
                 state[layers + j] = state[layers + j] + both[:, rank:]
             else:
-                one = mm(low, gram[l, j, :, :, rank:].reshape(rank, rank), 1, 0)
+                one = mm(low, gram[1, j, l].reshape(rank, rank), 1, 1)
                 state[layers + j] = state[layers + j] + one
         after = state[layers + l]
         square = square + jnp.sum(low.astype(F32) * (before + after), -1, keepdims=True)
         high = rinv.astype(BF).astype(F32)
         scal = jnp.where(lane == l, high, scal)
         scal = jnp.where(lane == layers + l, rinv - high, scal)
+    low_out[layers, here, :] = scal.astype(BF)
     lows = Cast(p, low_view, (l0, l1, l2, l3))
     lows.start()
+    scal = zero
     for l in range(layers - 1, -1, -1):
         err = state[2 * layers + l].astype(BF)
         mean = jnp.sum(err.astype(F32) * full[l], -1, keepdims=True) / width
         rinv = rin[l]
         cor = rinv * rinv * mean
         for j in range(l):
-            back = mm(err, gram[j, l, :, :, :rank].reshape(rank, rank), 1, 1)
+            back = mm(err, gram[0, j, l].reshape(rank, rank), 1, 1)
             state[2 * layers + j] = state[2 * layers + j] + rinv * back - cor * snap[l, j]
         err_out[l, here, :] = err
-        scal = jnp.where(lane == 2 * layers + l, cor, scal)
+        scal = jnp.where(lane == l, cor, scal)
     err_out[layers, here, :] = scal.astype(BF)
     errs = Cast(p, err_view, (e0, e1, e2, e3))
     errs.start()
     lows.relay()
-    errs.relay()
     lows.finish()
-    errs.finish()
 
     def drain():
         loop(n_plane - 1, lambda k: g_copy(lax.rem(me + 1 + k, n_plane), me).wait_send())
         ring.finish()
-        each_share(lambda layer, piece: share(layer, piece, p.core).wait_send())
+        each_share(p.core, lambda copy: copy.wait_send())
         loop(p.chips, lambda k: pre(p.ahead(k)).wait_send())
         p.others(lambda k: c_copy(p.ahead(k), p.chip).wait_send())
 
-    return drain
+    return drain, errs
 
 
 def finish_phase(
-    sizes, dims, bound, w_all, h_all, c_all, i_all, low_ref, err_ref, grad_out, row_out,
+    sizes, dims, bound, w_all, h_all, c_all, i_all, low_ref, err_ref, errs, grad_out, row_out,
     normed, deltas, hold, tot, gbuf, mid, acc, rbuf, lbuf, ts, tr, gs, gr, zs, zr, us, ur, lsem,
 ):
     n_s, n_z, n_x = sizes
@@ -438,36 +499,40 @@
     layers = n_s
     p = Plane(sizes)
     s, z, x = p.s, p.z, p.x
+    def factor(ref, i, l):
+        return ref[layers, i * rows : (i + 1) * rows, l : l + 1].astype(F32)
+
+    def rinv_of(i, l):
+        return factor(low_ref, i, l) + factor(low_ref, i, layers + l)
+
+    for i in range(n_x):
+        at = slice(i * rows, (i + 1) * rows)
+        h = h_all[i].reshape(rows, cols).astype(F32)
+        for l in range(layers):
+            gain = w_all[l, cols : cols + 8].astype(F32)[0:1, :]
+            normed[l, at] = (h * rinv_of(i, l) * gain).astype(BF)
+            hold[l, at] = h.astype(BF)
+            if l + 1 < layers:
+                h = h + mm(low_ref[l, at], w_all[l, :cols, rank:], 1, 1)
+    errs.relay()
+    errs.finish()
     sums = []
     for i in range(n_x):
         at = slice(i * rows, (i + 1) * rows)
         keyrow = i_all[i].astype(F32)[0:1, :]
         keys = jnp.broadcast_to(keyrow, (rows, rows))
         same = keys == keys.T
-        scal = err_ref[layers, at].astype(F32)
-        h = h_all[i].reshape(rows, cols).astype(F32)
         pairs = jnp.zeros((rows, rows), F32)
-        for l in range(layers):
-            gain = w_all[l, cols : cols + 8].astype(F32)[0:1, :]
-            rinv = scal[:, l : l + 1] + scal[:, layers + l : layers + l + 1]
-            n = (h * rinv * gain).astype(BF)
-            e = err_ref[l, at]
-            normed[l, at] = n
-            hold[l] = h.astype(BF)
-            pairs = pairs + mm(n, n, 1, 1) * mm(e, e, 1, 1)
-            if l + 1 < layers:
-                h = h + mm(low_ref[l, at], w_all[l, :cols, rank:], 1, 1)
         d = c_all[i].reshape(rows, cols).astype(F32)
         for l in range(layers - 1, -1, -1):
             db = d.astype(BF)
             deltas[l, at] = db
-            lo = low_ref[l, at]
+            lo, n, e = low_ref[l, at], normed[l, at], err_ref[l, at]
             pairs = pairs + mm(lo, lo, 1, 1) * mm(db, db, 1, 1)
+            pairs = pairs + mm(n, n, 1, 1) * mm(e, e, 1, 1)
             if l > 0:
-                rinv = scal[:, l : l + 1] + scal[:, layers + l : layers + l + 1]
-                cor = scal[:, 2 * layers + l : 2 * layers + l + 1]
-                d = d + rinv * mm(err_ref[l, at], w_all[l, :cols, :rank], 1, 1)
-                d = d - cor * hold[l].astype(F32)
+                d = d + rinv_of(i, l) * mm(e, w_all[l, :cols, :rank], 1, 1)
+                d = d - factor(err_ref, i, l) * hold[l, at].astype(F32)
         pairs = jnp.where(same, pairs, 0.0)
         rowsum = jnp.broadcast_to(jnp.sum(pairs, -1, keepdims=True), (rows, rows))
         sums.append(jnp.sum(jnp.where(same, rowsum, 0.0), 0, keepdims=True))
@@ -507,19 +572,22 @@
     def keep():
         return pltpu.make_async_copy(gbuf.at[s], mid.at[s], lsem.at[0])
 
-    for l in range(layers):
+    def gradient(k):
+        l = lax.rem(s + 1 + k, n_s)
         we = (weight * err_ref[l].astype(F32)).astype(BF)
         wl = (weight * low_ref[l].astype(F32)).astype(BF)
         gbuf[l, :, :rank] = mm(normed[l], we, 0, 0).astype(BF)
         gbuf[l, :, rank:] = mm(deltas[l], wl, 0, 0).astype(BF)
 
         @pl.when(s != l)
-        def _(l=l):
+        def _():
             g_copy(l, s).start()
 
         @pl.when(s == l)
         def _():
             keep().start()
+
+    loop(layers, gradient)
 
     def have(slot):
         @pl.when(slot == s)
@@ -530,14 +598,18 @@
         def _():
             g_copy(s, slot).wait_recv()
 
-    right = n_z // 2
-    left = n_z - 1 - right
+    far = n_z // 2
     halves = (slice(0, cols // 2), slice(cols // 2, cols))
 
+    def hops(way, piece):
+        return far if way == piece else far - 1
+
     def hop(way, step, piece, src):
-        last = step + 1 == (right, left)[way]
         part = halves[piece]
-        dst = grad_out.at[1 + way, part] if last else (rbuf, lbuf)[way].at[step, part]
+        if step + 1 == hops(way, piece):
+            dst = grad_out.at[1 + way, part]
+        else:
+            dst = (rbuf, lbuf)[way].at[step, part]
         send, recv = ((zs, zr), (us, ur))[way]
         to = lax.rem(z + (1, n_z - 1)[way], n_z)
         return remote(src, dst, send.at[step, piece], recv.at[step, piece], (s, to, x))
@@ -546,19 +618,24 @@
         part = halves[piece]
         return mid.at[slot, part] if step == 0 else acc.at[way, step - 1, part]
 
-    def slot_of(way, step):
-        gap = (right - step) if way == 0 else (n_z - left + step)
-        return lax.rem(z + gap, n_z)
-
-    for step in range(right):
-        for way in (0, 1):
-            if step < (right, left)[way]:
-                have(slot_of(way, step))
+    def slot_of(way, gap):
+        return lax.rem(z + (gap if way == 0 else n_z - gap), n_z)
+
+    seen = set()
+
+    def need(gap):
+        if gap % n_z not in seen:
+            seen.add(gap % n_z)
+            have(lax.rem(z + gap + n_z, n_z))
+
+    for step in range(far):
         for piece in (0, 1):
             for way in (0, 1):
-                if step >= (right, left)[way]:
+                if step >= hops(way, piece):
                     continue
-                slot = slot_of(way, step)
+                gap = hops(way, piece) - step
+                need(gap if way == 0 else -gap)
+                slot = slot_of(way, gap)
                 part = halves[piece]
                 src = source(way, step, piece, slot)
                 if step > 0:
@@ -566,17 +643,17 @@
                     came = (rbuf, lbuf)[way][step - 1, part].astype(F32)
                     acc[way, step - 1, part] = (came + mid[slot, part].astype(F32)).astype(BF)
                 hop(way, step, piece, src).start()
-    have(z)
+    need(0)
     grad_out[0] = mid[z]
     for way in (0, 1):
-        step = (right, left)[way] - 1
         for piece in (0, 1):
+            step = hops(way, piece) - 1
             hop(way, step, piece, source(way, step, piece, z)).wait_recv()
 
     def drain():
         for way in (0, 1):
-            for step in range((right, left)[way]):
-                for piece in (0, 1):
+            for piece in (0, 1):
+                for step in range(hops(way, piece)):
                     hop(way, step, piece, source(way, step, piece, z)).wait_send()
         loop(n_s - 1, lambda k: g_copy(lax.rem(s + 1 + k, n_s), s).wait_send())
         loop(n_plane - 1, lambda k: t_copy(lax.rem(me + 1 + k, n_plane), me).wait_send())
@@ -600,9 +677,9 @@
         sizes, a_ref, b_ref, g_ref, hid_ref, cot_ref, user_ref, inc_ref, w_all, h_all, c_all, i_all,
         lambda: pl.semaphore_wait(barrier, count + 2), *scratch[:n_ex],
     )
-    second = solve_phase(sizes, dims, w_all, h_all, c_all, low, err, *scratch[n_ex : n_ex + n_so])
+    second, errs = solve_phase(sizes, dims, w_all, h_all, c_all, low, err, *scratch[n_ex : n_ex + n_so])
     third = finish_phase(
-        sizes, dims, bound, w_all, h_all, c_all, i_all, low, err, grad_out, row_out,
+        sizes, dims, bound, w_all, h_all, c_all, i_all, low, err, errs, grad_out, row_out,
         *scratch[n_ex + n_so :],
     )
     first()
@@ -628,7 +705,7 @@
         v(slab, BF),
         v(slab, BF),
         v((n_x, 16, rows), BF),
-        v((layers, group, rank), BF),
+        v((layers + 1, group, rank), BF),
         v((layers + 1, group, rank), BF),
     ]
     ex = [
@@ -640,7 +717,7 @@
     so = [
         v((n_s, n_x, part, 2 * rank), BF),
         v((plane, part, 2 * rank), BF),
-        v((n_z, n_s, n_x, part, 2 * rank), BF),
+        v((2, n_z, n_s, n_x, part, rank), BF),
         v((plane, high, rank), BF),
         v((chips, high, rank), BF),
         v((chips, high, rank), BF),
@@ -651,11 +728,11 @@
         v((layers, own, rank), F32),
         dma((plane,)), dma((plane,)),
     ]
-    so += [dma((n_z, layers // 2))] * 6 + [dma((chips,))] * 16
+    so += [dma((n_z, layers))] * 6 + [dma((chips,))] * 16
     fi = [
         v((layers, group, cols), BF),
         v((layers, group, cols), BF),
-        v((layers, rows, cols), BF),
+        v((layers, group, cols), BF),
         v((plane, 8, rows), F32),
         v((layers, cols, 2 * rank), BF),
         v((n_s, cols, 2 * rank), BF),
@@ -684,16 +761,16 @@
     grad = parts[0].astype(F32) + parts[1].astype(F32) + parts[2].astype(F32)
     gi_out[...] = grad[:, :rank]
     go_out[...] = grad[:, rank:].T
-    micro, users = uw_out.shape
+    users, micro = uw_out.shape
     width = row.shape[1]
-    weight = jnp.broadcast_to(row[0:1, :], (micro, width))
-    key = jnp.broadcast_to(row[1:2, :], (micro, width))
-    first = (lax.broadcasted_iota(jnp.int32, (micro, width), 0) * users).astype(F32)
-    lane = lax.broadcasted_iota(jnp.int32, (micro, users), 1)
-    result = jnp.zeros((micro, users), F32)
-    for u in range(users):
-        most = jnp.max(jnp.where(key == first + u, weight, 0.0), -1, keepdims=True)
-        result = jnp.where(lane == u, most, result)
+    weight = jnp.broadcast_to(row[0:1, :], (users, width))
+    key = jnp.broadcast_to(row[1:2, :], (users, width))
+    user = lax.broadcasted_iota(jnp.int32, (users, width), 0).astype(F32)
+    lane = lax.broadcasted_iota(jnp.int32, (users, micro), 1)
+    result = jnp.zeros((users, micro), F32)
+    for m in range(micro):
+        most = jnp.max(jnp.where(key == user + m * users, weight, 0.0), -1, keepdims=True)
+        result = jnp.where(lane == m, most, result)
     uw_out[...] = result
 
 
@@ -706,20 +783,20 @@
     bound = 0.8 * math.sqrt(n_s * (rows // users) * width * width)
     parts, row = main(
         sizes, (micro * rows, cols, rank, width), bound, adapter_in[0], adapter_out[0], norm_gain,
-        hidden_in, cotangent, user_of_row, included,
+        hidden_in, cotangent, user_of_row, included.T,
     )
     gi, go, uw = pl.pallas_call(
         close_kernel,
         out_shape=(
             jax.ShapeDtypeStruct((cols, rank), F32),
             jax.ShapeDtypeStruct((rank, cols), F32),
-            jax.ShapeDtypeStruct((micro, users), F32),
+            jax.ShapeDtypeStruct((users, micro), F32),
         ),
         in_specs=[VMEM, VMEM],
         out_specs=(VMEM,) * 3,
         name="close",
     )(parts, row)
-    return (gi[None], go[None], uw)
+    return (gi[None], go[None], uw.T)
 
 
 def build(torus):

time: 158 us -> 164 us (1.038); the launches traced: 156 us -> 164 us
  Pallas kernels: 153 us -> 163 us
  local copies, waits for them, and re-layouts: 2.64 us -> 0 us
    pallas_call x1, Pallas kernels: 151 us -> 161 us  [main(): pl.pallas_call(functools.partial(main_kernel, sizes, dims, bound, len(ex)...]
    unnamed x2 -> x0, local copies, waits for them, and re-layouts: 2.64 us -> none
where the time goes in v5:
time: 164 us
  Pallas kernels  163 us (99%)
    pallas_call x1, Pallas kernels, main(): pl.pallas_call(functools.partial(main_kernel, sizes, dims, bound, len(ex)...  161 us

profile of v5, /device:TPU:1, one launch (start us, length us, event | category | flops | bytes accessed | tf_op | source)
XLA Modules:
  0.0 163.7 jit_solution(11621593625051927398)
XLA Ops:
  0.6 161.2 %main.1 = (bf16[3,256,256]{2,1,0:T(8,128)(2,1)}, f32[8,128]{1,0:T(8,128)}) custom-call(bf16[256,128]{1,0:T(8,128)(2,1)} %bitcast.6, bf16[128,256]{1,0:T(8,128)(2,1)} %bitcast.7, bf16[1,256]{1,0:T(2,128)(2,1)} %g_ref.1, bf16[4,32,8192]{2,1,0:T(8,128)(2,1)} %hid_ref.1, bf16[4,32,8192]{2,1,0:T(8,128)(2,1)} %cot_ref.1, s32[4,32]{1,0:T(4,128)} %user_ref.1, ...), custom_call_target="tpu_custom_call" | custom-call | tf_op jit(solution)/shard_map/main/pallas_call | solution.py:745
  161.9 1.8 %close.1 = (f32[256,128]{1,0:T(8,128)}, f32[128,256]{1,0:T(8,128)}, f32[2,4]{1,0:T(2,128)}) custom-call(bf16[3,256,256]{2,1,0:T(8,128)(2,1)} %get-tuple-element.8.parts, f32[8,128]{1,0:T(8,128)} %get-tuple-element.9.row), custom_call_target="tpu_custom_call" | custom-call | tf_op jit(solution)/shard_map/close/pallas_call | solution.py:788

commit v6 on v5

--- a/solution.py
+++ b/solution.py
@@ -304,13 +304,14 @@
 def solve_phase(
     sizes, dims, w_all, h_all, c_all, low_out, err_out,
     gsend, grecv, gram, pbuf, prev, psum, crev, state, snap, full, rin,
-    gs, gr, rs, rr, ls, lr, ns, nr, ps, pr, cs, cr, m0, m1, m2, m3, l0, l1, l2, l3, e0, e1, e2, e3,
+    gs, gr, rs, rr, ls, lr, ns, nr, ps, pr, cs, cr, m0, m1, m2, m3, k0, k1, k2, k3, l0, l1, l2, l3, e0, e1, e2, e3,
 ):
     n_s, n_z, n_x = sizes
     rows, cols, rank, width = dims
     layers = n_s
     own = rows // n_s
     part = rank // n_x
+    split = (2 * layers + 1) * own
     p = Plane(sizes)
     mine = w_all[p.z, :cols, rank:]
     for l in range(layers):
@@ -332,12 +333,12 @@
             ct = mm(c_all[i].reshape(rows, cols), w_all[l, :cols, rank:], 1, 0).astype(BF)
             at = slice(i * n_s, (i + 1) * n_s)
             for c, value in enumerate((zy[:, :rank], zy[:, rank:], ct)):
-                r0 = (c * layers + l) * own
+                r0 = (c * layers + l + c // 2) * own
                 pbuf[at, r0 : r0 + own, :] = value.reshape(n_s, own, rank)
     for i in range(n_x):
         xf = h_all[i].reshape(rows, cols).astype(F32)
         sq = jnp.broadcast_to(jnp.sum(xf * xf, -1, keepdims=True), (rows, rank)).astype(BF)
-        pbuf[i * n_s : (i + 1) * n_s, 3 * layers * own :, :] = sq.reshape(n_s, own, rank)
+        pbuf[i * n_s : (i + 1) * n_s, 2 * layers * own : split, :] = sq.reshape(n_s, own, rank)
 
     def block(chip, core):
         return (2 * (chip // n_x) + core) * n_x + lax.rem(chip, n_x)
@@ -348,24 +349,15 @@
     def pre_wait(i):
         return remote(pbuf.at[block(i, p.core)], prev.at[i], ps.at[i], pr.at[i], p.partner)
 
-    def c_copy(to, slot):
-        return remote(psum.at[to], crev.at[slot], cs.at[to], cr.at[slot], p.peer(to))
+    halves = (slice(0, split), slice(split, (3 * layers + 1) * own))
+
+    def c_copy(to, slot, piece):
+        return remote(
+            psum.at[to, halves[piece]], crev.at[slot, halves[piece]],
+            cs.at[to, piece], cr.at[slot, piece], p.peer(to),
+        )
 
     loop(p.chips, lambda k: pre(p.ahead(k)).start())
-
-    early = (p.chips - 1) // 4
-
-    def pair(k):
-        i = p.ahead(k)
-        pre_wait(i).wait_recv()
-        total = pbuf[block(i, p.core)].astype(F32) + prev[i].astype(F32)
-        psum[i] = total.astype(BF)
-
-        @pl.when(jnp.logical_and(k >= 1, k <= early))
-        def _():
-            c_copy(i, p.chip).start()
-
-    loop(p.chips, lambda k: pair(lax.rem(k + 1, p.chips)))
 
     loop(n_plane - 1, lambda k: g_copy(me, lax.rem(me + n_plane - 1 - k, n_plane)).wait_recv())
     grecv[me] = gsend[p.s, p.x]
@@ -398,19 +390,34 @@
     )
     ring.start()
 
-    loop(p.chips - 1 - early, lambda k: c_copy(p.ahead(k + 1 + early), p.chip).start())
+    def pair(k):
+        i = p.ahead(k)
+        pre_wait(i).wait_recv()
+        total = pbuf[block(i, p.core)].astype(F32) + prev[i].astype(F32)
+        psum[i] = total.astype(BF)
+
+        @pl.when(i != p.chip)
+        def _():
+            c_copy(i, p.chip, 0).start()
+
+    loop(p.chips, lambda k: pair(lax.rem(k + 1, p.chips)))
+    p.others(lambda k: c_copy(p.ahead(k), p.chip, 1).start())
 
     def share(layer, piece, core):
         ref = gram_part(layer, piece, core)
         return remote(ref, ref, ns.at[layer, piece], nr.at[layer, piece], p.partner)
 
     ring.run(lambda layer, piece: share(layer, piece, p.core).start())
-    p.others(lambda k: c_copy(p.chip, p.behind(k)).wait_recv())
     crev[p.chip] = psum[p.chip]
-    total = crev[0].astype(F32)
-    for k in range(1, p.chips):
-        total = total + crev[k].astype(F32)
-    state[...] = total.reshape(3 * layers + 1, own, rank)
+
+    def collect(piece, at):
+        p.others(lambda k: c_copy(p.chip, p.behind(k), piece).wait_recv())
+        total = crev[0, halves[piece]].astype(F32)
+        for k in range(1, p.chips):
+            total = total + crev[k, halves[piece]].astype(F32)
+        state[at] = total.reshape(-1, own, rank)
+
+    collect(0, slice(0, 2 * layers + 1))
 
     def each_share(core, fn):
         def body(k):
@@ -422,16 +429,24 @@
 
     each_share(1 - p.core, lambda copy: copy.wait_recv())
 
-    def low_view(chip, core):
-        dev = block(chip, core)
-        return low_out.at[:, pl.ds(pl.multiple_of(dev * own, own), own), :]
+    mid = layers // 2
+
+    def low_view(first, last):
+        def view(chip, core):
+            dev = block(chip, core)
+            return low_out.at[first:last, pl.ds(pl.multiple_of(dev * own, own), own), :]
+
+        return view
+
+    early = Cast(p, low_view(0, mid), (k0, k1, k2, k3))
+    lows = Cast(p, low_view(mid, layers + 1), (l0, l1, l2, l3))
 
     def err_view(chip, core):
         dev = block(chip, core)
         return err_out.at[:, pl.ds(pl.multiple_of(dev * own, own), own), :]
 
     here = pl.ds(pl.multiple_of(me * own, own), own)
-    square = state[3 * layers]
+    square = state[2 * layers]
     zero = jnp.zeros((own, rank), F32)
     lane = lax.broadcasted_iota(jnp.int32, (own, rank), 1)
     scal = zero
@@ -460,24 +475,28 @@
         high = rinv.astype(BF).astype(F32)
         scal = jnp.where(lane == l, high, scal)
         scal = jnp.where(lane == layers + l, rinv - high, scal)
+        if l == mid - 1:
+            early.start()
     low_out[layers, here, :] = scal.astype(BF)
-    lows = Cast(p, low_view, (l0, l1, l2, l3))
     lows.start()
+    early.relay()
+    collect(1, slice(2 * layers + 1, 3 * layers + 1))
     scal = zero
     for l in range(layers - 1, -1, -1):
-        err = state[2 * layers + l].astype(BF)
+        err = state[2 * layers + 1 + l].astype(BF)
         mean = jnp.sum(err.astype(F32) * full[l], -1, keepdims=True) / width
         rinv = rin[l]
         cor = rinv * rinv * mean
         for j in range(l):
             back = mm(err, gram[0, j, l].reshape(rank, rank), 1, 1)
-            state[2 * layers + j] = state[2 * layers + j] + rinv * back - cor * snap[l, j]
+            state[2 * layers + 1 + j] = state[2 * layers + 1 + j] + rinv * back - cor * snap[l, j]
         err_out[l, here, :] = err
         scal = jnp.where(lane == l, cor, scal)
     err_out[layers, here, :] = scal.astype(BF)
     errs = Cast(p, err_view, (e0, e1, e2, e3))
     errs.start()
     lows.relay()
+    early.finish()
     lows.finish()
 
     def drain():
@@ -485,7 +504,8 @@
         ring.finish()
         each_share(p.core, lambda copy: copy.wait_send())
         loop(p.chips, lambda k: pre(p.ahead(k)).wait_send())
-        p.others(lambda k: c_copy(p.ahead(k), p.chip).wait_send())
+        p.others(lambda k: c_copy(p.ahead(k), p.chip, 0).wait_send())
+        p.others(lambda k: c_copy(p.ahead(k), p.chip, 1).wait_send())
 
     return drain, errs
 
@@ -505,6 +525,8 @@
     def rinv_of(i, l):
         return factor(low_ref, i, l) + factor(low_ref, i, layers + l)
 
+    errs.relay()
+    errs.finish()
     for i in range(n_x):
         at = slice(i * rows, (i + 1) * rows)
         h = h_all[i].reshape(rows, cols).astype(F32)
@@ -514,8 +536,6 @@
             hold[l, at] = h.astype(BF)
             if l + 1 < layers:
                 h = h + mm(low_ref[l, at], w_all[l, :cols, rank:], 1, 1)
-    errs.relay()
-    errs.finish()
     sums = []
     for i in range(n_x):
         at = slice(i * rows, (i + 1) * rows)
@@ -572,8 +592,10 @@
     def keep():
         return pltpu.make_async_copy(gbuf.at[s], mid.at[s], lsem.at[0])
 
-    def gradient(k):
-        l = lax.rem(s + 1 + k, n_s)
+    gap_here = lax.rem(s + n_z - z, n_z)
+    soon = jnp.logical_and(gap_here >= n_z // 2 - 1, gap_here <= n_z // 2 + 1)
+
+    def gradient(l):
         we = (weight * err_ref[l].astype(F32)).astype(BF)
         wl = (weight * low_ref[l].astype(F32)).astype(BF)
         gbuf[l, :, :rank] = mm(normed[l], we, 0, 0).astype(BF)
@@ -643,6 +665,10 @@
                     came = (rbuf, lbuf)[way][step - 1, part].astype(F32)
                     acc[way, step - 1, part] = (came + mid[slot, part].astype(F32)).astype(BF)
                 hop(way, step, piece, src).start()
+        if step == 0:
+
+            pass
+
     need(0)
     grad_out[0] = mid[z]
     for way in (0, 1):
@@ -728,7 +754,7 @@
         v((layers, own, rank), F32),
         dma((plane,)), dma((plane,)),
     ]
-    so += [dma((n_z, layers))] * 6 + [dma((chips,))] * 16
+    so += [dma((n_z, layers))] * 6 + [dma((chips,))] * 2 + [dma((chips, 2))] * 2 + [dma((chips,))] * 16
     fi = [
         v((layers, group, cols), BF),
         v((layers, group, cols), BF),

time: 164 us -> 153 us (0.933)
  Pallas kernels: 163 us -> 152 us
    pallas_call x1, Pallas kernels: 161 us -> 150 us  [main(): pl.pallas_call(functools.partial(main_kernel, sizes, dims, bound, len(ex)...]
where the time goes in v6:
time: 153 us
  Pallas kernels  152 us (99%)
    pallas_call x1, Pallas kernels, main(): pl.pallas_call(functools.partial(main_kernel, sizes, dims, bound, len(ex)...  150 us

profile of v6, /device:TPU:1, one launch (start us, length us, event | category | flops | bytes accessed | tf_op | source)
XLA Modules:
  0.0 152.9 jit_solution(11064118820841882204)
XLA Ops:
  0.6 150.4 %main.1 = (bf16[3,256,256]{2,1,0:T(8,128)(2,1)}, f32[8,128]{1,0:T(8,128)}) custom-call(bf16[256,128]{1,0:T(8,128)(2,1)} %bitcast.6, bf16[128,256]{1,0:T(8,128)(2,1)} %bitcast.7, bf16[1,256]{1,0:T(2,128)(2,1)} %g_ref.1, bf16[4,32,8192]{2,1,0:T(8,128)(2,1)} %hid_ref.1, bf16[4,32,8192]{2,1,0:T(8,128)(2,1)} %cot_ref.1, s32[4,32]{1,0:T(4,128)} %user_ref.1, ...), custom_call_target="tpu_custom_call" | custom-call | tf_op jit(solution)/shard_map/main/pallas_call | solution.py:771
  151.1 1.8 %close.1 = (f32[256,128]{1,0:T(8,128)}, f32[128,256]{1,0:T(8,128)}, f32[2,4]{1,0:T(2,128)}) custom-call(bf16[3,256,256]{2,1,0:T(8,128)(2,1)} %get-tuple-element.8.parts, f32[8,128]{1,0:T(8,128)} %get-tuple-element.9.row), custom_call_target="tpu_custom_call" | custom-call | tf_op jit(solution)/shard_map/close/pallas_call | solution.py:814

commit v7 on v6

--- a/solution.py
+++ b/solution.py
@@ -15,6 +15,8 @@
 VMEM = pl.BlockSpec(memory_space=pltpu.VMEM)
 ANY = pl.BlockSpec(memory_space=pl.ANY)
 LIMIT = 60 * 1024 * 1024
+PIECES = 4
+WAVES = 2
 
 
 def mm(a, b, ca, cb):
@@ -166,13 +168,14 @@
         src, dst = act(which, to, slot)
         return remote(src, dst, asend.at[which, to], arecv.at[which, slot], (s, z, to))
 
-    split = cols // 2
-    half = (slice(0, split), slice(split, cols + 16))
+    step = cols // PIECES
+    half = [slice(i * step, (i + 1) * step) for i in range(PIECES - 1)]
+    half.append(slice((PIECES - 1) * step, cols + 16))
 
     def view(block, piece):
         return column.at[block, half[piece]]
 
-    ring = Ring(n_z, z, lambda to: (s, to, x), view, 2, (rs, rr, ls, lr))
+    ring = Ring(n_z, z, lambda to: (s, to, x), view, PIECES, (rs, rr, ls, lr))
     ring.start()
     for which in range(3):
         for k in range(1, n_x):
@@ -201,7 +204,7 @@
         def _():
             y_copy(block, s, piece).start()
 
-    for piece in (0, 1):
+    for piece in range(PIECES):
         onward(z, piece)
     ring.run(onward)
     for which in range(3):
@@ -212,12 +215,12 @@
 
     def not_me(fn):
         def body(k):
-            for piece in (0, 1):
+            for piece in range(PIECES):
                 fn(lax.rem(s + 1 + k, n_s), piece)
 
         loop(n_s - 1, body)
 
-    for piece in (0, 1):
+    for piece in range(PIECES):
         keep(piece).wait()
     not_me(lambda k, piece: y_copy(s, k, piece).wait_recv())
 
@@ -479,7 +482,6 @@
             early.start()
     low_out[layers, here, :] = scal.astype(BF)
     lows.start()
-    early.relay()
     collect(1, slice(2 * layers + 1, 3 * layers + 1))
     scal = zero
     for l in range(layers - 1, -1, -1):
@@ -495,6 +497,7 @@
     err_out[layers, here, :] = scal.astype(BF)
     errs = Cast(p, err_view, (e0, e1, e2, e3))
     errs.start()
+    early.relay()
     lows.relay()
     early.finish()
     lows.finish()
@@ -586,14 +589,17 @@
 
     weight = jnp.concatenate(weights, 0)
 
-    def g_copy(to, slot):
-        return remote(gbuf.at[to], mid.at[slot], gs.at[to], gr.at[slot], (to, z, x))
+    step_rows = cols // WAVES
+    waves = [slice(i * step_rows, (i + 1) * step_rows) for i in range(WAVES)]
+
+    def g_copy(to, slot, piece):
+        part = waves[piece]
+        return remote(
+            gbuf.at[to, part], mid.at[slot, part], gs.at[to, piece], gr.at[slot, piece], (to, z, x)
+        )
 
     def keep():
         return pltpu.make_async_copy(gbuf.at[s], mid.at[s], lsem.at[0])
-
-    gap_here = lax.rem(s + n_z - z, n_z)
-    soon = jnp.logical_and(gap_here >= n_z // 2 - 1, gap_here <= n_z // 2 + 1)
 
     def gradient(l):
         we = (weight * err_ref[l].astype(F32)).astype(BF)
@@ -603,31 +609,29 @@
 
         @pl.when(s != l)
         def _():
-            g_copy(l, s).start()
+            g_copy(l, s, 0).start()
 
         @pl.when(s == l)
         def _():
             keep().start()
 
     loop(layers, gradient)
-
-    def have(slot):
-        @pl.when(slot == s)
-        def _():
-            keep().wait()
-
+    for piece in range(1, WAVES):
+        loop(n_s - 1, lambda k, piece=piece: g_copy(lax.rem(s + 1 + k, n_s), s, piece).start())
+    keep().wait()
+
+    def have(slot, piece):
         @pl.when(slot != s)
         def _():
-            g_copy(s, slot).wait_recv()
+            g_copy(s, slot, piece).wait_recv()
 
     far = n_z // 2
-    halves = (slice(0, cols // 2), slice(cols // 2, cols))
 
     def hops(way, piece):
-        return far if way == piece else far - 1
+        return far if way == (piece * 2) // WAVES else far - 1
 
     def hop(way, step, piece, src):
-        part = halves[piece]
+        part = waves[piece]
         if step + 1 == hops(way, piece):
             dst = grad_out.at[1 + way, part]
         else:
@@ -637,7 +641,7 @@
         return remote(src, dst, send.at[step, piece], recv.at[step, piece], (s, to, x))
 
     def source(way, step, piece, slot):
-        part = halves[piece]
+        part = waves[piece]
         return mid.at[slot, part] if step == 0 else acc.at[way, step - 1, part]
 
     def slot_of(way, gap):
@@ -645,43 +649,41 @@
 
     seen = set()
 
-    def need(gap):
-        if gap % n_z not in seen:
-            seen.add(gap % n_z)
-            have(lax.rem(z + gap + n_z, n_z))
-
-    for step in range(far):
-        for piece in (0, 1):
-            for way in (0, 1):
-                if step >= hops(way, piece):
-                    continue
-                gap = hops(way, piece) - step
-                need(gap if way == 0 else -gap)
-                slot = slot_of(way, gap)
-                part = halves[piece]
-                src = source(way, step, piece, slot)
-                if step > 0:
-                    hop(way, step - 1, piece, source(way, step - 1, piece, slot)).wait_recv()
-                    came = (rbuf, lbuf)[way][step - 1, part].astype(F32)
-                    acc[way, step - 1, part] = (came + mid[slot, part].astype(F32)).astype(BF)
-                hop(way, step, piece, src).start()
-        if step == 0:
-
-            pass
-
-    need(0)
+    def need(gap, piece):
+        if (gap % n_z, piece) not in seen:
+            seen.add((gap % n_z, piece))
+            have(lax.rem(z + gap + n_z, n_z), piece)
+
+    order = sorted((step + piece, piece, step) for step in range(far) for piece in range(WAVES))
+    for _, piece, step in order:
+        for way in (0, 1):
+            if step >= hops(way, piece):
+                continue
+            gap = hops(way, piece) - step
+            need(gap if way == 0 else -gap, piece)
+            slot = slot_of(way, gap)
+            part = waves[piece]
+            src = source(way, step, piece, slot)
+            if step > 0:
+                hop(way, step - 1, piece, source(way, step - 1, piece, slot)).wait_recv()
+                came = (rbuf, lbuf)[way][step - 1, part].astype(F32)
+                acc[way, step - 1, part] = (came + mid[slot, part].astype(F32)).astype(BF)
+            hop(way, step, piece, src).start()
+    for piece in range(WAVES):
+        need(0, piece)
     grad_out[0] = mid[z]
     for way in (0, 1):
-        for piece in (0, 1):
+        for piece in range(WAVES):
             step = hops(way, piece) - 1
             hop(way, step, piece, source(way, step, piece, z)).wait_recv()
 
     def drain():
         for way in (0, 1):
-            for piece in (0, 1):
+            for piece in range(WAVES):
                 for step in range(hops(way, piece)):
                     hop(way, step, piece, source(way, step, piece, z)).wait_send()
-        loop(n_s - 1, lambda k: g_copy(lax.rem(s + 1 + k, n_s), s).wait_send())
+        for piece in range(WAVES):
+            loop(n_s - 1, lambda k, piece=piece: g_copy(lax.rem(s + 1 + k, n_s), s, piece).wait_send())
         loop(n_plane - 1, lambda k: t_copy(lax.rem(me + 1 + k, n_plane), me).wait_send())
 
     return drain
@@ -737,8 +739,8 @@
     ex = [
         v((n_z, cols + 16, 2 * rank), BF),
         v((16, rows), BF),
-        dma((n_z, 2)), dma((n_z, 2)), dma((n_z, 2)), dma((n_z, 2)),
-        dma((n_z, 2)), dma((n_s, 2)), dma((3, n_x)), dma((3, n_x)), dma((5,)),
+        dma((n_z, PIECES)), dma((n_z, PIECES)), dma((n_z, PIECES)), dma((n_z, PIECES)),
+        dma((n_z, PIECES)), dma((n_s, PIECES)), dma((3, n_x)), dma((3, n_x)), dma((3 + PIECES,)),
     ]
     so = [
         v((n_s, n_x, part, 2 * rank), BF),
@@ -765,9 +767,9 @@
         v((2, n_z // 2, cols, 2 * rank), BF),
         v((n_z // 2, cols, 2 * rank), BF),
         v((n_z // 2, cols, 2 * rank), BF),
-        dma((plane,)), dma((plane,)), dma((n_s,)), dma((n_s,)),
+        dma((plane,)), dma((plane,)), dma((n_s, WAVES)), dma((n_s, WAVES)),
     ]
-    fi += [dma((n_z // 2, 2))] * 4 + [dma((1,))]
+    fi += [dma((n_z // 2, WAVES))] * 4 + [dma((1,))]
     return pl.pallas_call(
         functools.partial(main_kernel, sizes, dims, bound, len(ex), len(so)),
         out_shape=(

time: 153 us -> 151 us (0.987); the launches traced: 153 us -> 149 us
  Pallas kernels: 152 us -> 148 us
    pallas_call x1, Pallas kernels: 150 us -> 146 us  [main(): pl.pallas_call(functools.partial(main_kernel, sizes, dims, bound, len(ex)...]
where the time goes in v7:
time: 151 us; the launch traced here: 149 us
  Pallas kernels  148 us (98%)
    pallas_call x1, Pallas kernels, main(): pl.pallas_call(functools.partial(main_kernel, sizes, dims, bound, len(ex)...  146 us

profile of v7, /device:TPU:1, one launch (start us, length us, event | category | flops | bytes accessed | tf_op | source)
XLA Modules:
  0.0 148.8 jit_solution(8181317152901642962)
XLA Ops:
  0.6 146.3 %main.1 = (bf16[3,256,256]{2,1,0:T(8,128)(2,1)}, f32[8,128]{1,0:T(8,128)}) custom-call(bf16[256,128]{1,0:T(8,128)(2,1)} %bitcast.6, bf16[128,256]{1,0:T(8,128)(2,1)} %bitcast.7, bf16[1,256]{1,0:T(2,128)(2,1)} %g_ref.1, bf16[4,32,8192]{2,1,0:T(8,128)(2,1)} %hid_ref.1, bf16[4,32,8192]{2,1,0:T(8,128)(2,1)} %cot_ref.1, s32[4,32]{1,0:T(4,128)} %user_ref.1, ...), custom_call_target="tpu_custom_call" | custom-call | tf_op jit(solution)/shard_map/main/pallas_call | solution.py:773
  147.0 1.8 %close.1 = (f32[256,128]{1,0:T(8,128)}, f32[128,256]{1,0:T(8,128)}, f32[2,4]{1,0:T(2,128)}) custom-call(bf16[3,256,256]{2,1,0:T(8,128)(2,1)} %get-tuple-element.8.parts, f32[8,128]{1,0:T(8,128)} %get-tuple-element.9.row), custom_call_target="tpu_custom_call" | custom-call | tf_op jit(solution)/shard_map/close/pallas_call | solution.py:816

commit v8 on v7

--- a/solution.py
+++ b/solution.py
@@ -376,7 +376,6 @@
     spread = Cast(p, gram_view, (m0, m1, m2, m3))
     spread.start()
     spread.relay()
-    spread.finish()
 
     def gram_part(layer, piece, core):
         return gram.at[lax.rem(piece, 2), layer, 2 * (piece // 2) + core]
@@ -411,6 +410,7 @@
         return remote(ref, ref, ns.at[layer, piece], nr.at[layer, piece], p.partner)
 
     ring.run(lambda layer, piece: share(layer, piece, p.core).start())
+    spread.finish()
     crev[p.chip] = psum[p.chip]
 
     def collect(piece, at):

time: 151 us -> 149 us (0.987)
  Pallas kernels: 148 us -> 146 us
    pallas_call x1, Pallas kernels: 146 us -> 144 us  [main(): pl.pallas_call(functools.partial(main_kernel, sizes, dims, bound, len(ex)...]
where the time goes in v8:
time: 149 us; the launch traced here: 147 us
  Pallas kernels  146 us (98%)
    pallas_call x1, Pallas kernels, main(): pl.pallas_call(functools.partial(main_kernel, sizes, dims, bound, len(ex)...  144 us

profile of v8, /device:TPU:1, one launch (start us, length us, event | category | flops | bytes accessed | tf_op | source)
XLA Modules:
  0.0 146.6 jit_solution(12334648166883282892)
XLA Ops:
  0.6 144.2 %main.1 = (bf16[3,256,256]{2,1,0:T(8,128)(2,1)}, f32[8,128]{1,0:T(8,128)}) custom-call(bf16[256,128]{1,0:T(8,128)(2,1)} %bitcast.6, bf16[128,256]{1,0:T(8,128)(2,1)} %bitcast.7, bf16[1,256]{1,0:T(2,128)(2,1)} %g_ref.1, bf16[4,32,8192]{2,1,0:T(8,128)(2,1)} %hid_ref.1, bf16[4,32,8192]{2,1,0:T(8,128)(2,1)} %cot_ref.1, s32[4,32]{1,0:T(4,128)} %user_ref.1, ...), custom_call_target="tpu_custom_call" | custom-call | tf_op jit(solution)/shard_map/main/pallas_call | solution.py:773
  144.8 1.8 %close.1 = (f32[256,128]{1,0:T(8,128)}, f32[128,256]{1,0:T(8,128)}, f32[2,4]{1,0:T(2,128)}) custom-call(bf16[3,256,256]{2,1,0:T(8,128)(2,1)} %get-tuple-element.8.parts, f32[8,128]{1,0:T(8,128)} %get-tuple-element.9.row), custom_call_target="tpu_custom_call" | custom-call | tf_op jit(solution)/shard_map/close/pallas_call | solution.py:816

commit v9 on v8

--- a/solution.py
+++ b/solution.py
@@ -499,6 +499,7 @@
     errs.start()
     early.relay()
     lows.relay()
+    errs.relay()
     early.finish()
     lows.finish()
 
@@ -528,7 +529,6 @@
     def rinv_of(i, l):
         return factor(low_ref, i, l) + factor(low_ref, i, layers + l)
 
-    errs.relay()
     errs.finish()
     for i in range(n_x):
         at = slice(i * rows, (i + 1) * rows)

time: 149 us -> 149 us (level)
  no operation moved by 1% of the time
where the time goes in v9:
time: 149 us; the launch traced here: 147 us
  Pallas kernels  146 us (98%)
    pallas_call x1, Pallas kernels, main(): pl.pallas_call(functools.partial(main_kernel, sizes, dims, bound, len(ex)...  144 us

profile of v9, /device:TPU:1, one launch (start us, length us, event | category | flops | bytes accessed | tf_op | source)
XLA Modules:
  0.0 146.6 jit_solution(4231355875250641107)
XLA Ops:
  0.6 144.2 %main.1 = (bf16[3,256,256]{2,1,0:T(8,128)(2,1)}, f32[8,128]{1,0:T(8,128)}) custom-call(bf16[256,128]{1,0:T(8,128)(2,1)} %bitcast.6, bf16[128,256]{1,0:T(8,128)(2,1)} %bitcast.7, bf16[1,256]{1,0:T(2,128)(2,1)} %g_ref.1, bf16[4,32,8192]{2,1,0:T(8,128)(2,1)} %hid_ref.1, bf16[4,32,8192]{2,1,0:T(8,128)(2,1)} %cot_ref.1, s32[4,32]{1,0:T(4,128)} %user_ref.1, ...), custom_call_target="tpu_custom_call" | custom-call | tf_op jit(solution)/shard_map/main/pallas_call | solution.py:773
  144.8 1.8 %close.1 = (f32[256,128]{1,0:T(8,128)}, f32[128,256]{1,0:T(8,128)}, f32[2,4]{1,0:T(2,128)}) custom-call(bf16[3,256,256]{2,1,0:T(8,128)(2,1)} %get-tuple-element.8.parts, f32[8,128]{1,0:T(8,128)} %get-tuple-element.9.row), custom_call_target="tpu_custom_call" | custom-call | tf_op jit(solution)/shard_map/close/pallas_call | solution.py:816
